TPU v7x, 32 devices: a whole 2x2x4 slice. The times are simulated.
32 devices in a mesh: band: 8 (over z, y), plane: 4 (over x, core).
Axes of the slice: x: 2, y: 2, z: 4, core: 2. Of those that a mesh axis runs over, the one named last changes fastest.
Arguments:
- coeffs: float32 [8, 4, 65, 2048], P('band', None, None, 'plane'), may hold values from -6 to 6
- potential: float32 [128, 128, 128], P('plane', 'band'), may hold values from -6 to 6
- stick_map: int32 [3, 2048], replicated, may hold values from -32 to 32, as said below
Outputs:
- applied_coeffs: float32 [8, 4, 65, 2048], P('band', None, None, 'plane')
Inputs may be any that keep to these rules, and one draw needn't show every extreme that they name: `stick_map`: column s describes stick slot s: rows 0 and 1 are its G_x and G_y, row 2 its half-height h, or -1 for an empty slot (then G_x = G_y = 0). The live slots hold every column (x, y) with x*x + y*y <= 32 squared and x > 0, or x = 0 and y > 0, exactly once, with h the largest integer for which x*x + y*y + h*h <= 32 squared. Which slot holds which column is drawn.
All inputs are finite; a program needn't handle non-finite values.
Results may differ from a plain program's by a relative error of at most 0.00007.
Values sent between devices are 32-bit elements; how exact they have to be, the bound alone decides.
No kernel may reach another device: no remote copies, remote signals or barrier semaphores. Data moves between devices by JAX's collectives and lax.ppermute only.
A program may use at most 64 MiB of HBM per device.

v0:
```python
import functools
import math

import jax
import jax.numpy as jnp
import ml_dtypes
import numpy as np
from jax import lax
from jax.experimental import pallas as pl
from jax.experimental.pallas import tpu as pltpu
from jax.sharding import PartitionSpec as P


bf16 = jnp.bfloat16
f32 = jnp.float32
VMEM = pl.BlockSpec(memory_space=pltpu.VMEM)


def up8(n):
    return -(-n // 8) * 8


def halves(table):
    high = table.astype(ml_dtypes.bfloat16)
    return high, (table - high.astype(np.float64)).astype(ml_dtypes.bfloat16)


def split(value):
    high = value.astype(bf16)
    return high, (value - high.astype(f32)).astype(bf16)


class Sizes:
    def __init__(self, span, sticks, length, planes, devices):
        self.span, self.length, self.planes, self.devices = span, length, planes, devices
        self.sticks = sticks
        self.radius = (span - 1) // 2
        self.rows_y = 2 * self.radius
        self.tiles = self.radius // 2 + 1
        self.even = up8(self.tiles)
        self.odd = up8(self.radius // 2)
        self.kept = 2 * (self.even + self.odd)
        self.batch = 2 * planes
        self.step = self.batch + 1
        self.depth_rows = -(-4 * span // 16) * 16


def tables(s):
    turn = 2.0 * math.pi / s.length
    grid = np.arange(s.length)
    depth = np.arange(s.span) - s.radius
    y = np.arange(s.rows_y) + 1 - s.radius

    def trig(left, right):
        angle = turn * np.mod(np.outer(left, right), s.length)
        return np.cos(angle), np.sin(angle)

    cos, sin = trig(depth, grid)
    ahead = np.zeros((s.devices, 2, 2, s.planes, s.span, 2, 2))
    back = np.zeros((s.devices, s.span, 2, 2, 2, 2, s.planes))
    scale = 1.0 / float(s.length) ** 3
    for d in range(s.devices):
        own = slice(d * s.planes, (d + 1) * s.planes)
        c, n = cos[:, own], sin[:, own]
        for o in range(2):
            ahead[d, 0, o, :, :, o, 0] = c.T
            ahead[d, 0, o, :, :, o, 1] = -n.T
            ahead[d, 1, o, :, :, o, 0] = n.T
            ahead[d, 1, o, :, :, o, 1] = c.T
            back[d, :, o, 0, 0, o] = c * scale
            back[d, :, o, 0, 1, o] = n * scale
            back[d, :, o, 1, 0, o] = -n * scale
            back[d, :, o, 1, 1, o] = c * scale
    gap = s.depth_rows - 4 * s.span
    ahead = np.pad(ahead.reshape(s.devices, 2 * s.batch, 4 * s.span), ((0, 0), (0, 0), (0, gap)))
    back = np.pad(back.reshape(s.devices, 4 * s.span, 2 * s.batch), ((0, 0), (0, gap), (0, 0)))

    cos, sin = trig(y, grid)
    y_ahead = np.zeros((2, 2, s.rows_y, 2, 2, s.length))
    y_back = np.zeros((2, 2, s.length, 2, 2, s.rows_y))
    for parity in range(2):
        y_ahead[0, parity, :, parity, 0] = cos
        y_ahead[1, parity, :, parity, 0] = -sin
        y_ahead[0, parity, :, parity, 1] = sin
        y_ahead[1, parity, :, parity, 1] = cos
        y_back[parity, 0, :, 0, parity] = cos.T
        y_back[parity, 1, :, 0, parity] = sin.T
        y_back[parity, 0, :, 1, parity] = -sin.T
        y_back[parity, 1, :, 1, parity] = cos.T
    y_ahead = y_ahead.reshape(4 * s.rows_y, 4 * s.length)
    y_back = y_back.reshape(4 * s.length, 4 * s.rows_y)

    x_ahead = np.zeros((s.length, s.kept))
    x_back = np.zeros((s.kept, s.length))
    at = 0
    for component in range(2):
        for parity in range(2):
            count = s.tiles if parity == 0 else s.radius // 2
            cos, sin = trig(2 * np.arange(count) + parity, grid)
            x_ahead[:, at : at + count] = 2.0 * cos.T if component == 0 else -2.0 * sin.T
            x_back[at : at + count] = cos if component == 0 else -sin
            at += s.even if parity == 0 else s.odd

    def beside(table, axis, order):
        parts = halves(table)
        return np.concatenate([parts[i] for i in order], axis)

    zero = np.zeros(x_back.shape, ml_dtypes.bfloat16)
    high, low = halves(x_back)
    return dict(
        z_ahead=beside(ahead, 2, (0, 1, 0)),
        z_back=beside(back, 2, (0, 1)),
        y_ahead=np.stack(halves(y_ahead)),
        y_back=np.stack(halves(y_back)),
        x_ahead=beside(x_ahead, 1, (0, 1, 0)),
        x_back=np.concatenate([np.concatenate([high, high], 1), np.concatenate([low, zero], 1)], 0),
    )


def dot(left, right):
    return jnp.dot(left, right, preferred_element_type=f32)


def partner(me, k):
    return jnp.bitwise_xor(me, k)


def live_of(s, sticks_ref, source):
    columns = pl.ds(pl.multiple_of(source * s.sticks, s.sticks), s.sticks)
    depth = lax.broadcasted_iota(jnp.int32, (4 * s.span, s.sticks), 0) // 4 - s.radius
    return jnp.abs(depth) <= sticks_ref[2:3, columns]


def ahead_kernel(s, coeffs_ref, sticks_ref, table_ref, *out_refs):
    me = lax.axis_index("plane")
    data = jnp.where(live_of(s, sticks_ref, me), coeffs_ref[0].reshape(4 * s.span, s.sticks), 0.0)
    gap = jnp.zeros((s.depth_rows - 4 * s.span, s.sticks), f32)
    high, low = split(jnp.concatenate([data, gap], 0))
    data = jnp.concatenate([high, high, low], 0)
    for k in reversed(range(s.devices)):
        out_refs[k][...] = dot(table_ref[partner(me, k)], data)


def back_kernel(s, *refs):
    in_refs, (sticks_ref, table_ref, out_ref) = refs[: s.devices], refs[s.devices :]
    me = lax.axis_index("plane")
    total = None
    for k in range(s.devices):
        high, low = split(in_refs[k][...])
        table = table_ref[partner(me, k)]
        table = jnp.concatenate([table, table[:, : 2 * s.batch]], 1)
        term = dot(table, jnp.concatenate([high, high, low], 0))
        total = term if total is None else total + term
    total = jnp.where(live_of(s, sticks_ref, me), total[: 4 * s.span], 0.0)
    out_ref[0] = total.reshape(s.span, 4, s.sticks)


def places(s, sticks_ref, sources, x_ref, y_ref):
    at = 0
    for source in sources:
        columns = pl.ds(pl.multiple_of(source * s.sticks, s.sticks), s.sticks)
        shape = (s.rows_y, s.sticks)
        x_ref[:, at : at + s.sticks] = jnp.broadcast_to(sticks_ref[0:1, columns].astype(f32), shape).astype(bf16)
        row = lax.broadcasted_iota(jnp.int32, shape, 0) + 1 - s.radius
        hit = sticks_ref[1:2, columns] == row
        y_ref[:, at : at + s.sticks] = jnp.where(hit, 1.0, 0.0).astype(bf16)
        at += s.sticks


def one_hot(x, x_all, y_all):
    return jnp.where(x_all == jnp.asarray(x, bf16), y_all, jnp.zeros_like(y_all))


def plane_kernel(s, *refs):
    in_refs, (sticks_ref, table_ref, out_ref, x_ref, y_ref, grid_ref, both_ref) = refs[: s.devices], refs[s.devices :]
    me = lax.axis_index("plane")
    places(s, sticks_ref, [partner(me, k) for k in range(s.devices)], x_ref, y_ref)
    rows = 2 * s.batch
    for k in range(s.devices):
        high, low = split(in_refs[k][...])
        both_ref[:rows, k * s.sticks : (k + 1) * s.sticks] = high
        both_ref[rows:, k * s.sticks : (k + 1) * s.sticks] = low
    lanes = 2 * s.rows_y
    for first in range(0, s.tiles, 2):
        count = min(2, s.tiles - first)
        hot = jnp.concatenate([one_hot(x, x_ref[...], y_ref[...]) for x in range(2 * first, 2 * (first + count))], 0)
        laid = lax.dot_general(both_ref[...], hot, (((1,), (1,)), ((), ())), preferred_element_type=f32)
        laid = laid[:rows] + laid[rows:]
        for t in range(count):
            for component in range(2):
                grid_ref[
                    pl.ds((first + t) * s.batch, s.batch), component * lanes : (component + 1) * lanes
                ] = laid[component * s.batch : (component + 1) * s.batch, t * lanes : (t + 1) * lanes]
    total = s.tiles * s.batch
    table = jnp.concatenate([table_ref[0], table_ref[0], table_ref[1]], 0)
    for start in range(0, total, 4 * s.batch):
        end = min(total, start + 4 * s.batch)
        high, low = split(grid_ref[start:end, :])
        moved = dot(jnp.concatenate([high, low, high], 1), table)
        for t in range(4):
            for row in range(0, end - start, s.batch):
                at = (start + row) // s.batch * s.step
                out_ref[t, at : at + s.batch, :] = moved[row : row + s.batch, t * s.length : (t + 1) * s.length]
    for t in range(4):
        out_ref[t, s.tiles * s.step :, :] = jnp.zeros(((s.even - s.tiles) * s.step, s.length), f32)


def space_kernel(s, bands, half_ref, *refs):
    slab_refs = refs[:bands]
    x_ahead_ref, x_back_ref, y_back_ref, flat_ref, field_ref, turned_ref = refs[bands:]
    width = s.length // bands
    band = lax.axis_index("band")
    at = place_on_ring(band, bands)
    for r, offset in enumerate(ring_offsets(bands)):
        owner = band_on_ring(lax.rem(at + offset + bands, bands), bands)
        field_ref[:, pl.ds(pl.multiple_of(owner * width, width), width), :] = slab_refs[r][...]
    total = s.tiles * s.batch
    for t in range(2, 4):
        turned_ref[t, s.odd * s.step :, :] = jnp.zeros(((s.even - s.odd) * s.step, s.length), f32)

    def plane(z, carry):
        parts = []
        for component in range(2):
            for parity in range(2):
                count = s.odd if parity else s.even
                parts.append(
                    jnp.concatenate(
                        [
                            half_ref[2 * parity + component, pl.ds(o * s.planes + z, count, stride=s.step), :]
                            for o in range(2)
                        ],
                        1,
                    )
                )
        high, low = split(jnp.concatenate(parts, 0))
        real = dot(x_ahead_ref[...], jnp.concatenate([high, high, low], 0))
        field = field_ref[z]
        high, low = split(real * jnp.concatenate([field, field], 1))
        turned = dot(x_back_ref[...], jnp.concatenate([high, low], 0))
        turned = turned[: s.kept] + turned[s.kept :]
        at = 0
        for component in range(2):
            for parity in range(2):
                count = s.odd if parity else s.even
                for o in range(2):
                    turned_ref[2 * parity + component, pl.ds(o * s.planes + z, count, stride=s.step), :] = turned[
                        at : at + count, o * s.length : (o + 1) * s.length
                    ]
                at += count
        return carry

    lax.fori_loop(0, s.planes, plane, 0, unroll=4)

    rows = 2 * s.batch
    lanes = 2 * s.rows_y
    table = jnp.concatenate([y_back_ref[0], y_back_ref[0], y_back_ref[1]], 0)
    for start in range(0, total, 4 * s.batch):
        end = min(total, start + 4 * s.batch)
        parts = []
        for row in range(start // s.batch * s.step, end // s.batch * s.step, s.step):
            parts.append(jnp.concatenate([turned_ref[t, row : row + s.batch, :] for t in range(4)], 1))
        high, low = split(jnp.concatenate(parts, 0))
        moved = dot(jnp.concatenate([high, low, high], 1), table)
        high, low = split(moved)
        for t in range((end - start) // s.batch):
            column = (start // s.batch + t) * lanes
            for component in range(2):
                row = component * s.batch
                mine = slice(t * s.batch, (t + 1) * s.batch), slice(component * lanes, (component + 1) * lanes)
                flat_ref[row : row + s.batch, column : column + lanes] = high[mine]
                flat_ref[rows + row : rows + row + s.batch, column : column + lanes] = low[mine]


def pick_kernel(s, which, flat_ref, sticks_ref, *refs):
    out_refs, (x_ref, y_ref, hot_ref) = refs[: len(which)], refs[len(which) :]
    me = lax.axis_index("plane")
    places(s, sticks_ref, [partner(me, k) for k in which], x_ref, y_ref)
    rows = 2 * s.batch
    for i in range(len(which)):
        columns = slice(i * s.sticks, (i + 1) * s.sticks)
        for x in range(2 * s.tiles):
            hot_ref[x * s.rows_y : (x + 1) * s.rows_y, :] = one_hot(x, x_ref[:, columns], y_ref[:, columns])
        found = dot(flat_ref[...], hot_ref[...])
        out_refs[i][...] = found[:rows] + found[rows:]


def band_on_ring(place, count):
    if count % 2:
        return place
    return jnp.where(2 * place < count, 2 * place, 2 * (count - 1 - place) + 1)


def place_on_ring(band, count):
    if count % 2:
        return band
    return jnp.where(lax.rem(band, 2) == 0, band // 2, count - 1 - band // 2)


def ring_offsets(count):
    offsets = [0]
    for step in range(1, count // 2 + 1):
        offsets += [-step, step]
    return offsets[:count]


def per_device(bands, coeffs, potential, stick_map):
    devices = stick_map.shape[1] // coeffs.shape[3]
    s = Sizes(coeffs.shape[2], coeffs.shape[3], potential.shape[2], potential.shape[0], devices)
    tab = {name: jnp.asarray(value) for name, value in tables(s).items()}
    rows = 2 * s.batch
    block = jax.ShapeDtypeStruct((rows, s.sticks), f32)

    order = list(range(bands)) if bands % 2 else list(range(0, bands, 2)) + list(range(bands - 1, 0, -2))
    along = [(order[i], order[(i + 1) % bands]) for i in range(bands)]
    against = [(b, a) for a, b in along]
    slabs = [potential]
    up = down = potential
    for _ in range(1, bands // 2 + 1):
        up = lax.ppermute(up, "band", along)
        slabs.append(up)
        if len(slabs) < bands:
            down = lax.ppermute(down, "band", against)
            slabs.append(down)

    def exchange(blocks):
        out = [blocks[0]] + [None] * (devices - 1)
        for k in reversed(range(1, devices)):
            out[k] = lax.ppermute(blocks[k], "plane", [(i, i ^ k) for i in range(devices)])
        return out

    def kernel(body, inputs, out_shape, limit, flops, scratch_shapes=()):
        return pl.pallas_call(
            body,
            in_specs=[VMEM] * len(inputs),
            out_specs=jax.tree.map(lambda _: VMEM, out_shape),
            out_shape=out_shape,
            scratch_shapes=scratch_shapes,
            compiler_params=pltpu.CompilerParams(vmem_limit_bytes=limit << 20),
            cost_estimate=pl.CostEstimate(flops=flops, bytes_accessed=1 << 20, transcendentals=0),
        )(*inputs)

    total = devices * s.sticks
    positions = 2 * s.tiles * s.rows_y
    results = []
    for pair in range(coeffs.shape[0]):
        given = jnp.transpose(coeffs[pair : pair + 1], (0, 2, 1, 3))
        sent = kernel(
            functools.partial(ahead_kernel, s), [given, stick_map, tab["z_ahead"]], [block] * devices, 16, 1 << 31
        )
        held = exchange(sent)
        half = kernel(
            functools.partial(plane_kernel, s),
            [*held, stick_map, tab["y_ahead"]],
            jax.ShapeDtypeStruct((4, s.even * s.step, s.length), f32),
            28,
            1 << 32,
            [
                pltpu.VMEM((s.rows_y, total), bf16),
                pltpu.VMEM((s.rows_y, total), bf16),
                pltpu.VMEM((s.tiles * s.batch, 4 * s.rows_y), f32),
                pltpu.VMEM((2 * rows, total), bf16),
            ],
        )
        flat = kernel(
            functools.partial(space_kernel, s, bands),
            [half, *slabs, tab["x_ahead"], tab["x_back"], tab["y_back"]],
            jax.ShapeDtypeStruct((2 * rows, positions), bf16),
            32,
            1 << 32,
            [
                pltpu.VMEM((s.planes, s.length, s.length), f32),
                pltpu.VMEM((4, s.even * s.step, s.length), f32),
            ],
        )
        mixed = [None] * devices
        groups = [[k] for k in reversed(range(2, devices))] + [list(range(min(2, devices)))[::-1]]
        for which in groups:
            parts = kernel(
                functools.partial(pick_kernel, s, which),
                [flat, stick_map],
                [block] * len(which),
                16,
                1 << 31,
                [
                    pltpu.VMEM((s.rows_y, len(which) * s.sticks), bf16),
                    pltpu.VMEM((s.rows_y, len(which) * s.sticks), bf16),
                    pltpu.VMEM((positions, s.sticks), bf16),
                ],
            )
            for k, part in zip(which, parts, strict=True):
                mixed[k] = part
        returned = exchange(mixed)
        result = kernel(
            functools.partial(back_kernel, s),
            [*returned, stick_map, tab["z_back"]],
            jax.ShapeDtypeStruct((1,) + given.shape[1:], f32),
            16,
            1 << 31,
        )
        results.append(jnp.transpose(result, (0, 2, 1, 3)))
    return results[0] if len(results) == 1 else jnp.concatenate(results, 0)


def solution(mesh):
    placed = (P("band", None, None, "plane"), P("plane", "band", None), P())
    return jax.shard_map(
        functools.partial(per_device, mesh.shape["band"]),
        mesh=mesh,
        in_specs=placed,
        out_specs=P("band", None, None, "plane"),
        check_vma=False,
    )
```

profile of v0, /device:TPU:1, one launch (start us, length us, event | category | flops | bytes accessed | tf_op | source)
XLA Modules:
  0.0 57.8 jit_solution(2478249232976800996)
XLA Ops:
  0.0 2.1 %collective-permute-start.3 = (f32[32,16,128]{2,1,0:T(8,128)}, f32[32,16,128]{2,1,0:T(8,128)S(1)}, u32[]{:S(2)}, u32[]{:S(2)}) collective-permute-start(f32[32,16,128]{2,1,0:T(8,128)} %refs_0_.1), channel_id=1, source_target_pairs={{0,8},{8,16},{16,24},{24,28},{28,20},{20,12},{12,4},{4,0},{1,9},{9... | collective-permute-start | bytes 786440 | tf_op jit(solution)/shard_map/ppermute | solution.py:319
  2.1 6.2 %collective-permute-done.3.refs_1_ = f32[32,16,128]{2,1,0:T(8,128)S(1)} collective-permute-done((f32[32,16,128]{2,1,0:T(8,128)}, f32[32,16,128]{2,1,0:T(8,128)S(1)}, u32[]{:S(2)}, u32[]{:S(2)}) %collective-permute-start.3) | collective-permute-done | bytes 262176 | tf_op jit(solution)/shard_map/ppermute | solution.py:319
  8.3 1.2 %collective-permute-start.5 = (f32[32,16,128]{2,1,0:T(8,128)S(1)}, f32[32,16,128]{2,1,0:T(8,128)S(1)}, u32[]{:S(2)}, u32[]{:S(2)}) collective-permute-start(f32[32,16,128]{2,1,0:T(8,128)S(1)} %collective-permute-done.3.refs_1_), channel_id=1, source_target_pairs={{0,8},{8,16},{16,24},{24,28},{28,20},{20,12},{12,4},{4,0},{1,9},{9... | collective-permute-start | bytes 786440 | tf_op jit(solution)/shard_map/ppermute | solution.py:319
  9.5 1.0 %copy-done = f32[1,4,65,512]{3,1,2,0:T(4,128)S(1)} copy-done((f32[1,4,65,512]{3,1,2,0:T(4,128)S(1)}, f32[1,4,65,512]{3,1,2,0:T(4,128)}, u32[]{:S(2)}) %copy-start) | copy-done | bytes 532504
  10.6 0.8 %copy-done.2 = s32[3,2048]{1,0:T(4,128)S(1)} copy-done((s32[3,2048]{1,0:T(4,128)S(1)}, s32[3,2048]{1,0:T(4,128)}, u32[]{:S(2)}) %copy-start.2) | copy-done | bytes 24600
  11.3 1.2 %copy-done.4 = bf16[4,128,816]{2,1,0:T(8,128)(2,1)S(1)} copy-done((bf16[4,128,816]{2,1,0:T(8,128)(2,1)S(1)}, bf16[4,128,816]{2,1,0:T(8,128)(2,1)}, u32[]{:S(2)}) %copy-start.4) | copy-done | bytes 835608
  12.5 0.8 %shard_map.91 = (f32[128,512]{1,0:T(8,128)S(1)}, f32[128,512]{1,0:T(8,128)S(1)}, f32[128,512]{1,0:T(8,128)S(1)}, f32[128,512]{1,0:T(8,128)S(1)}) custom-call(f32[1,65,4,512]{3,2,1,0:T(4,128)S(1)} %bitcast.2, s32[3,2048]{1,0:T(4,128)S(1)} %copy-done.2, bf16[4,128,816]{2,1,0:T(8,128)(2,1)S(1)} %copy-done.4), custom_call_target="tpu_custom_call" | custom-call | flops 2147483648 | bytes 1048576 | tf_op jit(solution)/shard_map/pallas_call | solution.py:332
  13.3 1.9 %collective-permute-start = (f32[128,512]{1,0:T(8,128)S(1)}, f32[128,512]{1,0:T(8,128)S(1)}, u32[]{:S(2)}, u32[]{:S(2)}) collective-permute-start(f32[128,512]{1,0:T(8,128)S(1)} %get-tuple-element.12), channel_id=1, source_target_pairs={{0,1},{1,0},{2,3},{3,2},{4,5},{5,4},{6,7},{7,6},{8,9},{9,8},{10,11... | collective-permute-start | bytes 786440 | tf_op jit(solution)/shard_map/ppermute | solution.py:328
  15.2 1.5 %collective-permute-start.7 = (f32[32,16,128]{2,1,0:T(8,128)S(1)}, f32[32,16,128]{2,1,0:T(8,128)S(1)}, u32[]{:S(2)}, u32[]{:S(2)}) collective-permute-start(f32[32,16,128]{2,1,0:T(8,128)S(1)} %collective-permute-done.5.refs_3_), channel_id=1, source_target_pairs={{0,8},{8,16},{16,24},{24,28},{28,20},{20,12},{12,4},{4,0},{1,9},{9... | collective-permute-start | bytes 786440 | tf_op jit(solution)/shard_map/ppermute | solution.py:319
  16.7 1.2 %collective-permute-start.1 = (f32[128,512]{1,0:T(8,128)S(1)}, f32[128,512]{1,0:T(8,128)S(1)}, u32[]{:S(2)}, u32[]{:S(2)}) collective-permute-start(f32[128,512]{1,0:T(8,128)S(1)} %get-tuple-element.13), channel_id=1, source_target_pairs={{0,2},{1,3},{2,0},{3,1},{4,6},{5,7},{6,4},{7,5},{8,10},{9,11},{10,... | collective-permute-start | bytes 786440 | tf_op jit(solution)/shard_map/ppermute | solution.py:328
  17.9 2.3 %collective-permute-start.2 = (f32[128,512]{1,0:T(8,128)S(1)}, f32[128,512]{1,0:T(8,128)S(1)}, u32[]{:S(2)}, u32[]{:S(2)}) collective-permute-start(f32[128,512]{1,0:T(8,128)S(1)} %get-tuple-element.14), channel_id=1, source_target_pairs={{0,3},{1,2},{2,1},{3,0},{4,7},{5,6},{6,5},{7,4},{8,11},{9,10},{10,... | collective-permute-start | bytes 786440 | tf_op jit(solution)/shard_map/ppermute | solution.py:328
  20.2 2.8 %collective-permute-done.6.refs_4_ = f32[32,16,128]{2,1,0:T(8,128)S(1)} collective-permute-done((f32[32,16,128]{2,1,0:T(8,128)S(1)}, f32[32,16,128]{2,1,0:T(8,128)S(1)}, u32[]{:S(2)}, u32[]{:S(2)}) %collective-permute-start.6) | collective-permute-done | bytes 262176 | tf_op jit(solution)/shard_map/ppermute | solution.py:322
  23.1 1.4 %collective-permute-start.9 = (f32[32,16,128]{2,1,0:T(8,128)S(1)}, f32[32,16,128]{2,1,0:T(8,128)S(1)}, u32[]{:S(2)}, u32[]{:S(2)}) collective-permute-start(f32[32,16,128]{2,1,0:T(8,128)S(1)} %collective-permute-done.7.refs_5_), channel_id=1, source_target_pairs={{0,8},{8,16},{16,24},{24,28},{28,20},{20,12},{12,4},{4,0},{1,9},{9... | collective-permute-start | bytes 786440 | tf_op jit(solution)/shard_map/ppermute | solution.py:319
  24.5 6.1 %collective-permute-done.2.refs_3_ = f32[128,512]{1,0:T(8,128)S(1)} collective-permute-done((f32[128,512]{1,0:T(8,128)S(1)}, f32[128,512]{1,0:T(8,128)S(1)}, u32[]{:S(2)}, u32[]{:S(2)}) %collective-permute-start.2) | collective-permute-done | bytes 262176 | tf_op jit(solution)/shard_map/ppermute | solution.py:328
  30.7 3.6 %shard_map.92.half_ref = f32[4,1560,128]{2,1,0:T(8,128)S(1)} custom-call(f32[128,512]{1,0:T(8,128)S(1)} %get-tuple-element.11.refs_0_, f32[128,512]{1,0:T(8,128)S(1)} %collective-permute-done.refs_1_, f32[128,512]{1,0:T(8,128)S(1)} %collective-permute-done.1.refs_2_, f32[128,512]{1,0:T(8,128)S(1)} %collective-permute-done.2.refs_3_, ...), custom_call_target="tpu_custom_call" | custom-call | flops 4294967296 | bytes 1048576 | tf_op jit(solution)/shard_map/pallas_call | solution.py:332
  34.4 5.1 %shard_map.93.flat_ref = bf16[256,2176]{1,0:T(8,128)(2,1)S(1)} custom-call(f32[4,1560,128]{2,1,0:T(8,128)S(1)} %shard_map.92.half_ref, f32[32,16,128]{2,1,0:T(8,128)S(1)} %copy-done.1, f32[32,16,128]{2,1,0:T(8,128)S(1)} %collective-permute-done.3.refs_1_, f32[32,16,128]{2,1,0:T(8,128)S(1)} %collective-permute-done.4.refs_2_, ...), custom_call_target="tpu_custom_call" | custom-call | flops 4294967296 | bytes 1048576 | tf_op jit(solution)/shard_map/pallas_call | solution.py:332
  39.4 0.8 %shard_map.96 = f32[128,512]{1,0:T(8,128)S(1)} custom-call(bf16[256,2176]{1,0:T(8,128)(2,1)S(1)} %shard_map.93.flat_ref, s32[3,2048]{1,0:T(4,128)S(1)} %copy-done.3), custom_call_target="tpu_custom_call" | custom-call | flops 2147483648 | bytes 1048576 | tf_op jit(solution)/shard_map/pallas_call | solution.py:332
  40.2 0.8 %shard_map.95 = f32[128,512]{1,0:T(8,128)S(1)} custom-call(bf16[256,2176]{1,0:T(8,128)(2,1)S(1)} %shard_map.93.flat_ref, s32[3,2048]{1,0:T(4,128)S(1)} %copy-done.3), custom_call_target="tpu_custom_call" | custom-call | flops 2147483648 | bytes 1048576 | tf_op jit(solution)/shard_map/pallas_call | solution.py:332
  41.1 1.4 %shard_map.94 = (f32[128,512]{1,0:T(8,128)S(1)}, f32[128,512]{1,0:T(8,128)S(1)}) custom-call(bf16[256,2176]{1,0:T(8,128)(2,1)S(1)} %shard_map.93.flat_ref, s32[3,2048]{1,0:T(4,128)S(1)} %copy-done.3), custom_call_target="tpu_custom_call" | custom-call | flops 2147483648 | bytes 1048576 | tf_op jit(solution)/shard_map/pallas_call | solution.py:332
  42.5 1.3 %collective-permute-start.11 = (f32[128,512]{1,0:T(8,128)S(1)}, f32[128,512]{1,0:T(8,128)S(1)}, u32[]{:S(2)}, u32[]{:S(2)}) collective-permute-start(f32[128,512]{1,0:T(8,128)S(1)} %shard_map.95), channel_id=1, source_target_pairs={{0,2},{1,3},{2,0},{3,1},{4,6},{5,7},{6,4},{7,5},{8,10},{9,11},{10,... | collective-permute-start | bytes 786440 | tf_op jit(solution)/shard_map/ppermute | solution.py:328
  43.8 0.9 %collective-permute-start.12 = (f32[128,512]{1,0:T(8,128)S(1)}, f32[128,512]{1,0:T(8,128)S(1)}, u32[]{:S(2)}, u32[]{:S(2)}) collective-permute-start(f32[128,512]{1,0:T(8,128)S(1)} %shard_map.96), channel_id=1, source_target_pairs={{0,3},{1,2},{2,1},{3,0},{4,7},{5,6},{6,5},{7,4},{8,11},{9,10},{10,... | collective-permute-start | bytes 786440 | tf_op jit(solution)/shard_map/ppermute | solution.py:328
  44.7 5.4 %collective-permute-done.11.refs_2_ = f32[128,512]{1,0:T(8,128)S(1)} collective-permute-done((f32[128,512]{1,0:T(8,128)S(1)}, f32[128,512]{1,0:T(8,128)S(1)}, u32[]{:S(2)}, u32[]{:S(2)}) %collective-permute-start.11) | collective-permute-done | bytes 262176 | tf_op jit(solution)/shard_map/ppermute | solution.py:328
  50.0 6.2 %collective-permute-done.12.refs_3_ = f32[128,512]{1,0:T(8,128)S(1)} collective-permute-done((f32[128,512]{1,0:T(8,128)S(1)}, f32[128,512]{1,0:T(8,128)S(1)}, u32[]{:S(2)}, u32[]{:S(2)}) %collective-permute-start.12) | collective-permute-done | bytes 262176 | tf_op jit(solution)/shard_map/ppermute | solution.py:328
  56.3 1.5 %shard_map.97 = f32[1,65,4,512]{3,2,1,0:T(4,128)} custom-call(f32[128,512]{1,0:T(8,128)S(1)} %get-tuple-element.15.refs_0_, f32[128,512]{1,0:T(8,128)S(1)} %collective-permute-done.10.refs_1_, f32[128,512]{1,0:T(8,128)S(1)} %collective-permute-done.11.refs_2_, f32[128,512]{1,0:T(8,128)S(1)} %collective-permute-done.12.refs_3_, s32[3,2048]{1,0:T(4,128)S(1)} %copy-done.3, ...), custom_call_target="tpu_custom_call" | custom-call | flops 2147483648 | bytes 1048576 | tf_op jit(solution)/shard_map/pallas_call | solution.py:332
  (29 shorter events, 0.2 us)
Async XLA Ops:
  0.0 8.3 %collective-permute-start.3 = (f32[32,16,128]{2,1,0:T(8,128)}, f32[32,16,128]{2,1,0:T(8,128)S(1)}, u32[]{:S(2)}, u32[]{:S(2)}) collective-permute-start(f32[32,16,128]{2,1,0:T(8,128)} %refs_0_.1), channel_id=1, source_target_pairs={{0,8},{8,16},{16,24},{24,28},{28,20},{20,12},{12,4},{4,0},{1,9},{9... | collective-permute-start | bytes 786440 | tf_op jit(solution)/shard_map/ppermute | solution.py:319
  2.1 13.1 %collective-permute-start.4 = (f32[32,16,128]{2,1,0:T(8,128)}, f32[32,16,128]{2,1,0:T(8,128)S(1)}, u32[]{:S(2)}, u32[]{:S(2)}) collective-permute-start(f32[32,16,128]{2,1,0:T(8,128)} %refs_0_.1), channel_id=1, source_target_pairs={{8,0},{16,8},{24,16},{28,24},{20,28},{12,20},{4,12},{0,4},{9,1},{1... | collective-permute-start | bytes 786440 | tf_op jit(solution)/shard_map/ppermute | solution.py:322
  8.3 6.9 %collective-permute-start.5 = (f32[32,16,128]{2,1,0:T(8,128)S(1)}, f32[32,16,128]{2,1,0:T(8,128)S(1)}, u32[]{:S(2)}, u32[]{:S(2)}) collective-permute-start(f32[32,16,128]{2,1,0:T(8,128)S(1)} %collective-permute-done.3.refs_1_), channel_id=1, source_target_pairs={{0,8},{8,16},{16,24},{24,28},{28,20},{20,12},{12,4},{4,0},{1,9},{9... | collective-permute-start | bytes 786440 | tf_op jit(solution)/shard_map/ppermute | solution.py:319
  9.5 1.0 %copy-start = (f32[1,4,65,512]{3,1,2,0:T(4,128)S(1)}, f32[1,4,65,512]{3,1,2,0:T(4,128)}, u32[]{:S(2)}) copy-start(f32[1,4,65,512]{3,1,2,0:T(4,128)} %param.9) | copy-start | bytes 1597444
  10.6 0.8 %copy-start.2 = (s32[3,2048]{1,0:T(4,128)S(1)}, s32[3,2048]{1,0:T(4,128)}, u32[]{:S(2)}) copy-start(s32[3,2048]{1,0:T(4,128)} %refs_4_.3) | copy-start | bytes 73732
  11.3 1.2 %copy-start.4 = (bf16[4,128,816]{2,1,0:T(8,128)(2,1)S(1)}, bf16[4,128,816]{2,1,0:T(8,128)(2,1)}, u32[]{:S(2)}) copy-start(bf16[4,128,816]{2,1,0:T(8,128)(2,1)} %constant.12.clone.table_ref) | copy-start | bytes 2506756
  12.5 18.1 %copy-start.3 = (s32[3,2048]{1,0:T(4,128)S(1)}, s32[3,2048]{1,0:T(4,128)}, u32[]{:S(2)}) copy-start(s32[3,2048]{1,0:T(4,128)} %refs_4_.3) | copy-start | bytes 73732
  12.5 18.1 %copy-start.7 = (bf16[2,256,512]{2,1,0:T(8,128)(2,1)S(1)}, bf16[2,256,512]{2,1,0:T(8,128)(2,1)}, u32[]{:S(2)}) copy-start(bf16[2,256,512]{2,1,0:T(8,128)(2,1)} %constant.14.clone.refs_5_) | copy-start | bytes 1572868
  13.3 11.1 %collective-permute-start = (f32[128,512]{1,0:T(8,128)S(1)}, f32[128,512]{1,0:T(8,128)S(1)}, u32[]{:S(2)}, u32[]{:S(2)}) collective-permute-start(f32[128,512]{1,0:T(8,128)S(1)} %get-tuple-element.12), channel_id=1, source_target_pairs={{0,1},{1,0},{2,3},{3,2},{4,5},{5,4},{6,7},{7,6},{8,9},{9,8},{10,11... | collective-permute-start | bytes 786440 | tf_op jit(solution)/shard_map/ppermute | solution.py:328
  15.2 7.8 %collective-permute-start.6 = (f32[32,16,128]{2,1,0:T(8,128)S(1)}, f32[32,16,128]{2,1,0:T(8,128)S(1)}, u32[]{:S(2)}, u32[]{:S(2)}) collective-permute-start(f32[32,16,128]{2,1,0:T(8,128)S(1)} %collective-permute-done.4.refs_2_), channel_id=1, source_target_pairs={{8,0},{16,8},{24,16},{28,24},{20,28},{12,20},{4,12},{0,4},{9,1},{1... | collective-permute-start | bytes 786440 | tf_op jit(solution)/shard_map/ppermute | solution.py:322
  15.2 7.8 %collective-permute-start.7 = (f32[32,16,128]{2,1,0:T(8,128)S(1)}, f32[32,16,128]{2,1,0:T(8,128)S(1)}, u32[]{:S(2)}, u32[]{:S(2)}) collective-permute-start(f32[32,16,128]{2,1,0:T(8,128)S(1)} %collective-permute-done.5.refs_3_), channel_id=1, source_target_pairs={{0,8},{8,16},{16,24},{24,28},{28,20},{20,12},{12,4},{4,0},{1,9},{9... | collective-permute-start | bytes 786440 | tf_op jit(solution)/shard_map/ppermute | solution.py:319
  16.7 7.8 %collective-permute-start.1 = (f32[128,512]{1,0:T(8,128)S(1)}, f32[128,512]{1,0:T(8,128)S(1)}, u32[]{:S(2)}, u32[]{:S(2)}) collective-permute-start(f32[128,512]{1,0:T(8,128)S(1)} %get-tuple-element.13), channel_id=1, source_target_pairs={{0,2},{1,3},{2,0},{3,1},{4,6},{5,7},{6,4},{7,5},{8,10},{9,11},{10,... | collective-permute-start | bytes 786440 | tf_op jit(solution)/shard_map/ppermute | solution.py:328
  17.9 12.7 %collective-permute-start.2 = (f32[128,512]{1,0:T(8,128)S(1)}, f32[128,512]{1,0:T(8,128)S(1)}, u32[]{:S(2)}, u32[]{:S(2)}) collective-permute-start(f32[128,512]{1,0:T(8,128)S(1)} %get-tuple-element.14), channel_id=1, source_target_pairs={{0,3},{1,2},{2,1},{3,0},{4,7},{5,6},{6,5},{7,4},{8,11},{9,10},{10,... | collective-permute-start | bytes 786440 | tf_op jit(solution)/shard_map/ppermute | solution.py:328
  23.0 11.3 %collective-permute-start.8 = (f32[32,16,128]{2,1,0:T(8,128)S(1)}, f32[32,16,128]{2,1,0:T(8,128)S(1)}, u32[]{:S(2)}, u32[]{:S(2)}) collective-permute-start(f32[32,16,128]{2,1,0:T(8,128)S(1)} %collective-permute-done.6.refs_4_), channel_id=1, source_target_pairs={{8,0},{16,8},{24,16},{28,24},{20,28},{12,20},{4,12},{0,4},{9,1},{1... | collective-permute-start | bytes 786440 | tf_op jit(solution)/shard_map/ppermute | solution.py:322
  23.1 11.2 %collective-permute-start.9 = (f32[32,16,128]{2,1,0:T(8,128)S(1)}, f32[32,16,128]{2,1,0:T(8,128)S(1)}, u32[]{:S(2)}, u32[]{:S(2)}) collective-permute-start(f32[32,16,128]{2,1,0:T(8,128)S(1)} %collective-permute-done.7.refs_5_), channel_id=1, source_target_pairs={{0,8},{8,16},{16,24},{24,28},{28,20},{20,12},{12,4},{4,0},{1,9},{9... | collective-permute-start | bytes 786440 | tf_op jit(solution)/shard_map/ppermute | solution.py:319
  30.6 3.7 %copy-start.1 = (f32[32,16,128]{2,1,0:T(8,128)S(1)}, f32[32,16,128]{2,1,0:T(8,128)}, u32[]{:S(2)}) copy-start(f32[32,16,128]{2,1,0:T(8,128)} %refs_0_.1) | copy-start | bytes 786436
  30.6 3.7 %copy-start.6 = (bf16[2,512,256]{2,1,0:T(8,128)(2,1)S(1)}, bf16[2,512,256]{2,1,0:T(8,128)(2,1)}, u32[]{:S(2)}) copy-start(bf16[2,512,256]{2,1,0:T(8,128)(2,1)} %constant.15.clone.refs_10_) | copy-start | bytes 1572868
  30.6 3.7 %copy-start.8 = (bf16[160,256]{1,0:T(8,128)(2,1)S(1)}, bf16[160,256]{1,0:T(8,128)(2,1)}, u32[]{:S(2)}) copy-start(bf16[160,256]{1,0:T(8,128)(2,1)} %constant.17.clone.refs_9_) | copy-start | bytes 245764
  30.6 3.7 %copy-start.9 = (bf16[128,240]{1,0:T(8,128)(2,1)S(1)}, bf16[128,240]{1,0:T(8,128)(2,1)}, u32[]{:S(2)}) copy-start(bf16[128,240]{1,0:T(8,128)(2,1)} %constant.16.clone.refs_8_) | copy-start | bytes 184324
  41.0 15.2 %copy-start.5 = (bf16[4,272,256]{2,1,0:T(8,128)(2,1)S(1)}, bf16[4,272,256]{2,1,0:T(8,128)(2,1)}, u32[]{:S(2)}) copy-start(bf16[4,272,256]{2,1,0:T(8,128)(2,1)} %constant.13.clone.refs_5_) | copy-start | bytes 1671172
  42.5 2.2 %collective-permute-start.10 = (f32[128,512]{1,0:T(8,128)S(1)}, f32[128,512]{1,0:T(8,128)S(1)}, u32[]{:S(2)}, u32[]{:S(2)}) collective-permute-start(f32[128,512]{1,0:T(8,128)S(1)} %get-tuple-element.16), channel_id=1, source_target_pairs={{0,1},{1,0},{2,3},{3,2},{4,5},{5,4},{6,7},{7,6},{8,9},{9,8},{10,11... | collective-permute-start | bytes 786440 | tf_op jit(solution)/shard_map/ppermute | solution.py:328
  42.5 7.5 %collective-permute-start.11 = (f32[128,512]{1,0:T(8,128)S(1)}, f32[128,512]{1,0:T(8,128)S(1)}, u32[]{:S(2)}, u32[]{:S(2)}) collective-permute-start(f32[128,512]{1,0:T(8,128)S(1)} %shard_map.95), channel_id=1, source_target_pairs={{0,2},{1,3},{2,0},{3,1},{4,6},{5,7},{6,4},{7,5},{8,10},{9,11},{10,... | collective-permute-start | bytes 786440 | tf_op jit(solution)/shard_map/ppermute | solution.py:328
  43.8 12.4 %collective-permute-start.12 = (f32[128,512]{1,0:T(8,128)S(1)}, f32[128,512]{1,0:T(8,128)S(1)}, u32[]{:S(2)}, u32[]{:S(2)}) collective-permute-start(f32[128,512]{1,0:T(8,128)S(1)} %shard_map.96), channel_id=1, source_target_pairs={{0,3},{1,2},{2,1},{3,0},{4,7},{5,6},{6,5},{7,4},{8,11},{9,10},{10,... | collective-permute-start | bytes 786440 | tf_op jit(solution)/shard_map/ppermute | solution.py:328
where the time goes:
time: 58.1 us; the launch traced here: 57.8 us
  waiting for transfers between devices  26.7 us (46%)
  Pallas kernels  14.1 us (24%)
  starting transfers between devices  13.8 us (24%)
  local copies, waits for them, and re-layouts  3.01 us (5%)
    ppermute x6, waiting for transfers between devices, exchange(): lax.ppermute(blocks[k], 'plane', [(i, i ^ k) for i in range(devices)])  17.7 us
    pallas_call x7, Pallas kernels, kernel(): pl.pallas_call(body, in_specs=[VMEM] * len(inputs), out_specs=jax.tree.ma...  14.1 us
    ppermute x6, starting transfers between devices, exchange(): lax.ppermute(blocks[k], 'plane', [(i, i ^ k) for i in range(devices)])  7.56 us
    ppermute x4, starting transfers between devices, per_device(): up = lax.ppermute(up, 'band', along)  6.22 us
    ppermute x4, waiting for transfers between devices, per_device(): up = lax.ppermute(up, 'band', along)  6.17 us
    unnamed x20, local copies, waits for them, and re-layouts  3.01 us
    ppermute x3, waiting for transfers between devices, per_device(): down = lax.ppermute(down, 'band', against)  2.85 us
  transfers between devices with their start and end apart: 13, of which 5 were waited for; matrix products, arithmetic and copies ran while one was open for 0% of the time, Pallas kernels for 8%

commit v1 on v0

--- a/solution.py
+++ b/solution.py
@@ -14,6 +14,7 @@
 bf16 = jnp.bfloat16
 f32 = jnp.float32
 VMEM = pl.BlockSpec(memory_space=pltpu.VMEM)
+HBM = pl.BlockSpec(memory_space=pltpu.HBM)
 
 
 def up8(n):
@@ -131,12 +132,21 @@
     return jnp.abs(depth) <= sticks_ref[2:3, columns]
 
 
-def ahead_kernel(s, coeffs_ref, sticks_ref, table_ref, *out_refs):
+def ahead_kernel(s, coeffs_hbm, sticks_hbm, table_hbm, *refs):
+    out_refs, (coeffs_ref, sticks_ref, table_ref, sems) = refs[: s.devices], refs[s.devices :]
+    pairs = [(sticks_hbm, sticks_ref), (coeffs_hbm, coeffs_ref), (table_hbm, table_ref)]
+    copies = [pltpu.make_async_copy(source, target, sems.at[i]) for i, (source, target) in enumerate(pairs)]
+    for copy in copies:
+        copy.start()
     me = lax.axis_index("plane")
-    data = jnp.where(live_of(s, sticks_ref, me), coeffs_ref[0].reshape(4 * s.span, s.sticks), 0.0)
+    copies[0].wait()
+    live = live_of(s, sticks_ref, me)
+    copies[1].wait()
+    data = jnp.where(live, coeffs_ref[0].reshape(4 * s.span, s.sticks), 0.0)
     gap = jnp.zeros((s.depth_rows - 4 * s.span, s.sticks), f32)
     high, low = split(jnp.concatenate([data, gap], 0))
     data = jnp.concatenate([high, high, low], 0)
+    copies[2].wait()
     for k in reversed(range(s.devices)):
         out_refs[k][...] = dot(table_ref[partner(me, k)], data)
 
@@ -206,14 +216,16 @@
 
 
 def space_kernel(s, bands, half_ref, *refs):
-    slab_refs = refs[:bands]
-    x_ahead_ref, x_back_ref, y_back_ref, flat_ref, field_ref, turned_ref = refs[bands:]
+    offsets = ring_offsets(bands)
+    slab_refs, refs = refs[: len(offsets)], refs[len(offsets) :]
+    x_ahead_ref, x_back_ref, y_back_ref, flat_ref, field_ref, turned_ref = refs
     width = s.length // bands
     band = lax.axis_index("band")
     at = place_on_ring(band, bands)
-    for r, offset in enumerate(ring_offsets(bands)):
+    for (offset, first, last), slab_ref in zip(offsets, slab_refs, strict=True):
         owner = band_on_ring(lax.rem(at + offset + bands, bands), bands)
-        field_ref[:, pl.ds(pl.multiple_of(owner * width, width), width), :] = slab_refs[r][...]
+        own = slice(first * s.planes // 2, last * s.planes // 2)
+        field_ref[own, pl.ds(pl.multiple_of(owner * width, width), width), :] = slab_ref[...]
     total = s.tiles * s.batch
     for t in range(2, 4):
         turned_ref[t, s.odd * s.step :, :] = jnp.zeros(((s.even - s.odd) * s.step, s.length), f32)
@@ -297,10 +309,11 @@
 
 
 def ring_offsets(count):
-    offsets = [0]
+    offsets = [(0, 0, 2)]
     for step in range(1, count // 2 + 1):
-        offsets += [-step, step]
-    return offsets[:count]
+        last = 2 * step == count
+        offsets += [(-step, 0, 1 if last else 2), (step, 1 if last else 0, 2)]
+    return offsets
 
 
 def per_device(bands, coeffs, potential, stick_map):
@@ -313,14 +326,6 @@
     order = list(range(bands)) if bands % 2 else list(range(0, bands, 2)) + list(range(bands - 1, 0, -2))
     along = [(order[i], order[(i + 1) % bands]) for i in range(bands)]
     against = [(b, a) for a, b in along]
-    slabs = [potential]
-    up = down = potential
-    for _ in range(1, bands // 2 + 1):
-        up = lax.ppermute(up, "band", along)
-        slabs.append(up)
-        if len(slabs) < bands:
-            down = lax.ppermute(down, "band", against)
-            slabs.append(down)
 
     def exchange(blocks):
         out = [blocks[0]] + [None] * (devices - 1)
@@ -328,31 +333,55 @@
             out[k] = lax.ppermute(blocks[k], "plane", [(i, i ^ k) for i in range(devices)])
         return out
 
-    def kernel(body, inputs, out_shape, limit, flops, scratch_shapes=()):
+    def ring():
+        slabs = [potential]
+        up = down = potential
+        for step in range(1, bands // 2 + 1):
+            last = 2 * step == bands
+            if last:
+                up, down = up[: s.planes // 2], down[s.planes // 2 :]
+            up = lax.ppermute(up, "band", along)
+            down = lax.ppermute(down, "band", against)
+            slabs += [up, down]
+        return slabs
+
+    def kernel(body, inputs, out_shape, limit, flops, scratch_shapes=(), place=VMEM):
         return pl.pallas_call(
             body,
-            in_specs=[VMEM] * len(inputs),
+            in_specs=[place] * len(inputs),
             out_specs=jax.tree.map(lambda _: VMEM, out_shape),
             out_shape=out_shape,
             scratch_shapes=scratch_shapes,
-            compiler_params=pltpu.CompilerParams(vmem_limit_bytes=limit << 20),
+            compiler_params=pltpu.CompilerParams(vmem_limit_bytes=limit << 10),
             cost_estimate=pl.CostEstimate(flops=flops, bytes_accessed=1 << 20, transcendentals=0),
         )(*inputs)
 
+    slabs = ring()
     total = devices * s.sticks
     positions = 2 * s.tiles * s.rows_y
     results = []
     for pair in range(coeffs.shape[0]):
         given = jnp.transpose(coeffs[pair : pair + 1], (0, 2, 1, 3))
         sent = kernel(
-            functools.partial(ahead_kernel, s), [given, stick_map, tab["z_ahead"]], [block] * devices, 16, 1 << 31
+            functools.partial(ahead_kernel, s),
+            [pltpu.with_memory_space_constraint(a, pltpu.HBM) for a in (given, stick_map, tab["z_ahead"])],
+            [block] * devices,
+            16 << 10,
+            1 << 31,
+            [
+                pltpu.VMEM(given.shape, f32),
+                pltpu.VMEM(stick_map.shape, jnp.int32),
+                pltpu.VMEM(tab["z_ahead"].shape, bf16),
+                pltpu.SemaphoreType.DMA((3,)),
+            ],
+            HBM,
         )
         held = exchange(sent)
         half = kernel(
             functools.partial(plane_kernel, s),
             [*held, stick_map, tab["y_ahead"]],
             jax.ShapeDtypeStruct((4, s.even * s.step, s.length), f32),
-            28,
+            28 << 10,
             1 << 32,
             [
                 pltpu.VMEM((s.rows_y, total), bf16),
@@ -365,7 +394,7 @@
             functools.partial(space_kernel, s, bands),
             [half, *slabs, tab["x_ahead"], tab["x_back"], tab["y_back"]],
             jax.ShapeDtypeStruct((2 * rows, positions), bf16),
-            32,
+            32 << 10,
             1 << 32,
             [
                 pltpu.VMEM((s.planes, s.length, s.length), f32),
@@ -379,7 +408,7 @@
                 functools.partial(pick_kernel, s, which),
                 [flat, stick_map],
                 [block] * len(which),
-                16,
+                16 << 10,
                 1 << 31,
                 [
                     pltpu.VMEM((s.rows_y, len(which) * s.sticks), bf16),
@@ -394,7 +423,7 @@
             functools.partial(back_kernel, s),
             [*returned, stick_map, tab["z_back"]],
             jax.ShapeDtypeStruct((1,) + given.shape[1:], f32),
-            16,
+            16 << 10,
             1 << 31,
         )
         results.append(jnp.transpose(result, (0, 2, 1, 3)))

time: 58.1 us -> 60.2 us (1.036)
  waiting for transfers between devices: 26.7 us -> 31.3 us
  local copies, waits for them, and re-layouts: 3.01 us -> 0.05 us
  Pallas kernels: 14.1 us -> 15.4 us
  starting transfers between devices: 13.8 us -> 13.1 us
    ppermute x6, waiting for transfers between devices: 17.7 us -> 22.1 us  [exchange(): lax.ppermute(blocks[k], 'plane', [(i, i ^ k) for i in range(devices)])]
    unnamed x20 -> x14, local copies, waits for them, and re-layouts: 3.01 us -> 0.04 us
    pallas_call x7, Pallas kernels: 14.1 us -> 15.4 us  [kernel(): pl.pallas_call(body, in_specs=[place] * len(inputs), out_specs=jax.tree.m...]
    ppermute x6, starting transfers between devices: 7.56 us -> 6.51 us  [exchange(): lax.ppermute(blocks[k], 'plane', [(i, i ^ k) for i in range(devices)])]
    ppermute x7 -> x8, starting transfers between devices: 6.29 us -> 6.62 us  [the longest x4 5.61 us: ring(): up = lax.ppermute(up, 'band', along)]
    ppermute x7 -> x8, waiting for transfers between devices: 9.01 us -> 9.14 us  [the longest x4 9.13 us: ring(): up = lax.ppermute(up, 'band', along)]
  transfers between devices with their start and end apart: 13 -> 14, of which waited for: 5 -> 6; matrix products, arithmetic and copies ran while one was open for 0% -> 0% of each run, Pallas kernels for 8% -> 10%
where the time goes in v1:
time: 60.2 us; the launch traced here: 60 us
  waiting for transfers between devices  31.3 us (52%)
  Pallas kernels  15.4 us (26%)
  starting transfers between devices  13.1 us (22%)
    ppermute x6, waiting for transfers between devices, exchange(): lax.ppermute(blocks[k], 'plane', [(i, i ^ k) for i in range(devices)])  22.1 us
    pallas_call x7, Pallas kernels, kernel(): pl.pallas_call(body, in_specs=[place] * len(inputs), out_specs=jax.tree.m...  15.4 us
    ppermute x4, waiting for transfers between devices, ring(): up = lax.ppermute(up, 'band', along)  9.13 us
    ppermute x6, starting transfers between devices, exchange(): lax.ppermute(blocks[k], 'plane', [(i, i ^ k) for i in range(devices)])  6.51 us
    ppermute x4, starting transfers between devices, ring(): up = lax.ppermute(up, 'band', along)  5.61 us
  transfers between devices with their start and end apart: 14, of which 6 were waited for; matrix products, arithmetic and copies ran while one was open for 0% of the time, Pallas kernels for 10%

profile of v1, /device:TPU:1, one launch (start us, length us, event | category | flops | bytes accessed | tf_op | source)
XLA Modules:
  0.0 60.0 jit_solution(3620240831369588138)
XLA Ops:
  0.0 2.1 %collective-permute-start.3 = (f32[32,16,128]{2,1,0:T(8,128)}, f32[32,16,128]{2,1,0:T(8,128)S(1)}, u32[]{:S(2)}, u32[]{:S(2)}) collective-permute-start(f32[32,16,128]{2,1,0:T(8,128)} %refs_0_.1), channel_id=1, source_target_pairs={{0,8},{8,16},{16,24},{24,28},{28,20},{20,12},{12,4},{4,0},{1,9},{9... | collective-permute-start | bytes 786440 | tf_op jit(solution)/shard_map/ppermute | solution.py:343
  2.1 6.2 %collective-permute-done.3.refs_1_ = f32[32,16,128]{2,1,0:T(8,128)S(1)} collective-permute-done((f32[32,16,128]{2,1,0:T(8,128)}, f32[32,16,128]{2,1,0:T(8,128)S(1)}, u32[]{:S(2)}, u32[]{:S(2)}) %collective-permute-start.3) | collective-permute-done | bytes 262176 | tf_op jit(solution)/shard_map/ppermute | solution.py:343
  8.3 1.2 %collective-permute-start.5 = (f32[32,16,128]{2,1,0:T(8,128)S(1)}, f32[32,16,128]{2,1,0:T(8,128)S(1)}, u32[]{:S(2)}, u32[]{:S(2)}) collective-permute-start(f32[32,16,128]{2,1,0:T(8,128)S(1)} %collective-permute-done.3.refs_1_), channel_id=1, source_target_pairs={{0,8},{8,16},{16,24},{24,28},{28,20},{20,12},{12,4},{4,0},{1,9},{9... | collective-permute-start | bytes 786440 | tf_op jit(solution)/shard_map/ppermute | solution.py:343
  9.8 2.2 %shard_map.91 = (f32[128,512]{1,0:T(8,128)S(1)}, f32[128,512]{1,0:T(8,128)S(1)}, f32[128,512]{1,0:T(8,128)S(1)}, f32[128,512]{1,0:T(8,128)S(1)}) custom-call(f32[1,65,4,512]{3,2,1,0:T(4,128)} %bitcast.2, s32[3,2048]{1,0:T(4,128)} %refs_4_.3, bf16[4,128,816]{2,1,0:T(8,128)(2,1)} %constant.12.clone.table_hbm), custom_call_target="tpu_custom_call" | custom-call | flops 2147483648 | bytes 1048576 | tf_op jit(solution)/shard_map/pallas_call | solution.py:349
  11.9 3.0 %collective-permute-done.5.refs_3_ = f32[32,16,128]{2,1,0:T(8,128)S(1)} collective-permute-done((f32[32,16,128]{2,1,0:T(8,128)S(1)}, f32[32,16,128]{2,1,0:T(8,128)S(1)}, u32[]{:S(2)}, u32[]{:S(2)}) %collective-permute-start.5) | collective-permute-done | bytes 262176 | tf_op jit(solution)/shard_map/ppermute | solution.py:343
  14.9 1.0 %collective-permute-start.7 = (f32[32,16,128]{2,1,0:T(8,128)S(1)}, f32[32,16,128]{2,1,0:T(8,128)S(1)}, u32[]{:S(2)}, u32[]{:S(2)}) collective-permute-start(f32[32,16,128]{2,1,0:T(8,128)S(1)} %collective-permute-done.5.refs_3_), channel_id=1, source_target_pairs={{0,8},{8,16},{16,24},{24,28},{28,20},{20,12},{12,4},{4,0},{1,9},{9... | collective-permute-start | bytes 786440 | tf_op jit(solution)/shard_map/ppermute | solution.py:343
  15.9 0.5 collective-permute-start.8
  16.4 2.7 %collective-permute-start = (f32[128,512]{1,0:T(8,128)S(1)}, f32[128,512]{1,0:T(8,128)S(1)}, u32[]{:S(2)}, u32[]{:S(2)}) collective-permute-start(f32[128,512]{1,0:T(8,128)S(1)} %get-tuple-element.12), channel_id=1, source_target_pairs={{0,1},{1,0},{2,3},{3,2},{4,5},{5,4},{6,7},{7,6},{8,9},{9,8},{10,11... | collective-permute-start | bytes 786440 | tf_op jit(solution)/shard_map/ppermute | solution.py:333
  19.0 1.2 %collective-permute-start.1 = (f32[128,512]{1,0:T(8,128)S(1)}, f32[128,512]{1,0:T(8,128)S(1)}, u32[]{:S(2)}, u32[]{:S(2)}) collective-permute-start(f32[128,512]{1,0:T(8,128)S(1)} %get-tuple-element.13), channel_id=1, source_target_pairs={{0,2},{1,3},{2,0},{3,1},{4,6},{5,7},{6,4},{7,5},{8,10},{9,11},{10,... | collective-permute-start | bytes 786440 | tf_op jit(solution)/shard_map/ppermute | solution.py:333
  20.2 0.5 collective-permute-start.2
  20.7 1.3 %collective-permute-start.9 = (f32[16,16,128]{2,1,0:T(8,128)S(1)}, f32[16,16,128]{2,1,0:T(8,128)S(1)}, u32[]{:S(2)}, u32[]{:S(2)}) collective-permute-start(f32[16,16,128]{2,1,0:T(8,128)S(1)} %slice.8), channel_id=1, source_target_pairs={{0,8},{8,16},{16,24},{24,28},{28,20},{20,12},{12,4},{4,0},{1,9},{9... | collective-permute-start | bytes 393224 | tf_op jit(solution)/shard_map/ppermute | solution.py:343
  22.3 4.6 %collective-permute-done.1.refs_2_ = f32[128,512]{1,0:T(8,128)S(1)} collective-permute-done((f32[128,512]{1,0:T(8,128)S(1)}, f32[128,512]{1,0:T(8,128)S(1)}, u32[]{:S(2)}, u32[]{:S(2)}) %collective-permute-start.1) | collective-permute-done | bytes 262176 | tf_op jit(solution)/shard_map/ppermute | solution.py:333
  26.9 5.8 %collective-permute-done.2.refs_3_ = f32[128,512]{1,0:T(8,128)S(1)} collective-permute-done((f32[128,512]{1,0:T(8,128)S(1)}, f32[128,512]{1,0:T(8,128)S(1)}, u32[]{:S(2)}, u32[]{:S(2)}) %collective-permute-start.2) | collective-permute-done | bytes 262176 | tf_op jit(solution)/shard_map/ppermute | solution.py:333
  32.7 3.6 %shard_map.92.half_ref = f32[4,1560,128]{2,1,0:T(8,128)S(1)} custom-call(f32[128,512]{1,0:T(8,128)S(1)} %get-tuple-element.11.refs_0_, f32[128,512]{1,0:T(8,128)S(1)} %collective-permute-done.refs_1_, f32[128,512]{1,0:T(8,128)S(1)} %collective-permute-done.1.refs_2_, f32[128,512]{1,0:T(8,128)S(1)} %collective-permute-done.2.refs_3_, ...), custom_call_target="tpu_custom_call" | custom-call | flops 4294967296 | bytes 1048576 | tf_op jit(solution)/shard_map/pallas_call | solution.py:349
  36.4 5.1 %shard_map.93.flat_ref = bf16[256,2176]{1,0:T(8,128)(2,1)S(1)} custom-call(f32[4,1560,128]{2,1,0:T(8,128)S(1)} %shard_map.92.half_ref, f32[32,16,128]{2,1,0:T(8,128)S(1)} %copy-done, f32[32,16,128]{2,1,0:T(8,128)S(1)} %collective-permute-done.3.refs_1_, f32[32,16,128]{2,1,0:T(8,128)S(1)} %collective-permute-done.4.refs_2_, ...), custom_call_target="tpu_custom_call" | custom-call | flops 4294967296 | bytes 1048576 | tf_op jit(solution)/shard_map/pallas_call | solution.py:349
  41.5 0.8 %shard_map.96 = f32[128,512]{1,0:T(8,128)S(1)} custom-call(bf16[256,2176]{1,0:T(8,128)(2,1)S(1)} %shard_map.93.flat_ref, s32[3,2048]{1,0:T(4,128)S(1)} %copy-done.1), custom_call_target="tpu_custom_call" | custom-call | flops 2147483648 | bytes 1048576 | tf_op jit(solution)/shard_map/pallas_call | solution.py:349
  42.3 0.8 %shard_map.95 = f32[128,512]{1,0:T(8,128)S(1)} custom-call(bf16[256,2176]{1,0:T(8,128)(2,1)S(1)} %shard_map.93.flat_ref, s32[3,2048]{1,0:T(4,128)S(1)} %copy-done.1), custom_call_target="tpu_custom_call" | custom-call | flops 2147483648 | bytes 1048576 | tf_op jit(solution)/shard_map/pallas_call | solution.py:349
  43.1 1.4 %shard_map.94 = (f32[128,512]{1,0:T(8,128)S(1)}, f32[128,512]{1,0:T(8,128)S(1)}) custom-call(bf16[256,2176]{1,0:T(8,128)(2,1)S(1)} %shard_map.93.flat_ref, s32[3,2048]{1,0:T(4,128)S(1)} %copy-done.1), custom_call_target="tpu_custom_call" | custom-call | flops 2147483648 | bytes 1048576 | tf_op jit(solution)/shard_map/pallas_call | solution.py:349
  44.5 0.3 collective-permute-start.11
  44.8 1.2 %collective-permute-start.12 = (f32[128,512]{1,0:T(8,128)S(1)}, f32[128,512]{1,0:T(8,128)S(1)}, u32[]{:S(2)}, u32[]{:S(2)}) collective-permute-start(f32[128,512]{1,0:T(8,128)S(1)} %shard_map.95), channel_id=1, source_target_pairs={{0,2},{1,3},{2,0},{3,1},{4,6},{5,7},{6,4},{7,5},{8,10},{9,11},{10,... | collective-permute-start | bytes 786440 | tf_op jit(solution)/shard_map/ppermute | solution.py:333
  46.0 0.8 %collective-permute-start.13 = (f32[128,512]{1,0:T(8,128)S(1)}, f32[128,512]{1,0:T(8,128)S(1)}, u32[]{:S(2)}, u32[]{:S(2)}) collective-permute-start(f32[128,512]{1,0:T(8,128)S(1)} %shard_map.96), channel_id=1, source_target_pairs={{0,3},{1,2},{2,1},{3,0},{4,7},{5,6},{6,5},{7,4},{8,11},{9,10},{10,... | collective-permute-start | bytes 786440 | tf_op jit(solution)/shard_map/ppermute | solution.py:333
  46.7 5.7 %collective-permute-done.12.refs_2_ = f32[128,512]{1,0:T(8,128)S(1)} collective-permute-done((f32[128,512]{1,0:T(8,128)S(1)}, f32[128,512]{1,0:T(8,128)S(1)}, u32[]{:S(2)}, u32[]{:S(2)}) %collective-permute-start.12) | collective-permute-done | bytes 262176 | tf_op jit(solution)/shard_map/ppermute | solution.py:333
  52.4 6.1 %collective-permute-done.13.refs_3_ = f32[128,512]{1,0:T(8,128)S(1)} collective-permute-done((f32[128,512]{1,0:T(8,128)S(1)}, f32[128,512]{1,0:T(8,128)S(1)}, u32[]{:S(2)}, u32[]{:S(2)}) %collective-permute-start.13) | collective-permute-done | bytes 262176 | tf_op jit(solution)/shard_map/ppermute | solution.py:333
  58.5 1.5 %shard_map.97 = f32[1,65,4,512]{3,2,1,0:T(4,128)} custom-call(f32[128,512]{1,0:T(8,128)S(1)} %get-tuple-element.15.refs_0_, f32[128,512]{1,0:T(8,128)S(1)} %collective-permute-done.11.refs_1_, f32[128,512]{1,0:T(8,128)S(1)} %collective-permute-done.12.refs_2_, f32[128,512]{1,0:T(8,128)S(1)} %collective-permute-done.13.refs_3_, s32[3,2048]{1,0:T(4,128)S(1)} %copy-done.1, ...), custom_call_target="tpu_custom_call" | custom-call | flops 2147483648 | bytes 1048576 | tf_op jit(solution)/shard_map/pallas_call | solution.py:349
  (27 shorter events, 0.6 us)
Async XLA Ops:
  0.0 8.3 %collective-permute-start.3 = (f32[32,16,128]{2,1,0:T(8,128)}, f32[32,16,128]{2,1,0:T(8,128)S(1)}, u32[]{:S(2)}, u32[]{:S(2)}) collective-permute-start(f32[32,16,128]{2,1,0:T(8,128)} %refs_0_.1), channel_id=1, source_target_pairs={{0,8},{8,16},{16,24},{24,28},{28,20},{20,12},{12,4},{4,0},{1,9},{9... | collective-permute-start | bytes 786440 | tf_op jit(solution)/shard_map/ppermute | solution.py:343
  2.1 7.4 %collective-permute-start.4 = (f32[32,16,128]{2,1,0:T(8,128)}, f32[32,16,128]{2,1,0:T(8,128)S(1)}, u32[]{:S(2)}, u32[]{:S(2)}) collective-permute-start(f32[32,16,128]{2,1,0:T(8,128)} %refs_0_.1), channel_id=1, source_target_pairs={{8,0},{16,8},{24,16},{28,24},{20,28},{12,20},{4,12},{0,4},{9,1},{1... | collective-permute-start | bytes 786440 | tf_op jit(solution)/shard_map/ppermute | solution.py:344
  8.3 6.6 %collective-permute-start.5 = (f32[32,16,128]{2,1,0:T(8,128)S(1)}, f32[32,16,128]{2,1,0:T(8,128)S(1)}, u32[]{:S(2)}, u32[]{:S(2)}) collective-permute-start(f32[32,16,128]{2,1,0:T(8,128)S(1)} %collective-permute-done.3.refs_1_), channel_id=1, source_target_pairs={{0,8},{8,16},{16,24},{24,28},{28,20},{20,12},{12,4},{4,0},{1,9},{9... | collective-permute-start | bytes 786440 | tf_op jit(solution)/shard_map/ppermute | solution.py:343
  9.5 6.3 %collective-permute-start.6 = (f32[32,16,128]{2,1,0:T(8,128)S(1)}, f32[32,16,128]{2,1,0:T(8,128)S(1)}, u32[]{:S(2)}, u32[]{:S(2)}) collective-permute-start(f32[32,16,128]{2,1,0:T(8,128)S(1)} %collective-permute-done.4.refs_2_), channel_id=1, source_target_pairs={{8,0},{16,8},{24,16},{28,24},{20,28},{12,20},{4,12},{0,4},{9,1},{1... | collective-permute-start | bytes 786440 | tf_op jit(solution)/shard_map/ppermute | solution.py:344
  9.7 22.9 %copy-start.1 = (s32[3,2048]{1,0:T(4,128)S(1)}, s32[3,2048]{1,0:T(4,128)}, u32[]{:S(2)}) copy-start(s32[3,2048]{1,0:T(4,128)} %refs_4_.3) | copy-start | bytes 73732
  9.7 22.9 %copy-start.4 = (bf16[2,256,512]{2,1,0:T(8,128)(2,1)S(1)}, bf16[2,256,512]{2,1,0:T(8,128)(2,1)}, u32[]{:S(2)}) copy-start(bf16[2,256,512]{2,1,0:T(8,128)(2,1)} %constant.14.clone.refs_5_) | copy-start | bytes 1572868
  14.9 5.8 %collective-permute-start.7 = (f32[32,16,128]{2,1,0:T(8,128)S(1)}, f32[32,16,128]{2,1,0:T(8,128)S(1)}, u32[]{:S(2)}, u32[]{:S(2)}) collective-permute-start(f32[32,16,128]{2,1,0:T(8,128)S(1)} %collective-permute-done.5.refs_3_), channel_id=1, source_target_pairs={{0,8},{8,16},{16,24},{24,28},{28,20},{20,12},{12,4},{4,0},{1,9},{9... | collective-permute-start | bytes 786440 | tf_op jit(solution)/shard_map/ppermute | solution.py:343
  15.9 6.1 %collective-permute-start.8 = (f32[32,16,128]{2,1,0:T(8,128)S(1)}, f32[32,16,128]{2,1,0:T(8,128)S(1)}, u32[]{:S(2)}, u32[]{:S(2)}) collective-permute-start(f32[32,16,128]{2,1,0:T(8,128)S(1)} %collective-permute-done.6.refs_4_), channel_id=1, source_target_pairs={{8,0},{16,8},{24,16},{28,24},{20,28},{12,20},{4,12},{0,4},{9,1},{1... | collective-permute-start | bytes 786440 | tf_op jit(solution)/shard_map/ppermute | solution.py:344
  16.4 5.9 %collective-permute-start = (f32[128,512]{1,0:T(8,128)S(1)}, f32[128,512]{1,0:T(8,128)S(1)}, u32[]{:S(2)}, u32[]{:S(2)}) collective-permute-start(f32[128,512]{1,0:T(8,128)S(1)} %get-tuple-element.12), channel_id=1, source_target_pairs={{0,1},{1,0},{2,3},{3,2},{4,5},{5,4},{6,7},{7,6},{8,9},{9,8},{10,11... | collective-permute-start | bytes 786440 | tf_op jit(solution)/shard_map/ppermute | solution.py:333
  19.0 7.9 %collective-permute-start.1 = (f32[128,512]{1,0:T(8,128)S(1)}, f32[128,512]{1,0:T(8,128)S(1)}, u32[]{:S(2)}, u32[]{:S(2)}) collective-permute-start(f32[128,512]{1,0:T(8,128)S(1)} %get-tuple-element.13), channel_id=1, source_target_pairs={{0,2},{1,3},{2,0},{3,1},{4,6},{5,7},{6,4},{7,5},{8,10},{9,11},{10,... | collective-permute-start | bytes 786440 | tf_op jit(solution)/shard_map/ppermute | solution.py:333
  20.2 12.5 %collective-permute-start.2 = (f32[128,512]{1,0:T(8,128)S(1)}, f32[128,512]{1,0:T(8,128)S(1)}, u32[]{:S(2)}, u32[]{:S(2)}) collective-permute-start(f32[128,512]{1,0:T(8,128)S(1)} %get-tuple-element.14), channel_id=1, source_target_pairs={{0,3},{1,2},{2,1},{3,0},{4,7},{5,6},{6,5},{7,4},{8,11},{9,10},{10,... | collective-permute-start | bytes 786440 | tf_op jit(solution)/shard_map/ppermute | solution.py:333
  20.7 15.7 %collective-permute-start.9 = (f32[16,16,128]{2,1,0:T(8,128)S(1)}, f32[16,16,128]{2,1,0:T(8,128)S(1)}, u32[]{:S(2)}, u32[]{:S(2)}) collective-permute-start(f32[16,16,128]{2,1,0:T(8,128)S(1)} %slice.8), channel_id=1, source_target_pairs={{0,8},{8,16},{16,24},{24,28},{28,20},{20,12},{12,4},{4,0},{1,9},{9... | collective-permute-start | bytes 393224 | tf_op jit(solution)/shard_map/ppermute | solution.py:343
  22.0 14.4 %collective-permute-start.10 = (f32[16,16,128]{2,1,0:T(8,128)S(1)}, f32[16,16,128]{2,1,0:T(8,128)S(1)}, u32[]{:S(2)}, u32[]{:S(2)}) collective-permute-start(f32[16,16,128]{2,1,0:T(8,128)S(1)} %slice.9), channel_id=1, source_target_pairs={{8,0},{16,8},{24,16},{28,24},{20,28},{12,20},{4,12},{0,4},{9,1},{1... | collective-permute-start | bytes 393224 | tf_op jit(solution)/shard_map/ppermute | solution.py:344
  32.7 3.7 %copy-start = (f32[32,16,128]{2,1,0:T(8,128)S(1)}, f32[32,16,128]{2,1,0:T(8,128)}, u32[]{:S(2)}) copy-start(f32[32,16,128]{2,1,0:T(8,128)} %refs_0_.1) | copy-start | bytes 786436
  32.7 3.7 %copy-start.3 = (bf16[2,512,256]{2,1,0:T(8,128)(2,1)S(1)}, bf16[2,512,256]{2,1,0:T(8,128)(2,1)}, u32[]{:S(2)}) copy-start(bf16[2,512,256]{2,1,0:T(8,128)(2,1)} %constant.15.clone.refs_11_) | copy-start | bytes 1572868
  32.7 3.7 %copy-start.5 = (bf16[160,256]{1,0:T(8,128)(2,1)S(1)}, bf16[160,256]{1,0:T(8,128)(2,1)}, u32[]{:S(2)}) copy-start(bf16[160,256]{1,0:T(8,128)(2,1)} %constant.17.clone.refs_10_) | copy-start | bytes 245764
  32.7 3.7 %copy-start.6 = (bf16[128,240]{1,0:T(8,128)(2,1)S(1)}, bf16[128,240]{1,0:T(8,128)(2,1)}, u32[]{:S(2)}) copy-start(bf16[128,240]{1,0:T(8,128)(2,1)} %constant.16.clone.refs_9_) | copy-start | bytes 184324
  43.1 15.4 %copy-start.2 = (bf16[4,272,256]{2,1,0:T(8,128)(2,1)S(1)}, bf16[4,272,256]{2,1,0:T(8,128)(2,1)}, u32[]{:S(2)}) copy-start(bf16[4,272,256]{2,1,0:T(8,128)(2,1)} %constant.13.clone.refs_5_) | copy-start | bytes 1671172
  44.5 2.2 %collective-permute-start.11 = (f32[128,512]{1,0:T(8,128)S(1)}, f32[128,512]{1,0:T(8,128)S(1)}, u32[]{:S(2)}, u32[]{:S(2)}) collective-permute-start(f32[128,512]{1,0:T(8,128)S(1)} %get-tuple-element.16), channel_id=1, source_target_pairs={{0,1},{1,0},{2,3},{3,2},{4,5},{5,4},{6,7},{7,6},{8,9},{9,8},{10,11... | collective-permute-start | bytes 786440 | tf_op jit(solution)/shard_map/ppermute | solution.py:333
  44.8 7.6 %collective-permute-start.12 = (f32[128,512]{1,0:T(8,128)S(1)}, f32[128,512]{1,0:T(8,128)S(1)}, u32[]{:S(2)}, u32[]{:S(2)}) collective-permute-start(f32[128,512]{1,0:T(8,128)S(1)} %shard_map.95), channel_id=1, source_target_pairs={{0,2},{1,3},{2,0},{3,1},{4,6},{5,7},{6,4},{7,5},{8,10},{9,11},{10,... | collective-permute-start | bytes 786440 | tf_op jit(solution)/shard_map/ppermute | solution.py:333
  46.0 12.5 %collective-permute-start.13 = (f32[128,512]{1,0:T(8,128)S(1)}, f32[128,512]{1,0:T(8,128)S(1)}, u32[]{:S(2)}, u32[]{:S(2)}) collective-permute-start(f32[128,512]{1,0:T(8,128)S(1)} %shard_map.96), channel_id=1, source_target_pairs={{0,3},{1,2},{2,1},{3,0},{4,7},{5,6},{6,5},{7,4},{8,11},{9,10},{10,... | collective-permute-start | bytes 786440 | tf_op jit(solution)/shard_map/ppermute | solution.py:333

commit v2 on v1

--- a/solution.py
+++ b/solution.py
@@ -46,7 +46,7 @@
         self.depth_rows = -(-4 * span // 16) * 16
 
 
-def tables(s):
+def tables(s, bands):
     turn = 2.0 * math.pi / s.length
     grid = np.arange(s.length)
     depth = np.arange(s.span) - s.radius
@@ -108,12 +108,14 @@
 
     zero = np.zeros(x_back.shape, ml_dtypes.bfloat16)
     high, low = halves(x_back)
+    by_slab = x_back.reshape(s.kept, bands, s.length // bands).transpose(1, 0, 2)
     return dict(
         z_ahead=beside(ahead, 2, (0, 1, 0)),
         z_back=beside(back, 2, (0, 1)),
         y_ahead=np.stack(halves(y_ahead)),
         y_back=np.stack(halves(y_back)),
         x_ahead=beside(x_ahead, 1, (0, 1, 0)),
+        x_last=beside(by_slab, 2, (0, 0, 1)),
         x_back=np.concatenate([np.concatenate([high, high], 1), np.concatenate([low, zero], 1)], 0),
     )
 
@@ -151,18 +153,22 @@
         out_refs[k][...] = dot(table_ref[partner(me, k)], data)
 
 
-def back_kernel(s, *refs):
-    in_refs, (sticks_ref, table_ref, out_ref) = refs[: s.devices], refs[s.devices :]
+def back_kernel(s, which, started, ended, *refs):
+    in_refs, refs = refs[: len(which)], refs[len(which) :]
+    table_ref, out_ref = refs[-2:]
     me = lax.axis_index("plane")
-    total = None
-    for k in range(s.devices):
-        high, low = split(in_refs[k][...])
+    total = refs[0][...] if started else None
+    for i, k in enumerate(which):
+        high, low = split(in_refs[i][...])
         table = table_ref[partner(me, k)]
         table = jnp.concatenate([table, table[:, : 2 * s.batch]], 1)
         term = dot(table, jnp.concatenate([high, high, low], 0))
         total = term if total is None else total + term
-    total = jnp.where(live_of(s, sticks_ref, me), total[: 4 * s.span], 0.0)
-    out_ref[0] = total.reshape(s.span, 4, s.sticks)
+    if ended:
+        total = jnp.where(live_of(s, refs[-3], me), total[: 4 * s.span], 0.0)
+        out_ref[0] = total.reshape(s.span, 4, s.sticks)
+    else:
+        out_ref[...] = total
 
 
 def places(s, sticks_ref, sources, x_ref, y_ref):
@@ -216,19 +222,19 @@
 
 
 def space_kernel(s, bands, half_ref, *refs):
-    offsets = ring_offsets(bands)
-    slab_refs, refs = refs[: len(offsets)], refs[len(offsets) :]
-    x_ahead_ref, x_back_ref, y_back_ref, flat_ref, field_ref, turned_ref = refs
+    offsets = ring_offsets(bands)[:-2]
+    slab_refs, (x_ahead_ref, x_back_ref, turned_ref, real_ref, field_ref) = refs[: len(offsets)], refs[len(offsets) :]
     width = s.length // bands
     band = lax.axis_index("band")
     at = place_on_ring(band, bands)
-    for (offset, first, last), slab_ref in zip(offsets, slab_refs, strict=True):
+    for (offset, _, _), slab_ref in zip(offsets, slab_refs, strict=True):
         owner = band_on_ring(lax.rem(at + offset + bands, bands), bands)
-        own = slice(first * s.planes // 2, last * s.planes // 2)
-        field_ref[own, pl.ds(pl.multiple_of(owner * width, width), width), :] = slab_ref[...]
-    total = s.tiles * s.batch
+        field_ref[:, pl.ds(pl.multiple_of(owner * width, width), width), :] = slab_ref[...]
+    last = pl.ds(pl.multiple_of(last_owner(bands) * width, width), width)
+    field_ref[:, last, :] = jnp.zeros((s.planes, width, s.length), f32)
     for t in range(2, 4):
         turned_ref[t, s.odd * s.step :, :] = jnp.zeros(((s.even - s.odd) * s.step, s.length), f32)
+    table = jnp.concatenate([x_ahead_ref[...], x_ahead_ref[last, :]], 0)
 
     def plane(z, carry):
         parts = []
@@ -245,23 +251,44 @@
                     )
                 )
         high, low = split(jnp.concatenate(parts, 0))
-        real = dot(x_ahead_ref[...], jnp.concatenate([high, high, low], 0))
+        real = dot(table, jnp.concatenate([high, high, low], 0))
+        real_ref[z] = real[s.length :]
         field = field_ref[z]
-        high, low = split(real * jnp.concatenate([field, field], 1))
+        high, low = split(real[: s.length] * jnp.concatenate([field, field], 1))
         turned = dot(x_back_ref[...], jnp.concatenate([high, low], 0))
-        turned = turned[: s.kept] + turned[s.kept :]
-        at = 0
-        for component in range(2):
-            for parity in range(2):
-                count = s.odd if parity else s.even
-                for o in range(2):
-                    turned_ref[2 * parity + component, pl.ds(o * s.planes + z, count, stride=s.step), :] = turned[
-                        at : at + count, o * s.length : (o + 1) * s.length
-                    ]
-                at += count
+        keep_turned(s, turned_ref, z, turned[: s.kept] + turned[s.kept :])
         return carry
 
     lax.fori_loop(0, s.planes, plane, 0, unroll=4)
+
+
+def keep_turned(s, turned_ref, z, turned):
+    at = 0
+    for component in range(2):
+        for parity in range(2):
+            count = s.odd if parity else s.even
+            for o in range(2):
+                turned_ref[2 * parity + component, pl.ds(o * s.planes + z, count, stride=s.step), :] = turned[
+                    at : at + count, o * s.length : (o + 1) * s.length
+                ]
+            at += count
+
+
+def finish_kernel(s, bands, first_ref, real_ref, up_ref, down_ref, x_last_ref, y_back_ref, flat_ref, turned_ref):
+    total = s.tiles * s.batch
+    for t in range(2, 4):
+        turned_ref[t, s.odd * s.step :, :] = jnp.zeros(((s.even - s.odd) * s.step, s.length), f32)
+    x_last = x_last_ref[last_owner(bands)]
+    part = s.planes // 2
+    for slab_ref, start in ((up_ref, 0), (down_ref, part)):
+
+        def plane(z, carry, slab_ref=slab_ref, start=start):
+            field = slab_ref[z]
+            high, low = split(real_ref[start + z] * jnp.concatenate([field, field], 1))
+            keep_turned(s, turned_ref, start + z, dot(x_last, jnp.concatenate([high, low, high], 0)))
+            return carry
+
+        lax.fori_loop(0, part, plane, 0, unroll=4)
 
     rows = 2 * s.batch
     lanes = 2 * s.rows_y
@@ -270,7 +297,8 @@
         end = min(total, start + 4 * s.batch)
         parts = []
         for row in range(start // s.batch * s.step, end // s.batch * s.step, s.step):
-            parts.append(jnp.concatenate([turned_ref[t, row : row + s.batch, :] for t in range(4)], 1))
+            own = slice(row, row + s.batch)
+            parts.append(jnp.concatenate([first_ref[t, own, :] + turned_ref[t, own, :] for t in range(4)], 1))
         high, low = split(jnp.concatenate(parts, 0))
         moved = dot(jnp.concatenate([high, low, high], 1), table)
         high, low = split(moved)
@@ -297,15 +325,15 @@
 
 
 def band_on_ring(place, count):
-    if count % 2:
-        return place
     return jnp.where(2 * place < count, 2 * place, 2 * (count - 1 - place) + 1)
 
 
 def place_on_ring(band, count):
-    if count % 2:
-        return band
     return jnp.where(lax.rem(band, 2) == 0, band // 2, count - 1 - band // 2)
+
+
+def last_owner(count):
+    return band_on_ring(lax.rem(place_on_ring(lax.axis_index("band"), count) + count // 2, count), count)
 
 
 def ring_offsets(count):
@@ -319,11 +347,11 @@
 def per_device(bands, coeffs, potential, stick_map):
     devices = stick_map.shape[1] // coeffs.shape[3]
     s = Sizes(coeffs.shape[2], coeffs.shape[3], potential.shape[2], potential.shape[0], devices)
-    tab = {name: jnp.asarray(value) for name, value in tables(s).items()}
+    tab = {name: jnp.asarray(value) for name, value in tables(s, bands).items()}
     rows = 2 * s.batch
     block = jax.ShapeDtypeStruct((rows, s.sticks), f32)
 
-    order = list(range(bands)) if bands % 2 else list(range(0, bands, 2)) + list(range(bands - 1, 0, -2))
+    order = list(range(0, bands, 2)) + list(range(bands - 1, 0, -2))
     along = [(order[i], order[(i + 1) % bands]) for i in range(bands)]
     against = [(b, a) for a, b in along]
 
@@ -390,16 +418,25 @@
                 pltpu.VMEM((2 * rows, total), bf16),
             ],
         )
+        turned_shape = (4, s.even * s.step, s.length)
+        turned, real = kernel(
+            functools.partial(space_kernel, s, bands),
+            [half, *slabs[:-2], tab["x_ahead"], tab["x_back"]],
+            [
+                jax.ShapeDtypeStruct(turned_shape, f32),
+                jax.ShapeDtypeStruct((s.planes, s.length // bands, 2 * s.length), f32),
+            ],
+            16 << 10,
+            1 << 32,
+            [pltpu.VMEM((s.planes, s.length, s.length), f32)],
+        )
         flat = kernel(
-            functools.partial(space_kernel, s, bands),
-            [half, *slabs, tab["x_ahead"], tab["x_back"], tab["y_back"]],
+            functools.partial(finish_kernel, s, bands),
+            [turned, real, *slabs[-2:], tab["x_last"], tab["y_back"]],
             jax.ShapeDtypeStruct((2 * rows, positions), bf16),
-            32 << 10,
+            24 << 10,
             1 << 32,
-            [
-                pltpu.VMEM((s.planes, s.length, s.length), f32),
-                pltpu.VMEM((4, s.even * s.step, s.length), f32),
-            ],
+            [pltpu.VMEM(turned_shape, f32)],
         )
         mixed = [None] * devices
         groups = [[k] for k in reversed(range(2, devices))] + [list(range(min(2, devices)))[::-1]]
@@ -419,9 +456,17 @@
             for k, part in zip(which, parts, strict=True):
                 mixed[k] = part
         returned = exchange(mixed)
+        early = [k for k in range(devices) if k != 2]
+        begun = kernel(
+            functools.partial(back_kernel, s, early, False, False),
+            [*(returned[k] for k in early), tab["z_back"]],
+            jax.ShapeDtypeStruct((s.depth_rows, s.sticks), f32),
+            16 << 10,
+            1 << 31,
+        )
         result = kernel(
-            functools.partial(back_kernel, s),
-            [*returned, stick_map, tab["z_back"]],
+            functools.partial(back_kernel, s, [2], True, True),
+            [returned[2], begun, stick_map, tab["z_back"]],
             jax.ShapeDtypeStruct((1,) + given.shape[1:], f32),
             16 << 10,
             1 << 31,

time: 60.2 us -> 54.9 us (0.912)
  the two profiles are of different devices: /device:TPU:1 before, /device:TPU:0 now
where the time goes in v2:
time: 54.9 us; the launch traced here: 54.7 us
  waiting for transfers between devices  24.1 us (44%)
  Pallas kernels  17.1 us (31%)
  starting transfers between devices  13.3 us (24%)
    pallas_call x9, Pallas kernels, kernel(): pl.pallas_call(body, in_specs=[place] * len(inputs), out_specs=jax.tree.m...  17.1 us
    ppermute x6, waiting for transfers between devices, exchange(): lax.ppermute(blocks[k], 'plane', [(i, i ^ k) for i in range(devices)])  14.7 us
    ppermute x4, waiting for transfers between devices, ring(): up = lax.ppermute(up, 'band', along)  9.43 us
    ppermute x4, starting transfers between devices, ring(): up = lax.ppermute(up, 'band', along)  6.93 us
    ppermute x6, starting transfers between devices, exchange(): lax.ppermute(blocks[k], 'plane', [(i, i ^ k) for i in range(devices)])  4.05 us
    ppermute x4, starting transfers between devices, ring(): down = lax.ppermute(down, 'band', against)  2.3 us
  transfers between devices with their start and end apart: 14, of which 7 were waited for; matrix products, arithmetic and copies ran while one was open for 0% of the time, Pallas kernels for 21%

profile of v2, /device:TPU:0, one launch (start us, length us, event | category | flops | bytes accessed | tf_op | source)
XLA Modules:
  0.0 54.7 jit_solution(10490045032680296395)
XLA Ops:
  0.0 3.1 %collective-permute-start.3 = (f32[32,16,128]{2,1,0:T(8,128)}, f32[32,16,128]{2,1,0:T(8,128)S(1)}, u32[]{:S(2)}, u32[]{:S(2)}) collective-permute-start(f32[32,16,128]{2,1,0:T(8,128)} %refs_0_.1), channel_id=1, source_target_pairs={{0,8},{8,16},{16,24},{24,28},{28,20},{20,12},{12,4},{4,0},{1,9},{9... | collective-permute-start | bytes 786440 | tf_op jit(solution)/shard_map/ppermute | solution.py:371
  3.1 2.2 %shard_map.100 = (f32[128,512]{1,0:T(8,128)S(1)}, f32[128,512]{1,0:T(8,128)S(1)}, f32[128,512]{1,0:T(8,128)S(1)}, f32[128,512]{1,0:T(8,128)S(1)}) custom-call(f32[1,65,4,512]{3,2,1,0:T(4,128)} %bitcast.2, s32[3,2048]{1,0:T(4,128)} %refs_2_.1, bf16[4,128,816]{2,1,0:T(8,128)(2,1)} %constant.14.clone.table_hbm), custom_call_target="tpu_custom_call" | custom-call | flops 2147483648 | bytes 1048576 | tf_op jit(solution)/shard_map/pallas_call | solution.py:377
  5.3 4.2 %collective-permute-done.3.refs_1_ = f32[32,16,128]{2,1,0:T(8,128)S(1)} collective-permute-done((f32[32,16,128]{2,1,0:T(8,128)}, f32[32,16,128]{2,1,0:T(8,128)S(1)}, u32[]{:S(2)}, u32[]{:S(2)}) %collective-permute-start.3) | collective-permute-done | bytes 262176 | tf_op jit(solution)/shard_map/ppermute | solution.py:371
  9.5 1.8 %collective-permute-start.5 = (f32[32,16,128]{2,1,0:T(8,128)S(1)}, f32[32,16,128]{2,1,0:T(8,128)S(1)}, u32[]{:S(2)}, u32[]{:S(2)}) collective-permute-start(f32[32,16,128]{2,1,0:T(8,128)S(1)} %collective-permute-done.3.refs_1_), channel_id=1, source_target_pairs={{0,8},{8,16},{16,24},{24,28},{28,20},{20,12},{12,4},{4,0},{1,9},{9... | collective-permute-start | bytes 786440 | tf_op jit(solution)/shard_map/ppermute | solution.py:371
  11.5 1.7 %collective-permute-start.1 = (f32[128,512]{1,0:T(8,128)S(1)}, f32[128,512]{1,0:T(8,128)S(1)}, u32[]{:S(2)}, u32[]{:S(2)}) collective-permute-start(f32[128,512]{1,0:T(8,128)S(1)} %get-tuple-element.15), channel_id=1, source_target_pairs={{0,2},{1,3},{2,0},{3,1},{4,6},{5,7},{6,4},{7,5},{8,10},{9,11},{10,... | collective-permute-start | bytes 786440 | tf_op jit(solution)/shard_map/ppermute | solution.py:361
  13.3 3.7 %collective-permute-done.5.refs_3_ = f32[32,16,128]{2,1,0:T(8,128)S(1)} collective-permute-done((f32[32,16,128]{2,1,0:T(8,128)S(1)}, f32[32,16,128]{2,1,0:T(8,128)S(1)}, u32[]{:S(2)}, u32[]{:S(2)}) %collective-permute-start.5) | collective-permute-done | bytes 262176 | tf_op jit(solution)/shard_map/ppermute | solution.py:371
  17.0 1.5 %collective-permute-start.7 = (f32[32,16,128]{2,1,0:T(8,128)S(1)}, f32[32,16,128]{2,1,0:T(8,128)S(1)}, u32[]{:S(2)}, u32[]{:S(2)}) collective-permute-start(f32[32,16,128]{2,1,0:T(8,128)S(1)} %collective-permute-done.5.refs_3_), channel_id=1, source_target_pairs={{0,8},{8,16},{16,24},{24,28},{28,20},{20,12},{12,4},{4,0},{1,9},{9... | collective-permute-start | bytes 786440 | tf_op jit(solution)/shard_map/ppermute | solution.py:371
  18.5 0.5 collective-permute-start.8
  19.0 1.6 %collective-permute-done.1.refs_2_ = f32[128,512]{1,0:T(8,128)S(1)} collective-permute-done((f32[128,512]{1,0:T(8,128)S(1)}, f32[128,512]{1,0:T(8,128)S(1)}, u32[]{:S(2)}, u32[]{:S(2)}) %collective-permute-start.1) | collective-permute-done | bytes 262176 | tf_op jit(solution)/shard_map/ppermute | solution.py:361
  20.7 2.4 %collective-permute-done.2.refs_3_ = f32[128,512]{1,0:T(8,128)S(1)} collective-permute-done((f32[128,512]{1,0:T(8,128)S(1)}, f32[128,512]{1,0:T(8,128)S(1)}, u32[]{:S(2)}, u32[]{:S(2)}) %collective-permute-start.2) | collective-permute-done | bytes 262176 | tf_op jit(solution)/shard_map/ppermute | solution.py:361
  23.0 3.6 %shard_map.101.half_ref = f32[4,1560,128]{2,1,0:T(8,128)S(1)} custom-call(f32[128,512]{1,0:T(8,128)S(1)} %get-tuple-element.13.refs_0_, f32[128,512]{1,0:T(8,128)S(1)} %collective-permute-done.refs_1_, f32[128,512]{1,0:T(8,128)S(1)} %collective-permute-done.1.refs_2_, f32[128,512]{1,0:T(8,128)S(1)} %collective-permute-done.2.refs_3_, ...), custom_call_target="tpu_custom_call" | custom-call | flops 4294967296 | bytes 1048576 | tf_op jit(solution)/shard_map/pallas_call | solution.py:377
  26.7 1.6 %collective-permute-start.10 = (f32[16,16,128]{2,1,0:T(8,128)S(1)}, f32[16,16,128]{2,1,0:T(8,128)S(1)}, u32[]{:S(2)}, u32[]{:S(2)}) collective-permute-start(f32[16,16,128]{2,1,0:T(8,128)S(1)} %slice.9), channel_id=1, source_target_pairs={{8,0},{16,8},{24,16},{28,24},{20,28},{12,20},{4,12},{0,4},{9,1},{1... | collective-permute-start | bytes 393224 | tf_op jit(solution)/shard_map/ppermute | solution.py:372
  28.3 0.6 %collective-permute-start.9 = (f32[16,16,128]{2,1,0:T(8,128)S(1)}, f32[16,16,128]{2,1,0:T(8,128)S(1)}, u32[]{:S(2)}, u32[]{:S(2)}) collective-permute-start(f32[16,16,128]{2,1,0:T(8,128)S(1)} %slice.8), channel_id=1, source_target_pairs={{0,8},{8,16},{16,24},{24,28},{28,20},{20,12},{12,4},{4,0},{1,9},{9... | collective-permute-start | bytes 393224 | tf_op jit(solution)/shard_map/ppermute | solution.py:371
  28.9 4.0 %shard_map.102 = (f32[4,1560,128]{2,1,0:T(8,128)S(1)}, f32[32,16,256]{2,1,0:T(8,128)S(1)}) custom-call(f32[4,1560,128]{2,1,0:T(8,128)S(1)} %shard_map.101.half_ref, f32[32,16,128]{2,1,0:T(8,128)S(1)} %copy-done, f32[32,16,128]{2,1,0:T(8,128)S(1)} %collective-permute-done.3.refs_1_, f32[32,16,128]{2,1,0:T(8,128)S(1)} %collective-permute-done.4.refs_2_, ...), custom_call_target="tpu_custom_call" | custom-call | flops 4294967296 | bytes 1048576 | tf_op jit(solution)/shard_map/pallas_call | solution.py:377
  32.9 1.5 %collective-permute-done.9.up_ref = f32[16,16,128]{2,1,0:T(8,128)S(1)} collective-permute-done((f32[16,16,128]{2,1,0:T(8,128)S(1)}, f32[16,16,128]{2,1,0:T(8,128)S(1)}, u32[]{:S(2)}, u32[]{:S(2)}) %collective-permute-start.9) | collective-permute-done | bytes 131104 | tf_op jit(solution)/shard_map/ppermute | solution.py:371
  34.5 2.6 %shard_map.103.flat_ref = bf16[256,2176]{1,0:T(8,128)(2,1)S(1)} custom-call(f32[4,1560,128]{2,1,0:T(8,128)S(1)} %get-tuple-element.17.first_ref, f32[32,16,256]{2,1,0:T(8,128)S(1)} %get-tuple-element.18.real_ref, f32[16,16,128]{2,1,0:T(8,128)S(1)} %collective-permute-done.9.up_ref, f32[16,16,128]{2,1,0:T(8,128)S(1)} %collective-permute-done.10.down_ref, ...), custom_call_target="tpu_custom_call" | custom-call | flops 4294967296 | bytes 1048576 | tf_op jit(solution)/shard_map/pallas_call | solution.py:377
  37.0 1.4 %shard_map.105 = (f32[128,512]{1,0:T(8,128)S(1)}, f32[128,512]{1,0:T(8,128)S(1)}) custom-call(bf16[256,2176]{1,0:T(8,128)(2,1)S(1)} %shard_map.103.flat_ref, s32[3,2048]{1,0:T(4,128)S(1)} %copy-done.1), custom_call_target="tpu_custom_call" | custom-call | flops 2147483648 | bytes 1048576 | tf_op jit(solution)/shard_map/pallas_call | solution.py:377
  38.4 0.8 %shard_map.106 = f32[128,512]{1,0:T(8,128)S(1)} custom-call(bf16[256,2176]{1,0:T(8,128)(2,1)S(1)} %shard_map.103.flat_ref, s32[3,2048]{1,0:T(4,128)S(1)} %copy-done.1), custom_call_target="tpu_custom_call" | custom-call | flops 2147483648 | bytes 1048576 | tf_op jit(solution)/shard_map/pallas_call | solution.py:377
  39.6 0.8 %shard_map.104 = f32[128,512]{1,0:T(8,128)S(1)} custom-call(bf16[256,2176]{1,0:T(8,128)(2,1)S(1)} %shard_map.103.flat_ref, s32[3,2048]{1,0:T(4,128)S(1)} %copy-done.1), custom_call_target="tpu_custom_call" | custom-call | flops 2147483648 | bytes 1048576 | tf_op jit(solution)/shard_map/pallas_call | solution.py:377
  40.4 1.9 %collective-permute-start.11 = (f32[128,512]{1,0:T(8,128)S(1)}, f32[128,512]{1,0:T(8,128)S(1)}, u32[]{:S(2)}, u32[]{:S(2)}) collective-permute-start(f32[128,512]{1,0:T(8,128)S(1)} %shard_map.104), channel_id=1, source_target_pairs={{0,2},{1,3},{2,0},{3,1},{4,6},{5,7},{6,4},{7,5},{8,10},{9,11},{10,... | collective-permute-start | bytes 786440 | tf_op jit(solution)/shard_map/ppermute | solution.py:361
  42.3 5.1 %collective-permute-done.13.refs_2_ = f32[128,512]{1,0:T(8,128)S(1)} collective-permute-done((f32[128,512]{1,0:T(8,128)S(1)}, f32[128,512]{1,0:T(8,128)S(1)}, u32[]{:S(2)}, u32[]{:S(2)}) %collective-permute-start.13) | collective-permute-done | bytes 262176 | tf_op jit(solution)/shard_map/ppermute | solution.py:361
  47.4 0.6 %shard_map.107.refs_1_ = f32[272,512]{1,0:T(8,128)S(1)} custom-call(f32[128,512]{1,0:T(8,128)S(1)} %get-tuple-element.19.refs_0_, f32[128,512]{1,0:T(8,128)S(1)} %collective-permute-done.12.refs_1_, f32[128,512]{1,0:T(8,128)S(1)} %collective-permute-done.13.refs_2_, bf16[4,272,256]{2,1,0:T(8,128)(2,1)S(1)} %copy-done.2), custom_call_target="tpu_custom_call" | custom-call | flops 2147483648 | bytes 1048576 | tf_op jit(solution)/shard_map/pallas_call | solution.py:377
  48.0 5.6 %collective-permute-done.11.refs_0_ = f32[128,512]{1,0:T(8,128)S(1)} collective-permute-done((f32[128,512]{1,0:T(8,128)S(1)}, f32[128,512]{1,0:T(8,128)S(1)}, u32[]{:S(2)}, u32[]{:S(2)}) %collective-permute-start.11) | collective-permute-done | bytes 262176 | tf_op jit(solution)/shard_map/ppermute | solution.py:361
  53.6 1.1 %shard_map.108 = f32[1,65,4,512]{3,2,1,0:T(4,128)} custom-call(f32[128,512]{1,0:T(8,128)S(1)} %collective-permute-done.11.refs_0_, f32[272,512]{1,0:T(8,128)S(1)} %shard_map.107.refs_1_, s32[3,2048]{1,0:T(4,128)S(1)} %copy-done.1, bf16[4,272,256]{2,1,0:T(8,128)(2,1)S(1)} %copy-done.2), custom_call_target="tpu_custom_call" | custom-call | flops 2147483648 | bytes 1048576 | tf_op jit(solution)/shard_map/pallas_call | solution.py:377
  (31 shorter events, 0.8 us)
Async XLA Ops:
  0.0 9.5 %collective-permute-start.3 = (f32[32,16,128]{2,1,0:T(8,128)}, f32[32,16,128]{2,1,0:T(8,128)S(1)}, u32[]{:S(2)}, u32[]{:S(2)}) collective-permute-start(f32[32,16,128]{2,1,0:T(8,128)} %refs_0_.1), channel_id=1, source_target_pairs={{0,8},{8,16},{16,24},{24,28},{28,20},{20,12},{12,4},{4,0},{1,9},{9... | collective-permute-start | bytes 786440 | tf_op jit(solution)/shard_map/ppermute | solution.py:371
  3.1 8.3 %collective-permute-start.4 = (f32[32,16,128]{2,1,0:T(8,128)}, f32[32,16,128]{2,1,0:T(8,128)S(1)}, u32[]{:S(2)}, u32[]{:S(2)}) collective-permute-start(f32[32,16,128]{2,1,0:T(8,128)} %refs_0_.1), channel_id=1, source_target_pairs={{8,0},{16,8},{24,16},{28,24},{20,28},{12,20},{4,12},{0,4},{9,1},{1... | collective-permute-start | bytes 786440 | tf_op jit(solution)/shard_map/ppermute | solution.py:372
  3.1 20.0 %copy-start.1 = (s32[3,2048]{1,0:T(4,128)S(1)}, s32[3,2048]{1,0:T(4,128)}, u32[]{:S(2)}) copy-start(s32[3,2048]{1,0:T(4,128)} %refs_2_.1) | copy-start | bytes 73732
  3.1 20.0 %copy-start.4 = (bf16[2,256,512]{2,1,0:T(8,128)(2,1)S(1)}, bf16[2,256,512]{2,1,0:T(8,128)(2,1)}, u32[]{:S(2)}) copy-start(bf16[2,256,512]{2,1,0:T(8,128)(2,1)} %constant.16.clone.refs_5_) | copy-start | bytes 1572868
  5.2 13.8 %collective-permute-start = (f32[128,512]{1,0:T(8,128)S(1)}, f32[128,512]{1,0:T(8,128)S(1)}, u32[]{:S(2)}, u32[]{:S(2)}) collective-permute-start(f32[128,512]{1,0:T(8,128)S(1)} %get-tuple-element.14), channel_id=1, source_target_pairs={{0,1},{1,0},{2,3},{3,2},{4,5},{5,4},{6,7},{7,6},{8,9},{9,8},{10,11... | collective-permute-start | bytes 786440 | tf_op jit(solution)/shard_map/ppermute | solution.py:361
  9.5 7.5 %collective-permute-start.5 = (f32[32,16,128]{2,1,0:T(8,128)S(1)}, f32[32,16,128]{2,1,0:T(8,128)S(1)}, u32[]{:S(2)}, u32[]{:S(2)}) collective-permute-start(f32[32,16,128]{2,1,0:T(8,128)S(1)} %collective-permute-done.3.refs_1_), channel_id=1, source_target_pairs={{0,8},{8,16},{16,24},{24,28},{28,20},{20,12},{12,4},{4,0},{1,9},{9... | collective-permute-start | bytes 786440 | tf_op jit(solution)/shard_map/ppermute | solution.py:371
  11.3 7.2 %collective-permute-start.6 = (f32[32,16,128]{2,1,0:T(8,128)S(1)}, f32[32,16,128]{2,1,0:T(8,128)S(1)}, u32[]{:S(2)}, u32[]{:S(2)}) collective-permute-start(f32[32,16,128]{2,1,0:T(8,128)S(1)} %collective-permute-done.4.refs_2_), channel_id=1, source_target_pairs={{8,0},{16,8},{24,16},{28,24},{20,28},{12,20},{4,12},{0,4},{9,1},{1... | collective-permute-start | bytes 786440 | tf_op jit(solution)/shard_map/ppermute | solution.py:372
  11.5 9.1 %collective-permute-start.1 = (f32[128,512]{1,0:T(8,128)S(1)}, f32[128,512]{1,0:T(8,128)S(1)}, u32[]{:S(2)}, u32[]{:S(2)}) collective-permute-start(f32[128,512]{1,0:T(8,128)S(1)} %get-tuple-element.15), channel_id=1, source_target_pairs={{0,2},{1,3},{2,0},{3,1},{4,6},{5,7},{6,4},{7,5},{8,10},{9,11},{10,... | collective-permute-start | bytes 786440 | tf_op jit(solution)/shard_map/ppermute | solution.py:361
  13.3 9.8 %collective-permute-start.2 = (f32[128,512]{1,0:T(8,128)S(1)}, f32[128,512]{1,0:T(8,128)S(1)}, u32[]{:S(2)}, u32[]{:S(2)}) collective-permute-start(f32[128,512]{1,0:T(8,128)S(1)} %get-tuple-element.16), channel_id=1, source_target_pairs={{0,3},{1,2},{2,1},{3,0},{4,7},{5,6},{6,5},{7,4},{8,11},{9,10},{10,... | collective-permute-start | bytes 786440 | tf_op jit(solution)/shard_map/ppermute | solution.py:361
  17.0 11.3 %collective-permute-start.7 = (f32[32,16,128]{2,1,0:T(8,128)S(1)}, f32[32,16,128]{2,1,0:T(8,128)S(1)}, u32[]{:S(2)}, u32[]{:S(2)}) collective-permute-start(f32[32,16,128]{2,1,0:T(8,128)S(1)} %collective-permute-done.5.refs_3_), channel_id=1, source_target_pairs={{0,8},{8,16},{16,24},{24,28},{28,20},{20,12},{12,4},{4,0},{1,9},{9... | collective-permute-start | bytes 786440 | tf_op jit(solution)/shard_map/ppermute | solution.py:371
  18.5 8.2 %collective-permute-start.8 = (f32[32,16,128]{2,1,0:T(8,128)S(1)}, f32[32,16,128]{2,1,0:T(8,128)S(1)}, u32[]{:S(2)}, u32[]{:S(2)}) collective-permute-start(f32[32,16,128]{2,1,0:T(8,128)S(1)} %collective-permute-done.6.refs_4_), channel_id=1, source_target_pairs={{8,0},{16,8},{24,16},{28,24},{20,28},{12,20},{4,12},{0,4},{9,1},{1... | collective-permute-start | bytes 786440 | tf_op jit(solution)/shard_map/ppermute | solution.py:372
  23.0 5.9 %copy-start = (f32[32,16,128]{2,1,0:T(8,128)S(1)}, f32[32,16,128]{2,1,0:T(8,128)}, u32[]{:S(2)}) copy-start(f32[32,16,128]{2,1,0:T(8,128)} %refs_0_.1) | copy-start | bytes 786436
  23.0 5.9 %copy-start.6 = (bf16[160,256]{1,0:T(8,128)(2,1)S(1)}, bf16[160,256]{1,0:T(8,128)(2,1)}, u32[]{:S(2)}) copy-start(bf16[160,256]{1,0:T(8,128)(2,1)} %constant.20.clone.refs_8_) | copy-start | bytes 245764
  23.0 5.9 %copy-start.7 = (bf16[128,240]{1,0:T(8,128)(2,1)S(1)}, bf16[128,240]{1,0:T(8,128)(2,1)}, u32[]{:S(2)}) copy-start(bf16[128,240]{1,0:T(8,128)(2,1)} %constant.18.clone.refs_7_) | copy-start | bytes 184324
  26.7 6.2 %collective-permute-start.10 = (f32[16,16,128]{2,1,0:T(8,128)S(1)}, f32[16,16,128]{2,1,0:T(8,128)S(1)}, u32[]{:S(2)}, u32[]{:S(2)}) collective-permute-start(f32[16,16,128]{2,1,0:T(8,128)S(1)} %slice.9), channel_id=1, source_target_pairs={{8,0},{16,8},{24,16},{28,24},{20,28},{12,20},{4,12},{0,4},{9,1},{1... | collective-permute-start | bytes 393224 | tf_op jit(solution)/shard_map/ppermute | solution.py:372
  28.3 6.2 %copy-start.3 = (bf16[2,512,256]{2,1,0:T(8,128)(2,1)S(1)}, bf16[2,512,256]{2,1,0:T(8,128)(2,1)}, u32[]{:S(2)}) copy-start(bf16[2,512,256]{2,1,0:T(8,128)(2,1)} %constant.17.clone.y_back_ref) | copy-start | bytes 1572868
  28.3 6.1 %copy-start.5 = (bf16[8,80,48]{2,1,0:T(8,128)(2,1)S(1)}, bf16[8,80,48]{2,1,0:T(8,128)(2,1)}, u32[]{:S(2)}) copy-start(bf16[8,80,48]{2,1,0:T(8,128)(2,1)} %constant.19.clone.x_last_ref) | copy-start | bytes 184324
  28.3 6.1 %collective-permute-start.9 = (f32[16,16,128]{2,1,0:T(8,128)S(1)}, f32[16,16,128]{2,1,0:T(8,128)S(1)}, u32[]{:S(2)}, u32[]{:S(2)}) collective-permute-start(f32[16,16,128]{2,1,0:T(8,128)S(1)} %slice.8), channel_id=1, source_target_pairs={{0,8},{8,16},{16,24},{24,28},{28,20},{20,12},{12,4},{4,0},{1,9},{9... | collective-permute-start | bytes 393224 | tf_op jit(solution)/shard_map/ppermute | solution.py:371
  39.2 8.2 %copy-start.2 = (bf16[4,272,256]{2,1,0:T(8,128)(2,1)S(1)}, bf16[4,272,256]{2,1,0:T(8,128)(2,1)}, u32[]{:S(2)}) copy-start(bf16[4,272,256]{2,1,0:T(8,128)(2,1)} %constant.15.clone.refs_3_) | copy-start | bytes 1671172
  39.2 3.1 %collective-permute-start.12 = (f32[128,512]{1,0:T(8,128)S(1)}, f32[128,512]{1,0:T(8,128)S(1)}, u32[]{:S(2)}, u32[]{:S(2)}) collective-permute-start(f32[128,512]{1,0:T(8,128)S(1)} %get-tuple-element.20), channel_id=1, source_target_pairs={{0,1},{1,0},{2,3},{3,2},{4,5},{5,4},{6,7},{7,6},{8,9},{9,8},{10,11... | collective-permute-start | bytes 786440 | tf_op jit(solution)/shard_map/ppermute | solution.py:361
  39.3 8.1 %collective-permute-start.13 = (f32[128,512]{1,0:T(8,128)S(1)}, f32[128,512]{1,0:T(8,128)S(1)}, u32[]{:S(2)}, u32[]{:S(2)}) collective-permute-start(f32[128,512]{1,0:T(8,128)S(1)} %shard_map.106), channel_id=1, source_target_pairs={{0,3},{1,2},{2,1},{3,0},{4,7},{5,6},{6,5},{7,4},{8,11},{9,10},{10,... | collective-permute-start | bytes 786440 | tf_op jit(solution)/shard_map/ppermute | solution.py:361
  40.4 13.2 %collective-permute-start.11 = (f32[128,512]{1,0:T(8,128)S(1)}, f32[128,512]{1,0:T(8,128)S(1)}, u32[]{:S(2)}, u32[]{:S(2)}) collective-permute-start(f32[128,512]{1,0:T(8,128)S(1)} %shard_map.104), channel_id=1, source_target_pairs={{0,2},{1,3},{2,0},{3,1},{4,6},{5,7},{6,4},{7,5},{8,10},{9,11},{10,... | collective-permute-start | bytes 786440 | tf_op jit(solution)/shard_map/ppermute | solution.py:361

commit v3 on v2

--- a/solution.py
+++ b/solution.py
@@ -149,7 +149,7 @@
     high, low = split(jnp.concatenate([data, gap], 0))
     data = jnp.concatenate([high, high, low], 0)
     copies[2].wait()
-    for k in reversed(range(s.devices)):
+    for k in [*partners(s.devices), 0]:
         out_refs[k][...] = dot(table_ref[partner(me, k)], data)
 
 
@@ -187,15 +187,19 @@
     return jnp.where(x_all == jnp.asarray(x, bf16), y_all, jnp.zeros_like(y_all))
 
 
-def plane_kernel(s, *refs):
-    in_refs, (sticks_ref, table_ref, out_ref, x_ref, y_ref, grid_ref, both_ref) = refs[: s.devices], refs[s.devices :]
+def lay_kernel(s, which, started, ended, *refs):
+    in_refs, refs = refs[: len(which)], refs[len(which) :]
+    before_ref, refs = (refs[0], refs[1:]) if started else (None, refs)
+    sticks_ref, refs = refs[0], refs[1:]
+    table_ref, out_ref, grid_ref = refs[:3] if ended else (None, None, refs[0])
+    x_ref, y_ref, both_ref = refs[-3:]
     me = lax.axis_index("plane")
-    places(s, sticks_ref, [partner(me, k) for k in range(s.devices)], x_ref, y_ref)
+    places(s, sticks_ref, [partner(me, k) for k in which], x_ref, y_ref)
     rows = 2 * s.batch
-    for k in range(s.devices):
-        high, low = split(in_refs[k][...])
-        both_ref[:rows, k * s.sticks : (k + 1) * s.sticks] = high
-        both_ref[rows:, k * s.sticks : (k + 1) * s.sticks] = low
+    for i in range(len(which)):
+        high, low = split(in_refs[i][...])
+        both_ref[:rows, i * s.sticks : (i + 1) * s.sticks] = high
+        both_ref[rows:, i * s.sticks : (i + 1) * s.sticks] = low
     lanes = 2 * s.rows_y
     for first in range(0, s.tiles, 2):
         count = min(2, s.tiles - first)
@@ -204,9 +208,11 @@
         laid = laid[:rows] + laid[rows:]
         for t in range(count):
             for component in range(2):
-                grid_ref[
-                    pl.ds((first + t) * s.batch, s.batch), component * lanes : (component + 1) * lanes
-                ] = laid[component * s.batch : (component + 1) * s.batch, t * lanes : (t + 1) * lanes]
+                own = pl.ds((first + t) * s.batch, s.batch), slice(component * lanes, (component + 1) * lanes)
+                part = laid[component * s.batch : (component + 1) * s.batch, t * lanes : (t + 1) * lanes]
+                grid_ref[own] = part + before_ref[own] if started else part
+    if not ended:
+        return
     total = s.tiles * s.batch
     table = jnp.concatenate([table_ref[0], table_ref[0], table_ref[1]], 0)
     for start in range(0, total, 4 * s.batch):
@@ -344,6 +350,15 @@
     return offsets
 
 
+def partners(devices):
+    return sorted(range(1, devices), key=lambda k: (k == 1, k % 2, k))
+
+
+def stages(devices):
+    far = partners(devices)[:-1]
+    return [("lay1", [0, 1]), ("lay2", far[:-1]), ("lay3", far[-1:])]
+
+
 def per_device(bands, coeffs, potential, stick_map):
     devices = stick_map.shape[1] // coeffs.shape[3]
     s = Sizes(coeffs.shape[2], coeffs.shape[3], potential.shape[2], potential.shape[0], devices)
@@ -357,7 +372,7 @@
 
     def exchange(blocks):
         out = [blocks[0]] + [None] * (devices - 1)
-        for k in reversed(range(1, devices)):
+        for k in partners(devices):
             out[k] = lax.ppermute(blocks[k], "plane", [(i, i ^ k) for i in range(devices)])
         return out
 
@@ -385,7 +400,6 @@
         )(*inputs)
 
     slabs = ring()
-    total = devices * s.sticks
     positions = 2 * s.tiles * s.rows_y
     results = []
     for pair in range(coeffs.shape[0]):
@@ -405,19 +419,21 @@
             HBM,
         )
         held = exchange(sent)
-        half = kernel(
-            functools.partial(plane_kernel, s),
-            [*held, stick_map, tab["y_ahead"]],
-            jax.ShapeDtypeStruct((4, s.even * s.step, s.length), f32),
-            28 << 10,
-            1 << 32,
-            [
-                pltpu.VMEM((s.rows_y, total), bf16),
-                pltpu.VMEM((s.rows_y, total), bf16),
-                pltpu.VMEM((s.tiles * s.batch, 4 * s.rows_y), f32),
-                pltpu.VMEM((2 * rows, total), bf16),
-            ],
-        )
+        half = None
+        grid_shape = (s.tiles * s.batch, 4 * s.rows_y)
+        for name, which in stages(devices):
+            started, ended = half is not None, name == "lay3"
+            shape = (4, s.even * s.step, s.length) if ended else grid_shape
+            own = [pltpu.VMEM((s.rows_y, len(which) * s.sticks), bf16)] * 2
+            own.append(pltpu.VMEM((2 * rows, len(which) * s.sticks), bf16))
+            half = kernel(
+                functools.partial(lay_kernel, s, which, started, ended),
+                [held[k] for k in which] + [half] * started + [stick_map] + [tab["y_ahead"]] * ended,
+                jax.ShapeDtypeStruct(shape, f32),
+                24 << 10,
+                1 << 31,
+                [pltpu.VMEM(grid_shape, f32)] * ended + own,
+            )
         turned_shape = (4, s.even * s.step, s.length)
         turned, real = kernel(
             functools.partial(space_kernel, s, bands),
@@ -439,7 +455,7 @@
             [pltpu.VMEM(turned_shape, f32)],
         )
         mixed = [None] * devices
-        groups = [[k] for k in reversed(range(2, devices))] + [list(range(min(2, devices)))[::-1]]
+        groups = [[k] for k in partners(devices)[:-1]] + [[1, 0]]
         for which in groups:
             parts = kernel(
                 functools.partial(pick_kernel, s, which),
@@ -456,7 +472,8 @@
             for k, part in zip(which, parts, strict=True):
                 mixed[k] = part
         returned = exchange(mixed)
-        early = [k for k in range(devices) if k != 2]
+        late = partners(devices)[-2]
+        early = [k for k in range(devices) if k != late]
         begun = kernel(
             functools.partial(back_kernel, s, early, False, False),
             [*(returned[k] for k in early), tab["z_back"]],
@@ -465,8 +482,8 @@
             1 << 31,
         )
         result = kernel(
-            functools.partial(back_kernel, s, [2], True, True),
-            [returned[2], begun, stick_map, tab["z_back"]],
+            functools.partial(back_kernel, s, [late], True, True),
+            [returned[late], begun, stick_map, tab["z_back"]],
             jax.ShapeDtypeStruct((1,) + given.shape[1:], f32),
             16 << 10,
             1 << 31,

time: 54.9 us -> 52.5 us (0.956)
  the two profiles are of different devices: /device:TPU:0 before, /device:TPU:1 now
where the time goes in v3:
time: 52.5 us; the launch traced here: 52.2 us
  waiting for transfers between devices  20.9 us (40%)
  Pallas kernels  17.4 us (33%)
  starting transfers between devices  13.6 us (26%)
    pallas_call x11, Pallas kernels, kernel(): pl.pallas_call(body, in_specs=[place] * len(inputs), out_specs=jax.tree.m...  17.4 us
    ppermute x6, waiting for transfers between devices, exchange(): lax.ppermute(blocks[k], 'plane', [(i, i ^ k) for i in range(devices)])  16.9 us
    ppermute x6, starting transfers between devices, exchange(): lax.ppermute(blocks[k], 'plane', [(i, i ^ k) for i in range(devices)])  6.97 us
    ppermute x4, starting transfers between devices, ring(): up = lax.ppermute(up, 'band', along)  5.18 us
    ppermute x4, waiting for transfers between devices, ring(): up = lax.ppermute(up, 'band', along)  3.99 us
    ppermute x4, starting transfers between devices, ring(): down = lax.ppermute(down, 'band', against)  1.44 us
  transfers between devices with their start and end apart: 14, of which 6 were waited for; matrix products, arithmetic and copies ran while one was open for 0% of the time, Pallas kernels for 22%

profile of v3, /device:TPU:1, one launch (start us, length us, event | category | flops | bytes accessed | tf_op | source)
XLA Modules:
  0.0 52.2 jit_solution(829790247800173869)
XLA Ops:
  0.0 2.1 %collective-permute-start.3 = (f32[32,16,128]{2,1,0:T(8,128)}, f32[32,16,128]{2,1,0:T(8,128)S(1)}, u32[]{:S(2)}, u32[]{:S(2)}) collective-permute-start(f32[32,16,128]{2,1,0:T(8,128)} %refs_0_.1), channel_id=1, source_target_pairs={{0,8},{8,16},{16,24},{24,28},{28,20},{20,12},{12,4},{4,0},{1,9},{9... | collective-permute-start | bytes 786440 | tf_op jit(solution)/shard_map/ppermute | solution.py:386
  2.1 2.1 %shard_map.100 = (f32[128,512]{1,0:T(8,128)S(1)}, f32[128,512]{1,0:T(8,128)S(1)}, f32[128,512]{1,0:T(8,128)S(1)}, f32[128,512]{1,0:T(8,128)S(1)}) custom-call(f32[1,65,4,512]{3,2,1,0:T(4,128)} %bitcast.2, s32[3,2048]{1,0:T(4,128)} %refs_2_.7, bf16[4,128,816]{2,1,0:T(8,128)(2,1)} %constant.14.clone.table_hbm), custom_call_target="tpu_custom_call" | custom-call | flops 2147483648 | bytes 1048576 | tf_op jit(solution)/shard_map/pallas_call | solution.py:392
  4.2 1.0 %collective-permute-start.2 = (f32[128,512]{1,0:T(8,128)S(1)}, f32[128,512]{1,0:T(8,128)S(1)}, u32[]{:S(2)}, u32[]{:S(2)}) collective-permute-start(f32[128,512]{1,0:T(8,128)S(1)} %get-tuple-element.16), channel_id=1, source_target_pairs={{0,1},{1,0},{2,3},{3,2},{4,5},{5,4},{6,7},{7,6},{8,9},{9,8},{10,11... | collective-permute-start | bytes 786440 | tf_op jit(solution)/shard_map/ppermute | solution.py:376
  5.3 3.0 %collective-permute-done.3.refs_1_ = f32[32,16,128]{2,1,0:T(8,128)S(1)} collective-permute-done((f32[32,16,128]{2,1,0:T(8,128)}, f32[32,16,128]{2,1,0:T(8,128)S(1)}, u32[]{:S(2)}, u32[]{:S(2)}) %collective-permute-start.3) | collective-permute-done | bytes 262176 | tf_op jit(solution)/shard_map/ppermute | solution.py:386
  8.3 1.2 %collective-permute-start.5 = (f32[32,16,128]{2,1,0:T(8,128)S(1)}, f32[32,16,128]{2,1,0:T(8,128)S(1)}, u32[]{:S(2)}, u32[]{:S(2)}) collective-permute-start(f32[32,16,128]{2,1,0:T(8,128)S(1)} %collective-permute-done.3.refs_1_), channel_id=1, source_target_pairs={{0,8},{8,16},{16,24},{24,28},{28,20},{20,12},{12,4},{4,0},{1,9},{9... | collective-permute-start | bytes 786440 | tf_op jit(solution)/shard_map/ppermute | solution.py:386
  9.7 1.2 %collective-permute-start.1 = (f32[128,512]{1,0:T(8,128)S(1)}, f32[128,512]{1,0:T(8,128)S(1)}, u32[]{:S(2)}, u32[]{:S(2)}) collective-permute-start(f32[128,512]{1,0:T(8,128)S(1)} %get-tuple-element.14), channel_id=1, source_target_pairs={{0,2},{1,3},{2,0},{3,1},{4,6},{5,7},{6,4},{7,5},{8,10},{9,11},{10,... | collective-permute-start | bytes 786440 | tf_op jit(solution)/shard_map/ppermute | solution.py:376
  10.9 2.3 %collective-permute-start = (f32[128,512]{1,0:T(8,128)S(1)}, f32[128,512]{1,0:T(8,128)S(1)}, u32[]{:S(2)}, u32[]{:S(2)}) collective-permute-start(f32[128,512]{1,0:T(8,128)S(1)} %get-tuple-element.13), channel_id=1, source_target_pairs={{0,3},{1,2},{2,1},{3,0},{4,7},{5,6},{6,5},{7,4},{8,11},{9,10},{10,... | collective-permute-start | bytes 786440 | tf_op jit(solution)/shard_map/ppermute | solution.py:376
  13.2 1.4 %shard_map.101.refs_1_ = f32[1088,256]{1,0:T(8,128)S(1)} custom-call(f32[128,512]{1,0:T(8,128)S(1)} %get-tuple-element.15.refs_0_, f32[128,512]{1,0:T(8,128)S(1)} %collective-permute-done.2.refs_1_, s32[3,2048]{1,0:T(4,128)S(1)} %copy-done.1), custom_call_target="tpu_custom_call" | custom-call | flops 2147483648 | bytes 1048576 | tf_op jit(solution)/shard_map/pallas_call | solution.py:392
  14.9 1.3 %collective-permute-start.7 = (f32[32,16,128]{2,1,0:T(8,128)S(1)}, f32[32,16,128]{2,1,0:T(8,128)S(1)}, u32[]{:S(2)}, u32[]{:S(2)}) collective-permute-start(f32[32,16,128]{2,1,0:T(8,128)S(1)} %collective-permute-done.5.refs_3_), channel_id=1, source_target_pairs={{0,8},{8,16},{16,24},{24,28},{28,20},{20,12},{12,4},{4,0},{1,9},{9... | collective-permute-start | bytes 786440 | tf_op jit(solution)/shard_map/ppermute | solution.py:386
  16.4 0.8 %shard_map.102.refs_1_ = f32[1088,256]{1,0:T(8,128)S(1)} custom-call(f32[128,512]{1,0:T(8,128)S(1)} %collective-permute-done.1.refs_0_, f32[1088,256]{1,0:T(8,128)S(1)} %shard_map.101.refs_1_, s32[3,2048]{1,0:T(4,128)S(1)} %copy-done.1), custom_call_target="tpu_custom_call" | custom-call | flops 2147483648 | bytes 1048576 | tf_op jit(solution)/shard_map/pallas_call | solution.py:392
  17.2 6.5 %collective-permute-done.refs_0_ = f32[128,512]{1,0:T(8,128)S(1)} collective-permute-done((f32[128,512]{1,0:T(8,128)S(1)}, f32[128,512]{1,0:T(8,128)S(1)}, u32[]{:S(2)}, u32[]{:S(2)}) %collective-permute-start) | collective-permute-done | bytes 262176 | tf_op jit(solution)/shard_map/ppermute | solution.py:376
  23.7 1.8 %shard_map.103.half_ref = f32[4,1560,128]{2,1,0:T(8,128)S(1)} custom-call(f32[128,512]{1,0:T(8,128)S(1)} %collective-permute-done.refs_0_, f32[1088,256]{1,0:T(8,128)S(1)} %shard_map.102.refs_1_, s32[3,2048]{1,0:T(4,128)S(1)} %copy-done.1, bf16[2,256,512]{2,1,0:T(8,128)(2,1)S(1)} %copy-done.4), custom_call_target="tpu_custom_call" | custom-call | flops 2147483648 | bytes 1048576 | tf_op jit(solution)/shard_map/pallas_call | solution.py:392
  25.5 1.1 %collective-permute-start.10 = (f32[16,16,128]{2,1,0:T(8,128)S(1)}, f32[16,16,128]{2,1,0:T(8,128)S(1)}, u32[]{:S(2)}, u32[]{:S(2)}) collective-permute-start(f32[16,16,128]{2,1,0:T(8,128)S(1)} %slice.9), channel_id=1, source_target_pairs={{8,0},{16,8},{24,16},{28,24},{20,28},{12,20},{4,12},{0,4},{9,1},{1... | collective-permute-start | bytes 393224 | tf_op jit(solution)/shard_map/ppermute | solution.py:387
  27.1 4.0 %shard_map.104 = (f32[4,1560,128]{2,1,0:T(8,128)S(1)}, f32[32,16,256]{2,1,0:T(8,128)S(1)}) custom-call(f32[4,1560,128]{2,1,0:T(8,128)S(1)} %shard_map.103.half_ref, f32[32,16,128]{2,1,0:T(8,128)S(1)} %copy-done, f32[32,16,128]{2,1,0:T(8,128)S(1)} %collective-permute-done.3.refs_1_, f32[32,16,128]{2,1,0:T(8,128)S(1)} %collective-permute-done.4.refs_2_, ...), custom_call_target="tpu_custom_call" | custom-call | flops 4294967296 | bytes 1048576 | tf_op jit(solution)/shard_map/pallas_call | solution.py:392
  31.2 0.7 %collective-permute-done.9.up_ref = f32[16,16,128]{2,1,0:T(8,128)S(1)} collective-permute-done((f32[16,16,128]{2,1,0:T(8,128)S(1)}, f32[16,16,128]{2,1,0:T(8,128)S(1)}, u32[]{:S(2)}, u32[]{:S(2)}) %collective-permute-start.9) | collective-permute-done | bytes 131104 | tf_op jit(solution)/shard_map/ppermute | solution.py:386
  31.9 2.6 %shard_map.105.flat_ref = bf16[256,2176]{1,0:T(8,128)(2,1)S(1)} custom-call(f32[4,1560,128]{2,1,0:T(8,128)S(1)} %get-tuple-element.17.first_ref, f32[32,16,256]{2,1,0:T(8,128)S(1)} %get-tuple-element.18.real_ref, f32[16,16,128]{2,1,0:T(8,128)S(1)} %collective-permute-done.9.up_ref, f32[16,16,128]{2,1,0:T(8,128)S(1)} %collective-permute-done.10.down_ref, ...), custom_call_target="tpu_custom_call" | custom-call | flops 4294967296 | bytes 1048576 | tf_op jit(solution)/shard_map/pallas_call | solution.py:392
  34.5 1.4 %shard_map.107 = (f32[128,512]{1,0:T(8,128)S(1)}, f32[128,512]{1,0:T(8,128)S(1)}) custom-call(bf16[256,2176]{1,0:T(8,128)(2,1)S(1)} %shard_map.105.flat_ref, s32[3,2048]{1,0:T(4,128)S(1)} %copy-done.1), custom_call_target="tpu_custom_call" | custom-call | flops 2147483648 | bytes 1048576 | tf_op jit(solution)/shard_map/pallas_call | solution.py:392
  35.9 0.8 %shard_map.108 = f32[128,512]{1,0:T(8,128)S(1)} custom-call(bf16[256,2176]{1,0:T(8,128)(2,1)S(1)} %shard_map.105.flat_ref, s32[3,2048]{1,0:T(4,128)S(1)} %copy-done.1), custom_call_target="tpu_custom_call" | custom-call | flops 2147483648 | bytes 1048576 | tf_op jit(solution)/shard_map/pallas_call | solution.py:392
  36.7 0.7 %collective-permute-start.12 = (f32[128,512]{1,0:T(8,128)S(1)}, f32[128,512]{1,0:T(8,128)S(1)}, u32[]{:S(2)}, u32[]{:S(2)}) collective-permute-start(f32[128,512]{1,0:T(8,128)S(1)} %get-tuple-element.20), channel_id=1, source_target_pairs={{0,1},{1,0},{2,3},{3,2},{4,5},{5,4},{6,7},{7,6},{8,9},{9,8},{10,11... | collective-permute-start | bytes 786440 | tf_op jit(solution)/shard_map/ppermute | solution.py:376
  37.4 0.8 %shard_map.106 = f32[128,512]{1,0:T(8,128)S(1)} custom-call(bf16[256,2176]{1,0:T(8,128)(2,1)S(1)} %shard_map.105.flat_ref, s32[3,2048]{1,0:T(4,128)S(1)} %copy-done.1), custom_call_target="tpu_custom_call" | custom-call | flops 2147483648 | bytes 1048576 | tf_op jit(solution)/shard_map/pallas_call | solution.py:392
  38.2 1.7 %collective-permute-start.11 = (f32[128,512]{1,0:T(8,128)S(1)}, f32[128,512]{1,0:T(8,128)S(1)}, u32[]{:S(2)}, u32[]{:S(2)}) collective-permute-start(f32[128,512]{1,0:T(8,128)S(1)} %shard_map.106), channel_id=1, source_target_pairs={{0,3},{1,2},{2,1},{3,0},{4,7},{5,6},{6,5},{7,4},{8,11},{9,10},{10,... | collective-permute-start | bytes 786440 | tf_op jit(solution)/shard_map/ppermute | solution.py:376
  40.0 5.2 %collective-permute-done.13.refs_2_ = f32[128,512]{1,0:T(8,128)S(1)} collective-permute-done((f32[128,512]{1,0:T(8,128)S(1)}, f32[128,512]{1,0:T(8,128)S(1)}, u32[]{:S(2)}, u32[]{:S(2)}) %collective-permute-start.13) | collective-permute-done | bytes 262176 | tf_op jit(solution)/shard_map/ppermute | solution.py:376
  45.8 5.2 %collective-permute-done.11.refs_0_ = f32[128,512]{1,0:T(8,128)S(1)} collective-permute-done((f32[128,512]{1,0:T(8,128)S(1)}, f32[128,512]{1,0:T(8,128)S(1)}, u32[]{:S(2)}, u32[]{:S(2)}) %collective-permute-start.11) | collective-permute-done | bytes 262176 | tf_op jit(solution)/shard_map/ppermute | solution.py:376
  51.1 1.1 %shard_map.110 = f32[1,65,4,512]{3,2,1,0:T(4,128)} custom-call(f32[128,512]{1,0:T(8,128)S(1)} %collective-permute-done.11.refs_0_, f32[272,512]{1,0:T(8,128)S(1)} %shard_map.109.refs_1_, s32[3,2048]{1,0:T(4,128)S(1)} %copy-done.1, bf16[4,272,256]{2,1,0:T(8,128)(2,1)S(1)} %copy-done.2), custom_call_target="tpu_custom_call" | custom-call | flops 2147483648 | bytes 1048576 | tf_op jit(solution)/shard_map/pallas_call | solution.py:392
  (33 shorter events, 1.8 us)
Async XLA Ops:
  0.0 8.3 %collective-permute-start.3 = (f32[32,16,128]{2,1,0:T(8,128)}, f32[32,16,128]{2,1,0:T(8,128)S(1)}, u32[]{:S(2)}, u32[]{:S(2)}) collective-permute-start(f32[32,16,128]{2,1,0:T(8,128)} %refs_0_.1), channel_id=1, source_target_pairs={{0,8},{8,16},{16,24},{24,28},{28,20},{20,12},{12,4},{4,0},{1,9},{9... | collective-permute-start | bytes 786440 | tf_op jit(solution)/shard_map/ppermute | solution.py:386
  2.1 7.4 %collective-permute-start.4 = (f32[32,16,128]{2,1,0:T(8,128)}, f32[32,16,128]{2,1,0:T(8,128)S(1)}, u32[]{:S(2)}, u32[]{:S(2)}) collective-permute-start(f32[32,16,128]{2,1,0:T(8,128)} %refs_0_.1), channel_id=1, source_target_pairs={{8,0},{16,8},{24,16},{28,24},{20,28},{12,20},{4,12},{0,4},{9,1},{1... | collective-permute-start | bytes 786440 | tf_op jit(solution)/shard_map/ppermute | solution.py:387
  2.1 11.1 %copy-start.1 = (s32[3,2048]{1,0:T(4,128)S(1)}, s32[3,2048]{1,0:T(4,128)}, u32[]{:S(2)}) copy-start(s32[3,2048]{1,0:T(4,128)} %refs_2_.7) | copy-start | bytes 73732
  4.2 9.0 %collective-permute-start.2 = (f32[128,512]{1,0:T(8,128)S(1)}, f32[128,512]{1,0:T(8,128)S(1)}, u32[]{:S(2)}, u32[]{:S(2)}) collective-permute-start(f32[128,512]{1,0:T(8,128)S(1)} %get-tuple-element.16), channel_id=1, source_target_pairs={{0,1},{1,0},{2,3},{3,2},{4,5},{5,4},{6,7},{7,6},{8,9},{9,8},{10,11... | collective-permute-start | bytes 786440 | tf_op jit(solution)/shard_map/ppermute | solution.py:376
  8.3 6.6 %collective-permute-start.5 = (f32[32,16,128]{2,1,0:T(8,128)S(1)}, f32[32,16,128]{2,1,0:T(8,128)S(1)}, u32[]{:S(2)}, u32[]{:S(2)}) collective-permute-start(f32[32,16,128]{2,1,0:T(8,128)S(1)} %collective-permute-done.3.refs_1_), channel_id=1, source_target_pairs={{0,8},{8,16},{16,24},{24,28},{28,20},{20,12},{12,4},{4,0},{1,9},{9... | collective-permute-start | bytes 786440 | tf_op jit(solution)/shard_map/ppermute | solution.py:386
  9.5 6.7 %collective-permute-start.6 = (f32[32,16,128]{2,1,0:T(8,128)S(1)}, f32[32,16,128]{2,1,0:T(8,128)S(1)}, u32[]{:S(2)}, u32[]{:S(2)}) collective-permute-start(f32[32,16,128]{2,1,0:T(8,128)S(1)} %collective-permute-done.4.refs_2_), channel_id=1, source_target_pairs={{8,0},{16,8},{24,16},{28,24},{20,28},{12,20},{4,12},{0,4},{9,1},{1... | collective-permute-start | bytes 786440 | tf_op jit(solution)/shard_map/ppermute | solution.py:387
  9.7 6.6 %collective-permute-start.1 = (f32[128,512]{1,0:T(8,128)S(1)}, f32[128,512]{1,0:T(8,128)S(1)}, u32[]{:S(2)}, u32[]{:S(2)}) collective-permute-start(f32[128,512]{1,0:T(8,128)S(1)} %get-tuple-element.14), channel_id=1, source_target_pairs={{0,2},{1,3},{2,0},{3,1},{4,6},{5,7},{6,4},{7,5},{8,10},{9,11},{10,... | collective-permute-start | bytes 786440 | tf_op jit(solution)/shard_map/ppermute | solution.py:376
  10.9 12.8 %collective-permute-start = (f32[128,512]{1,0:T(8,128)S(1)}, f32[128,512]{1,0:T(8,128)S(1)}, u32[]{:S(2)}, u32[]{:S(2)}) collective-permute-start(f32[128,512]{1,0:T(8,128)S(1)} %get-tuple-element.13), channel_id=1, source_target_pairs={{0,3},{1,2},{2,1},{3,0},{4,7},{5,6},{6,5},{7,4},{8,11},{9,10},{10,... | collective-permute-start | bytes 786440 | tf_op jit(solution)/shard_map/ppermute | solution.py:376
  14.6 9.1 %copy-start.4 = (bf16[2,256,512]{2,1,0:T(8,128)(2,1)S(1)}, bf16[2,256,512]{2,1,0:T(8,128)(2,1)}, u32[]{:S(2)}) copy-start(bf16[2,256,512]{2,1,0:T(8,128)(2,1)} %constant.16.clone.refs_3_) | copy-start | bytes 1572868
  14.9 11.7 %collective-permute-start.7 = (f32[32,16,128]{2,1,0:T(8,128)S(1)}, f32[32,16,128]{2,1,0:T(8,128)S(1)}, u32[]{:S(2)}, u32[]{:S(2)}) collective-permute-start(f32[32,16,128]{2,1,0:T(8,128)S(1)} %collective-permute-done.5.refs_3_), channel_id=1, source_target_pairs={{0,8},{8,16},{16,24},{24,28},{28,20},{20,12},{12,4},{4,0},{1,9},{9... | collective-permute-start | bytes 786440 | tf_op jit(solution)/shard_map/ppermute | solution.py:386
  16.2 9.2 %collective-permute-start.8 = (f32[32,16,128]{2,1,0:T(8,128)S(1)}, f32[32,16,128]{2,1,0:T(8,128)S(1)}, u32[]{:S(2)}, u32[]{:S(2)}) collective-permute-start(f32[32,16,128]{2,1,0:T(8,128)S(1)} %collective-permute-done.6.refs_4_), channel_id=1, source_target_pairs={{8,0},{16,8},{24,16},{28,24},{20,28},{12,20},{4,12},{0,4},{9,1},{1... | collective-permute-start | bytes 786440 | tf_op jit(solution)/shard_map/ppermute | solution.py:387
  17.2 9.9 %copy-start = (f32[32,16,128]{2,1,0:T(8,128)S(1)}, f32[32,16,128]{2,1,0:T(8,128)}, u32[]{:S(2)}) copy-start(f32[32,16,128]{2,1,0:T(8,128)} %refs_0_.1) | copy-start | bytes 786436
  17.2 9.9 %copy-start.6 = (bf16[160,256]{1,0:T(8,128)(2,1)S(1)}, bf16[160,256]{1,0:T(8,128)(2,1)}, u32[]{:S(2)}) copy-start(bf16[160,256]{1,0:T(8,128)(2,1)} %constant.20.clone.refs_8_) | copy-start | bytes 245764
  17.2 9.9 %copy-start.7 = (bf16[128,240]{1,0:T(8,128)(2,1)S(1)}, bf16[128,240]{1,0:T(8,128)(2,1)}, u32[]{:S(2)}) copy-start(bf16[128,240]{1,0:T(8,128)(2,1)} %constant.18.clone.refs_7_) | copy-start | bytes 184324
  25.5 5.7 %collective-permute-start.10 = (f32[16,16,128]{2,1,0:T(8,128)S(1)}, f32[16,16,128]{2,1,0:T(8,128)S(1)}, u32[]{:S(2)}, u32[]{:S(2)}) collective-permute-start(f32[16,16,128]{2,1,0:T(8,128)S(1)} %slice.9), channel_id=1, source_target_pairs={{8,0},{16,8},{24,16},{28,24},{20,28},{12,20},{4,12},{0,4},{9,1},{1... | collective-permute-start | bytes 393224 | tf_op jit(solution)/shard_map/ppermute | solution.py:387
  26.6 5.3 %copy-start.3 = (bf16[2,512,256]{2,1,0:T(8,128)(2,1)S(1)}, bf16[2,512,256]{2,1,0:T(8,128)(2,1)}, u32[]{:S(2)}) copy-start(bf16[2,512,256]{2,1,0:T(8,128)(2,1)} %constant.17.clone.y_back_ref) | copy-start | bytes 1572868
  26.6 5.3 %copy-start.5 = (bf16[8,80,48]{2,1,0:T(8,128)(2,1)S(1)}, bf16[8,80,48]{2,1,0:T(8,128)(2,1)}, u32[]{:S(2)}) copy-start(bf16[8,80,48]{2,1,0:T(8,128)(2,1)} %constant.19.clone.x_last_ref) | copy-start | bytes 184324
  26.6 5.3 %collective-permute-start.9 = (f32[16,16,128]{2,1,0:T(8,128)S(1)}, f32[16,16,128]{2,1,0:T(8,128)S(1)}, u32[]{:S(2)}, u32[]{:S(2)}) collective-permute-start(f32[16,16,128]{2,1,0:T(8,128)S(1)} %slice.8), channel_id=1, source_target_pairs={{0,8},{8,16},{16,24},{24,28},{28,20},{20,12},{12,4},{4,0},{1,9},{9... | collective-permute-start | bytes 393224 | tf_op jit(solution)/shard_map/ppermute | solution.py:386
  36.7 8.5 %copy-start.2 = (bf16[4,272,256]{2,1,0:T(8,128)(2,1)S(1)}, bf16[4,272,256]{2,1,0:T(8,128)(2,1)}, u32[]{:S(2)}) copy-start(bf16[4,272,256]{2,1,0:T(8,128)(2,1)} %constant.15.clone.refs_3_) | copy-start | bytes 1671172
  36.7 3.3 %collective-permute-start.12 = (f32[128,512]{1,0:T(8,128)S(1)}, f32[128,512]{1,0:T(8,128)S(1)}, u32[]{:S(2)}, u32[]{:S(2)}) collective-permute-start(f32[128,512]{1,0:T(8,128)S(1)} %get-tuple-element.20), channel_id=1, source_target_pairs={{0,1},{1,0},{2,3},{3,2},{4,5},{5,4},{6,7},{7,6},{8,9},{9,8},{10,11... | collective-permute-start | bytes 786440 | tf_op jit(solution)/shard_map/ppermute | solution.py:376
  37.4 7.8 %collective-permute-start.13 = (f32[128,512]{1,0:T(8,128)S(1)}, f32[128,512]{1,0:T(8,128)S(1)}, u32[]{:S(2)}, u32[]{:S(2)}) collective-permute-start(f32[128,512]{1,0:T(8,128)S(1)} %shard_map.108), channel_id=1, source_target_pairs={{0,2},{1,3},{2,0},{3,1},{4,6},{5,7},{6,4},{7,5},{8,10},{9,11},{10,... | collective-permute-start | bytes 786440 | tf_op jit(solution)/shard_map/ppermute | solution.py:376
  38.2 12.8 %collective-permute-start.11 = (f32[128,512]{1,0:T(8,128)S(1)}, f32[128,512]{1,0:T(8,128)S(1)}, u32[]{:S(2)}, u32[]{:S(2)}) collective-permute-start(f32[128,512]{1,0:T(8,128)S(1)} %shard_map.106), channel_id=1, source_target_pairs={{0,3},{1,2},{2,1},{3,0},{4,7},{5,6},{6,5},{7,4},{8,11},{9,10},{10,... | collective-permute-start | bytes 786440 | tf_op jit(solution)/shard_map/ppermute | solution.py:376

commit v4 on v3

--- a/solution.py
+++ b/solution.py
@@ -74,6 +74,7 @@
             back[d, :, o, 1, 1, o] = c * scale
     gap = s.depth_rows - 4 * s.span
     ahead = np.pad(ahead.reshape(s.devices, 2 * s.batch, 4 * s.span), ((0, 0), (0, 0), (0, gap)))
+    back = back.reshape(s.devices, 4 * s.span, 4, 2, s.planes // 2).transpose(0, 1, 3, 2, 4)
     back = np.pad(back.reshape(s.devices, 4 * s.span, 2 * s.batch), ((0, 0), (0, gap), (0, 0)))
 
     cos, sin = trig(y, grid)
@@ -154,12 +155,14 @@
 
 
 def back_kernel(s, which, started, ended, *refs):
-    in_refs, refs = refs[: len(which)], refs[len(which) :]
+    in_refs, refs = refs[: sum(which.values())], refs[sum(which.values()) :]
     table_ref, out_ref = refs[-2:]
     me = lax.axis_index("plane")
     total = refs[0][...] if started else None
-    for i, k in enumerate(which):
-        high, low = split(in_refs[i][...])
+    at = 0
+    for k, count in which.items():
+        high, low = split(jnp.concatenate([ref[...] for ref in in_refs[at : at + count]], 0))
+        at += count
         table = table_ref[partner(me, k)]
         table = jnp.concatenate([table, table[:, : 2 * s.batch]], 1)
         term = dot(table, jnp.concatenate([high, high, low], 0))
@@ -169,6 +172,16 @@
         out_ref[0] = total.reshape(s.span, 4, s.sticks)
     else:
         out_ref[...] = total
+
+
+def fetching_kernel(body, inputs, outs, count, *refs):
+    sources, targets = refs[inputs : inputs + count], refs[inputs + count + outs : inputs + 2 * count + outs]
+    copies = [pltpu.make_async_copy(sources[i], targets[i], refs[-1].at[i]) for i in range(count)]
+    for copy in copies:
+        copy.start()
+    body(*refs[:inputs], *refs[inputs + count : inputs + count + outs], *refs[inputs + 2 * count + outs : -1])
+    for copy in copies:
+        copy.wait()
 
 
 def places(s, sticks_ref, sources, x_ref, y_ref):
@@ -227,19 +240,9 @@
         out_ref[t, s.tiles * s.step :, :] = jnp.zeros(((s.even - s.tiles) * s.step, s.length), f32)
 
 
-def space_kernel(s, bands, half_ref, *refs):
-    offsets = ring_offsets(bands)[:-2]
-    slab_refs, (x_ahead_ref, x_back_ref, turned_ref, real_ref, field_ref) = refs[: len(offsets)], refs[len(offsets) :]
+def turn_kernel(s, bands, half_ref, x_ahead_ref, real_ref):
     width = s.length // bands
-    band = lax.axis_index("band")
-    at = place_on_ring(band, bands)
-    for (offset, _, _), slab_ref in zip(offsets, slab_refs, strict=True):
-        owner = band_on_ring(lax.rem(at + offset + bands, bands), bands)
-        field_ref[:, pl.ds(pl.multiple_of(owner * width, width), width), :] = slab_ref[...]
     last = pl.ds(pl.multiple_of(last_owner(bands) * width, width), width)
-    field_ref[:, last, :] = jnp.zeros((s.planes, width, s.length), f32)
-    for t in range(2, 4):
-        turned_ref[t, s.odd * s.step :, :] = jnp.zeros(((s.even - s.odd) * s.step, s.length), f32)
     table = jnp.concatenate([x_ahead_ref[...], x_ahead_ref[last, :]], 0)
 
     def plane(z, carry):
@@ -257,10 +260,29 @@
                     )
                 )
         high, low = split(jnp.concatenate(parts, 0))
-        real = dot(table, jnp.concatenate([high, high, low], 0))
-        real_ref[z] = real[s.length :]
+        real_ref[z] = dot(table, jnp.concatenate([high, high, low], 0))
+        return carry
+
+    lax.fori_loop(0, s.planes, plane, 0, unroll=4)
+
+
+def space_kernel(s, bands, real_ref, *refs):
+    offsets = ring_offsets(bands)[:-2]
+    slab_refs, (x_back_ref, turned_ref, field_ref) = refs[: len(offsets)], refs[len(offsets) :]
+    width = s.length // bands
+    band = lax.axis_index("band")
+    at = place_on_ring(band, bands)
+    for (offset, _, _), slab_ref in zip(offsets, slab_refs, strict=True):
+        owner = band_on_ring(lax.rem(at + offset + bands, bands), bands)
+        field_ref[:, pl.ds(pl.multiple_of(owner * width, width), width), :] = slab_ref[...]
+    last = pl.ds(pl.multiple_of(last_owner(bands) * width, width), width)
+    field_ref[:, last, :] = jnp.zeros((s.planes, width, s.length), f32)
+    for t in range(2, 4):
+        turned_ref[t, s.odd * s.step :, :] = jnp.zeros(((s.even - s.odd) * s.step, s.length), f32)
+
+    def plane(z, carry):
         field = field_ref[z]
-        high, low = split(real[: s.length] * jnp.concatenate([field, field], 1))
+        high, low = split(real_ref[z, : s.length, :] * jnp.concatenate([field, field], 1))
         turned = dot(x_back_ref[...], jnp.concatenate([high, low], 0))
         keep_turned(s, turned_ref, z, turned[: s.kept] + turned[s.kept :])
         return carry
@@ -280,54 +302,56 @@
             at += count
 
 
-def finish_kernel(s, bands, first_ref, real_ref, up_ref, down_ref, x_last_ref, y_back_ref, flat_ref, turned_ref):
-    total = s.tiles * s.batch
+def finish_kernel(s, bands, half, first_ref, real_ref, slab_ref, x_last_ref, y_back_ref, flat_ref, turned_ref):
     for t in range(2, 4):
         turned_ref[t, s.odd * s.step :, :] = jnp.zeros(((s.even - s.odd) * s.step, s.length), f32)
     x_last = x_last_ref[last_owner(bands)]
     part = s.planes // 2
-    for slab_ref, start in ((up_ref, 0), (down_ref, part)):
-
-        def plane(z, carry, slab_ref=slab_ref, start=start):
-            field = slab_ref[z]
-            high, low = split(real_ref[start + z] * jnp.concatenate([field, field], 1))
-            keep_turned(s, turned_ref, start + z, dot(x_last, jnp.concatenate([high, low, high], 0)))
-            return carry
-
-        lax.fori_loop(0, part, plane, 0, unroll=4)
-
-    rows = 2 * s.batch
+
+    def plane(z, carry):
+        field = slab_ref[z]
+        high, low = split(real_ref[half * part + z, s.length :, :] * jnp.concatenate([field, field], 1))
+        keep_turned(s, turned_ref, half * part + z, dot(x_last, jnp.concatenate([high, low, high], 0)))
+        return carry
+
+    lax.fori_loop(0, part, plane, 0, unroll=4)
+
     lanes = 2 * s.rows_y
     table = jnp.concatenate([y_back_ref[0], y_back_ref[0], y_back_ref[1]], 0)
-    for start in range(0, total, 4 * s.batch):
-        end = min(total, start + 4 * s.batch)
+    for start in range(0, s.tiles, 8):
+        end = min(s.tiles, start + 8)
         parts = []
-        for row in range(start // s.batch * s.step, end // s.batch * s.step, s.step):
-            own = slice(row, row + s.batch)
-            parts.append(jnp.concatenate([first_ref[t, own, :] + turned_ref[t, own, :] for t in range(4)], 1))
+        for tile in range(start, end):
+            for o in range(2):
+                row = tile * s.step + o * s.planes + half * part
+                own = slice(row, row + part)
+                parts.append(jnp.concatenate([first_ref[t, own, :] + turned_ref[t, own, :] for t in range(4)], 1))
         high, low = split(jnp.concatenate(parts, 0))
         moved = dot(jnp.concatenate([high, low, high], 1), table)
         high, low = split(moved)
-        for t in range((end - start) // s.batch):
-            column = (start // s.batch + t) * lanes
+        for tile in range(start, end):
+            at = (tile - start) * s.planes
             for component in range(2):
-                row = component * s.batch
-                mine = slice(t * s.batch, (t + 1) * s.batch), slice(component * lanes, (component + 1) * lanes)
-                flat_ref[row : row + s.batch, column : column + lanes] = high[mine]
-                flat_ref[rows + row : rows + row + s.batch, column : column + lanes] = low[mine]
-
-
-def pick_kernel(s, which, flat_ref, sticks_ref, *refs):
+                mine = slice(at, at + s.planes), slice(component * lanes, (component + 1) * lanes)
+                for row, value in ((component, high), (2 + component, low)):
+                    flat_ref[row * s.planes : (row + 1) * s.planes, tile * lanes : (tile + 1) * lanes] = value[mine]
+
+
+def pick_kernel(s, which, count, *refs):
+    flat_refs, sticks_ref, refs = refs[:count], refs[count], refs[count + 1 :]
     out_refs, (x_ref, y_ref, hot_ref) = refs[: len(which)], refs[len(which) :]
     me = lax.axis_index("plane")
     places(s, sticks_ref, [partner(me, k) for k in which], x_ref, y_ref)
-    rows = 2 * s.batch
+    rows = 2 * s.planes
+    flat = jnp.concatenate([flat_ref[...] for flat_ref in flat_refs], 0)
     for i in range(len(which)):
         columns = slice(i * s.sticks, (i + 1) * s.sticks)
         for x in range(2 * s.tiles):
             hot_ref[x * s.rows_y : (x + 1) * s.rows_y, :] = one_hot(x, x_ref[:, columns], y_ref[:, columns])
-        found = dot(flat_ref[...], hot_ref[...])
-        out_refs[i][...] = found[:rows] + found[rows:]
+        found = dot(flat, hot_ref[...])
+        for h in range(count):
+            row = 2 * h * rows
+            out_refs[i][h * rows : (h + 1) * rows, :] = found[row : row + rows] + found[row + rows : row + 2 * rows]
 
 
 def band_on_ring(place, count):
@@ -388,16 +412,24 @@
             slabs += [up, down]
         return slabs
 
-    def kernel(body, inputs, out_shape, limit, flops, scratch_shapes=(), place=VMEM):
-        return pl.pallas_call(
+    def kernel(body, inputs, out_shape, limit, flops, scratch_shapes=(), place=VMEM, fetched=()):
+        single = not isinstance(out_shape, list)
+        outs = [out_shape] if single else out_shape
+        extra = [jax.ShapeDtypeStruct(a.shape, a.dtype) for a in fetched]
+        if fetched:
+            body = functools.partial(fetching_kernel, body, len(inputs), len(outs), len(fetched))
+        results = pl.pallas_call(
             body,
-            in_specs=[place] * len(inputs),
-            out_specs=jax.tree.map(lambda _: VMEM, out_shape),
-            out_shape=out_shape,
-            scratch_shapes=scratch_shapes,
+            in_specs=[place] * len(inputs) + [HBM] * len(fetched),
+            out_specs=[VMEM] * (len(outs) + len(fetched)),
+            out_shape=outs + extra,
+            scratch_shapes=[*scratch_shapes] + [pltpu.SemaphoreType.DMA((len(fetched),))] * bool(fetched),
             compiler_params=pltpu.CompilerParams(vmem_limit_bytes=limit << 10),
             cost_estimate=pl.CostEstimate(flops=flops, bytes_accessed=1 << 20, transcendentals=0),
-        )(*inputs)
+        )(*inputs, *(pltpu.with_memory_space_constraint(a, pltpu.HBM) for a in fetched))
+        if fetched:
+            return results[: len(outs)], results[len(outs) :]
+        return results[0] if single else results
 
     slabs = ring()
     positions = 2 * s.tiles * s.rows_y
@@ -420,12 +452,15 @@
         )
         held = exchange(sent)
         half = None
+        ready = results
+        later = ["y_ahead", "x_ahead", "x_back", "x_last", "y_back", "z_back"]
         grid_shape = (s.tiles * s.batch, 4 * s.rows_y)
         for name, which in stages(devices):
             started, ended = half is not None, name == "lay3"
             shape = (4, s.even * s.step, s.length) if ended else grid_shape
             own = [pltpu.VMEM((s.rows_y, len(which) * s.sticks), bf16)] * 2
             own.append(pltpu.VMEM((2 * rows, len(which) * s.sticks), bf16))
+            fetch = [] if started or ready else [tab[key] for key in later] + [potential]
             half = kernel(
                 functools.partial(lay_kernel, s, which, started, ended),
                 [held[k] for k in which] + [half] * started + [stick_map] + [tab["y_ahead"]] * ended,
@@ -433,34 +468,44 @@
                 24 << 10,
                 1 << 31,
                 [pltpu.VMEM(grid_shape, f32)] * ended + own,
+                fetched=fetch,
             )
+            if fetch:
+                (half,), (*ready, slabs[0]) = half
+                tab.update(zip(later, ready, strict=True))
         turned_shape = (4, s.even * s.step, s.length)
-        turned, real = kernel(
+        real = kernel(
+            functools.partial(turn_kernel, s, bands),
+            [half, tab["x_ahead"]],
+            jax.ShapeDtypeStruct((s.planes, s.length + s.length // bands, 2 * s.length), f32),
+            16 << 10,
+            1 << 31,
+        )
+        turned = kernel(
             functools.partial(space_kernel, s, bands),
-            [half, *slabs[:-2], tab["x_ahead"], tab["x_back"]],
-            [
-                jax.ShapeDtypeStruct(turned_shape, f32),
-                jax.ShapeDtypeStruct((s.planes, s.length // bands, 2 * s.length), f32),
-            ],
+            [real, *slabs[:-2], tab["x_back"]],
+            jax.ShapeDtypeStruct(turned_shape, f32),
             16 << 10,
-            1 << 32,
+            1 << 31,
             [pltpu.VMEM((s.planes, s.length, s.length), f32)],
         )
-        flat = kernel(
-            functools.partial(finish_kernel, s, bands),
-            [turned, real, *slabs[-2:], tab["x_last"], tab["y_back"]],
-            jax.ShapeDtypeStruct((2 * rows, positions), bf16),
-            24 << 10,
-            1 << 32,
-            [pltpu.VMEM(turned_shape, f32)],
-        )
-        mixed = [None] * devices
-        groups = [[k] for k in partners(devices)[:-1]] + [[1, 0]]
-        for which in groups:
-            parts = kernel(
-                functools.partial(pick_kernel, s, which),
-                [flat, stick_map],
-                [block] * len(which),
+        flats = [
+            kernel(
+                functools.partial(finish_kernel, s, bands, half),
+                [turned, real, slabs[half - 2], tab["x_last"], tab["y_back"]],
+                jax.ShapeDtypeStruct((4 * s.planes, positions), bf16),
+                20 << 10,
+                1 << 31,
+                [pltpu.VMEM(turned_shape, f32)],
+            )
+            for half in range(2)
+        ]
+
+        def pick(which, flats):
+            return kernel(
+                functools.partial(pick_kernel, s, which, len(flats)),
+                [*flats, stick_map],
+                [jax.ShapeDtypeStruct((len(flats) * 2 * s.planes, s.sticks), f32)] * len(which),
                 16 << 10,
                 1 << 31,
                 [
@@ -469,21 +514,28 @@
                     pltpu.VMEM((positions, s.sticks), bf16),
                 ],
             )
-            for k, part in zip(which, parts, strict=True):
-                mixed[k] = part
-        returned = exchange(mixed)
-        late = partners(devices)[-2]
-        early = [k for k in range(devices) if k != late]
+
+        def send(k, block):
+            return lax.ppermute(block, "plane", [(i, i ^ k) for i in range(devices)])
+
+        soon, *far, near = partners(devices)
+        returned = {soon: [send(soon, *pick([soon], [flats[h]])) for h in range(2)]}
+        for k in far:
+            returned[k] = [send(k, *pick([k], flats))]
+        beside, own = pick([near, 0], flats)
+        returned |= {near: [send(near, beside)], 0: [own]}
+        late = far[-1]
+        counts = {k: len(blocks) for k, blocks in returned.items() if k != late}
         begun = kernel(
-            functools.partial(back_kernel, s, early, False, False),
-            [*(returned[k] for k in early), tab["z_back"]],
+            functools.partial(back_kernel, s, counts, False, False),
+            [*(block for k in counts for block in returned[k]), tab["z_back"]],
             jax.ShapeDtypeStruct((s.depth_rows, s.sticks), f32),
             16 << 10,
             1 << 31,
         )
         result = kernel(
-            functools.partial(back_kernel, s, [late], True, True),
-            [returned[late], begun, stick_map, tab["z_back"]],
+            functools.partial(back_kernel, s, {late: 1}, True, True),
+            [*returned[late], begun, stick_map, tab["z_back"]],
             jax.ShapeDtypeStruct((1,) + given.shape[1:], f32),
             16 << 10,
             1 << 31,

time: 52.5 us -> 50.2 us (0.956)
  waiting for transfers between devices: 20.9 us -> 15.8 us
  starting transfers between devices: 13.6 us -> 15.7 us
  Pallas kernels: 17.4 us -> 18.3 us
    ppermute x6 -> x3, waiting for transfers between devices: 16.9 us -> 4.83 us  [exchange(): lax.ppermute(blocks[k], 'plane', [(i, i ^ k) for i in range(devices)])]
    ppermute x0 -> x4, waiting for transfers between devices: none -> 8.99 us  [send(): return lax.ppermute(block, 'plane', [(i, i ^ k) for i in range(devices)])]
    ppermute x0 -> x4, starting transfers between devices: none -> 6.27 us  [send(): return lax.ppermute(block, 'plane', [(i, i ^ k) for i in range(devices)])]
    ppermute x6 -> x3, starting transfers between devices: 6.97 us -> 2.73 us  [exchange(): lax.ppermute(blocks[k], 'plane', [(i, i ^ k) for i in range(devices)])]
    ppermute x4, waiting for transfers between devices: 3.99 us -> 1.92 us  [ring(): up = lax.ppermute(up, 'band', along)]
    pallas_call x11 -> x14, Pallas kernels: 17.4 us -> 18.3 us  [kernel(): pl.pallas_call(body, in_specs=[place] * len(inputs) + [HBM] * len(fetched...]
    ppermute x4, starting transfers between devices: 1.44 us -> 2.28 us  [ring(): down = lax.ppermute(down, 'band', against)]
    ppermute x4, starting transfers between devices: 5.18 us -> 4.45 us  [ring(): up = lax.ppermute(up, 'band', along)]
  transfers between devices with their start and end apart: 14 -> 15, of which waited for: 6 -> 7; matrix products, arithmetic and copies ran while one was open for 0% -> 0% of each run, Pallas kernels for 22% -> 28%
where the time goes in v4:
time: 50.2 us; the launch traced here: 49.9 us
  Pallas kernels  18.3 us (36%)
  waiting for transfers between devices  15.8 us (31%)
  starting transfers between devices  15.7 us (31%)
    pallas_call x14, Pallas kernels, kernel(): pl.pallas_call(body, in_specs=[place] * len(inputs) + [HBM] * len(fetched...  18.3 us
    ppermute x4, waiting for transfers between devices, send(): return lax.ppermute(block, 'plane', [(i, i ^ k) for i in range(devices)])  8.99 us
    ppermute x4, starting transfers between devices, send(): return lax.ppermute(block, 'plane', [(i, i ^ k) for i in range(devices)])  6.27 us
    ppermute x3, waiting for transfers between devices, exchange(): lax.ppermute(blocks[k], 'plane', [(i, i ^ k) for i in range(devices)])  4.83 us
    ppermute x4, starting transfers between devices, ring(): up = lax.ppermute(up, 'band', along)  4.45 us
    ppermute x3, starting transfers between devices, exchange(): lax.ppermute(blocks[k], 'plane', [(i, i ^ k) for i in range(devices)])  2.73 us
    ppermute x4, starting transfers between devices, ring(): down = lax.ppermute(down, 'band', against)  2.28 us
    ppermute x4, waiting for transfers between devices, ring(): up = lax.ppermute(up, 'band', along)  1.92 us
  transfers between devices with their start and end apart: 15, of which 7 were waited for; matrix products, arithmetic and copies ran while one was open for 0% of the time, Pallas kernels for 28%

profile of v4, /device:TPU:1, one launch (start us, length us, event | category | flops | bytes accessed | tf_op | source)
XLA Modules:
  0.0 49.9 jit_solution(11449518470535141751)
XLA Ops:
  0.0 2.1 %collective-permute-start.3 = (f32[32,16,128]{2,1,0:T(8,128)}, f32[32,16,128]{2,1,0:T(8,128)S(1)}, u32[]{:S(2)}, u32[]{:S(2)}) collective-permute-start(f32[32,16,128]{2,1,0:T(8,128)} %refs_9_.1), channel_id=1, source_target_pairs={{0,8},{8,16},{16,24},{24,28},{28,20},{20,12},{12,4},{4,0},{1,9},{9... | collective-permute-start | bytes 786440 | tf_op jit(solution)/shard_map/ppermute | solution.py:410
  2.1 2.1 %shard_map.100 = (f32[128,512]{1,0:T(8,128)S(1)}, f32[128,512]{1,0:T(8,128)S(1)}, f32[128,512]{1,0:T(8,128)S(1)}, f32[128,512]{1,0:T(8,128)S(1)}) custom-call(f32[1,65,4,512]{3,2,1,0:T(4,128)} %bitcast.2, s32[3,2048]{1,0:T(4,128)} %refs_2_.11, bf16[4,128,816]{2,1,0:T(8,128)(2,1)} %constant.14.clone.table_hbm), custom_call_target="tpu_custom_call" | custom-call | flops 2147483648 | bytes 1048576 | tf_op jit(solution)/shard_map/pallas_call | solution.py:421
  4.2 1.0 %collective-permute-start.2 = (f32[128,512]{1,0:T(8,128)S(1)}, f32[128,512]{1,0:T(8,128)S(1)}, u32[]{:S(2)}, u32[]{:S(2)}) collective-permute-start(f32[128,512]{1,0:T(8,128)S(1)} %get-tuple-element.22), channel_id=1, source_target_pairs={{0,1},{1,0},{2,3},{3,2},{4,5},{5,4},{6,7},{7,6},{8,9},{9,8},{10,11... | collective-permute-start | bytes 786440 | tf_op jit(solution)/shard_map/ppermute | solution.py:400
  5.3 1.7 %collective-permute-start.1 = (f32[128,512]{1,0:T(8,128)S(1)}, f32[128,512]{1,0:T(8,128)S(1)}, u32[]{:S(2)}, u32[]{:S(2)}) collective-permute-start(f32[128,512]{1,0:T(8,128)S(1)} %get-tuple-element.20), channel_id=1, source_target_pairs={{0,2},{1,3},{2,0},{3,1},{4,6},{5,7},{6,4},{7,5},{8,10},{9,11},{10,... | collective-permute-start | bytes 786440 | tf_op jit(solution)/shard_map/ppermute | solution.py:400
  7.0 1.3 %collective-permute-done.3.refs_1_ = f32[32,16,128]{2,1,0:T(8,128)S(1)} collective-permute-done((f32[32,16,128]{2,1,0:T(8,128)}, f32[32,16,128]{2,1,0:T(8,128)S(1)}, u32[]{:S(2)}, u32[]{:S(2)}) %collective-permute-start.3) | collective-permute-done | bytes 262176 | tf_op jit(solution)/shard_map/ppermute | solution.py:410
  8.3 1.2 %collective-permute-start.5 = (f32[32,16,128]{2,1,0:T(8,128)S(1)}, f32[32,16,128]{2,1,0:T(8,128)S(1)}, u32[]{:S(2)}, u32[]{:S(2)}) collective-permute-start(f32[32,16,128]{2,1,0:T(8,128)S(1)} %collective-permute-done.3.refs_1_), channel_id=1, source_target_pairs={{0,8},{8,16},{16,24},{24,28},{28,20},{20,12},{12,4},{4,0},{1,9},{9... | collective-permute-start | bytes 786440 | tf_op jit(solution)/shard_map/ppermute | solution.py:410
  9.8 1.6 %shard_map.101 = (f32[1088,256]{1,0:T(8,128)S(1)}, bf16[2,256,512]{2,1,0:T(8,128)(2,1)S(1)}, bf16[128,240]{1,0:T(8,128)(2,1)S(1)}, bf16[160,256]{1,0:T(8,128)(2,...) custom-call(f32[128,512]{1,0:T(8,128)S(1)} %get-tuple-element.21.ref, ...), custom_call_target="tpu_custom_call" | custom-call | flops 2147483648 | bytes 1048576 | tf_op jit(solution)/shard_map/pallas_call | solution.py:421
  11.4 2.1 %collective-permute-done.1.refs_0_ = f32[128,512]{1,0:T(8,128)S(1)} collective-permute-done((f32[128,512]{1,0:T(8,128)S(1)}, f32[128,512]{1,0:T(8,128)S(1)}, u32[]{:S(2)}, u32[]{:S(2)}) %collective-permute-start.1) | collective-permute-done | bytes 262176 | tf_op jit(solution)/shard_map/ppermute | solution.py:400
  14.9 1.0 %collective-permute-start.7 = (f32[32,16,128]{2,1,0:T(8,128)S(1)}, f32[32,16,128]{2,1,0:T(8,128)S(1)}, u32[]{:S(2)}, u32[]{:S(2)}) collective-permute-start(f32[32,16,128]{2,1,0:T(8,128)S(1)} %collective-permute-done.5.refs_3_), channel_id=1, source_target_pairs={{0,8},{8,16},{16,24},{24,28},{28,20},{20,12},{12,4},{4,0},{1,9},{9... | collective-permute-start | bytes 786440 | tf_op jit(solution)/shard_map/ppermute | solution.py:410
  16.4 2.7 %collective-permute-done.refs_0_ = f32[128,512]{1,0:T(8,128)S(1)} collective-permute-done((f32[128,512]{1,0:T(8,128)S(1)}, f32[128,512]{1,0:T(8,128)S(1)}, u32[]{:S(2)}, u32[]{:S(2)}) %collective-permute-start) | collective-permute-done | bytes 262176 | tf_op jit(solution)/shard_map/ppermute | solution.py:400
  19.1 1.8 %shard_map.103.half_ref = f32[4,1560,128]{2,1,0:T(8,128)S(1)} custom-call(f32[128,512]{1,0:T(8,128)S(1)} %collective-permute-done.refs_0_, f32[1088,256]{1,0:T(8,128)S(1)} %shard_map.102.refs_1_, s32[3,2048]{1,0:T(4,128)S(1)} %copy-done, bf16[2,256,512]{2,1,0:T(8,128)(2,1)S(1)} %get-tuple-element.24.refs_3_), custom_call_target="tpu_custom_call" | custom-call | flops 2147483648 | bytes 1048576 | tf_op jit(solution)/shard_map/pallas_call | solution.py:421
  20.9 2.0 %shard_map.104.real_ref = f32[32,144,256]{2,1,0:T(8,128)S(1)} custom-call(f32[4,1560,128]{2,1,0:T(8,128)S(1)} %shard_map.103.half_ref, bf16[128,240]{1,0:T(8,128)(2,1)S(1)} %get-tuple-element.25.x_ahead_ref), custom_call_target="tpu_custom_call" | custom-call | flops 2147483648 | bytes 1048576 | tf_op jit(solution)/shard_map/pallas_call | solution.py:421
  22.9 1.5 %collective-permute-start.10 = (f32[16,16,128]{2,1,0:T(8,128)S(1)}, f32[16,16,128]{2,1,0:T(8,128)S(1)}, u32[]{:S(2)}, u32[]{:S(2)}) collective-permute-start(f32[16,16,128]{2,1,0:T(8,128)S(1)} %slice.9), channel_id=1, source_target_pairs={{8,0},{16,8},{24,16},{28,24},{20,28},{12,20},{4,12},{0,4},{9,1},{1... | collective-permute-start | bytes 393224 | tf_op jit(solution)/shard_map/ppermute | solution.py:411
  24.6 2.4 %shard_map.105.first_ref = f32[4,1560,128]{2,1,0:T(8,128)S(1)} custom-call(f32[32,144,256]{2,1,0:T(8,128)S(1)} %shard_map.104.real_ref, f32[32,16,128]{2,1,0:T(8,128)S(1)} %get-tuple-element.26.refs_0_, f32[32,16,128]{2,1,0:T(8,128)S(1)} %collective-permute-done.3.refs_1_, f32[32,16,128]{2,1,0:T(8,128)S(1)} %collective-permute-done.4.refs_2_, ...), custom_call_target="tpu_custom_call" | custom-call | flops 2147483648 | bytes 1048576 | tf_op jit(solution)/shard_map/pallas_call | solution.py:421
  27.0 1.4 %shard_map.107.refs_1_.refs_0_ = bf16[128,2176]{1,0:T(8,128)(2,1)S(1)} custom-call(f32[4,1560,128]{2,1,0:T(8,128)S(1)} %shard_map.105.first_ref, f32[32,144,256]{2,1,0:T(8,128)S(1)} %shard_map.104.real_ref, f32[16,16,128]{2,1,0:T(8,128)S(1)} %collective-permute-done.10.slab_ref, bf16[8,80,48]{2,1,0:T(8,128)(2,1)S(1)} %get-tuple-element.28.x_last_ref, ...), custom_call_target="tpu_custom_call" | custom-call | flops 2147483648 | bytes 1048576 | tf_op jit(solution)/shard_map/pallas_call | solution.py:421
  28.9 1.4 %shard_map.106.refs_0_ = bf16[128,2176]{1,0:T(8,128)(2,1)S(1)} custom-call(f32[4,1560,128]{2,1,0:T(8,128)S(1)} %shard_map.105.first_ref, f32[32,144,256]{2,1,0:T(8,128)S(1)} %shard_map.104.real_ref, f32[16,16,128]{2,1,0:T(8,128)S(1)} %collective-permute-done.9.slab_ref, bf16[8,80,48]{2,1,0:T(8,128)(2,1)S(1)} %get-tuple-element.28.x_last_ref, ...), custom_call_target="tpu_custom_call" | custom-call | flops 2147483648 | bytes 1048576 | tf_op jit(solution)/shard_map/pallas_call | solution.py:421
  30.3 1.4 %shard_map.111 = (f32[128,512]{1,0:T(8,128)S(1)}, f32[128,512]{1,0:T(8,128)S(1)}) custom-call(bf16[128,2176]{1,0:T(8,128)(2,1)S(1)} %shard_map.106.refs_0_, bf16[128,2176]{1,0:T(8,128)(2,1)S(1)} %shard_map.107.refs_1_.refs_0_, s32[3,2048]{1,0:T(4,128)S(1)} %copy-done), custom_call_target="tpu_custom_call" | custom-call | flops 2147483648 | bytes 1048576 | tf_op jit(solution)/shard_map/pallas_call | solution.py:421
  32.2 3.0 %collective-permute-start.14 = (f32[128,512]{1,0:T(8,128)S(1)}, f32[128,512]{1,0:T(8,128)S(1)}, u32[]{:S(2)}, u32[]{:S(2)}) collective-permute-start(f32[128,512]{1,0:T(8,128)S(1)} %get-tuple-element.30), channel_id=1, source_target_pairs={{0,1},{1,0},{2,3},{3,2},{4,5},{5,4},{6,7},{7,6},{8,9},{9,8},{10,11... | collective-permute-start | bytes 786440 | tf_op jit(solution)/shard_map/ppermute | solution.py:519
  35.2 1.2 %collective-permute-start.13 = (f32[64,512]{1,0:T(8,128)S(1)}, f32[64,512]{1,0:T(8,128)S(1)}, u32[]{:S(2)}, u32[]{:S(2)}) collective-permute-start(f32[64,512]{1,0:T(8,128)S(1)} %shard_map.110), channel_id=1, source_target_pairs={{0,2},{1,3},{2,0},{3,1},{4,6},{5,7},{6,4},{7,5},{8,10},{9,11},{10,... | collective-permute-start | bytes 393224 | tf_op jit(solution)/shard_map/ppermute | solution.py:519
  37.4 1.8 %collective-permute-start.11 = (f32[128,512]{1,0:T(8,128)S(1)}, f32[128,512]{1,0:T(8,128)S(1)}, u32[]{:S(2)}, u32[]{:S(2)}) collective-permute-start(f32[128,512]{1,0:T(8,128)S(1)} %shard_map.108), channel_id=1, source_target_pairs={{0,3},{1,2},{2,1},{3,0},{4,7},{5,6},{6,5},{7,4},{8,11},{9,10},{10,... | collective-permute-start | bytes 786440 | tf_op jit(solution)/shard_map/ppermute | solution.py:519
  39.2 0.9 %collective-permute-done.13.refs_1_ = f32[64,512]{1,0:T(8,128)S(1)} collective-permute-done((f32[64,512]{1,0:T(8,128)S(1)}, f32[64,512]{1,0:T(8,128)S(1)}, u32[]{:S(2)}, u32[]{:S(2)}) %collective-permute-start.13) | collective-permute-done | bytes 131104 | tf_op jit(solution)/shard_map/ppermute | solution.py:519
  40.2 2.8 %collective-permute-done.12.refs_0_ = f32[64,512]{1,0:T(8,128)S(1)} collective-permute-done((f32[64,512]{1,0:T(8,128)S(1)}, f32[64,512]{1,0:T(8,128)S(1)}, u32[]{:S(2)}, u32[]{:S(2)}) %collective-permute-start.12) | collective-permute-done | bytes 131104 | tf_op jit(solution)/shard_map/ppermute | solution.py:519
  43.6 5.3 %collective-permute-done.11.refs_0_ = f32[128,512]{1,0:T(8,128)S(1)} collective-permute-done((f32[128,512]{1,0:T(8,128)S(1)}, f32[128,512]{1,0:T(8,128)S(1)}, u32[]{:S(2)}, u32[]{:S(2)}) %collective-permute-start.11) | collective-permute-done | bytes 262176 | tf_op jit(solution)/shard_map/ppermute | solution.py:519
  48.8 1.1 %shard_map.113 = f32[1,65,4,512]{3,2,1,0:T(4,128)} custom-call(f32[128,512]{1,0:T(8,128)S(1)} %collective-permute-done.11.refs_0_, f32[272,512]{1,0:T(8,128)S(1)} %shard_map.112.refs_1_, s32[3,2048]{1,0:T(4,128)S(1)} %copy-done, bf16[4,272,256]{2,1,0:T(8,128)(2,1)S(1)} %get-tuple-element.32.refs_4_.refs_3_), custom_call_target="tpu_custom_call" | custom-call | flops 2147483648 | bytes 1048576 | tf_op jit(solution)/shard_map/pallas_call | solution.py:421
  (24 shorter events, 5.0 us)
Async XLA Ops:
  0.0 8.3 %collective-permute-start.3 = (f32[32,16,128]{2,1,0:T(8,128)}, f32[32,16,128]{2,1,0:T(8,128)S(1)}, u32[]{:S(2)}, u32[]{:S(2)}) collective-permute-start(f32[32,16,128]{2,1,0:T(8,128)} %refs_9_.1), channel_id=1, source_target_pairs={{0,8},{8,16},{16,24},{24,28},{28,20},{20,12},{12,4},{4,0},{1,9},{9... | collective-permute-start | bytes 786440 | tf_op jit(solution)/shard_map/ppermute | solution.py:410
  2.1 7.4 %collective-permute-start.4 = (f32[32,16,128]{2,1,0:T(8,128)}, f32[32,16,128]{2,1,0:T(8,128)S(1)}, u32[]{:S(2)}, u32[]{:S(2)}) collective-permute-start(f32[32,16,128]{2,1,0:T(8,128)} %refs_9_.1), channel_id=1, source_target_pairs={{8,0},{16,8},{24,16},{28,24},{20,28},{12,20},{4,12},{0,4},{9,1},{1... | collective-permute-start | bytes 786440 | tf_op jit(solution)/shard_map/ppermute | solution.py:411
  2.1 7.6 %copy-start = (s32[3,2048]{1,0:T(4,128)S(1)}, s32[3,2048]{1,0:T(4,128)}, u32[]{:S(2)}) copy-start(s32[3,2048]{1,0:T(4,128)} %refs_2_.11) | copy-start | bytes 73732
  4.2 5.5 %collective-permute-start.2 = (f32[128,512]{1,0:T(8,128)S(1)}, f32[128,512]{1,0:T(8,128)S(1)}, u32[]{:S(2)}, u32[]{:S(2)}) collective-permute-start(f32[128,512]{1,0:T(8,128)S(1)} %get-tuple-element.22), channel_id=1, source_target_pairs={{0,1},{1,0},{2,3},{3,2},{4,5},{5,4},{6,7},{7,6},{8,9},{9,8},{10,11... | collective-permute-start | bytes 786440 | tf_op jit(solution)/shard_map/ppermute | solution.py:400
  5.3 8.2 %collective-permute-start.1 = (f32[128,512]{1,0:T(8,128)S(1)}, f32[128,512]{1,0:T(8,128)S(1)}, u32[]{:S(2)}, u32[]{:S(2)}) collective-permute-start(f32[128,512]{1,0:T(8,128)S(1)} %get-tuple-element.20), channel_id=1, source_target_pairs={{0,2},{1,3},{2,0},{3,1},{4,6},{5,7},{6,4},{7,5},{8,10},{9,11},{10,... | collective-permute-start | bytes 786440 | tf_op jit(solution)/shard_map/ppermute | solution.py:400
  6.9 12.2 %collective-permute-start = (f32[128,512]{1,0:T(8,128)S(1)}, f32[128,512]{1,0:T(8,128)S(1)}, u32[]{:S(2)}, u32[]{:S(2)}) collective-permute-start(f32[128,512]{1,0:T(8,128)S(1)} %get-tuple-element.19), channel_id=1, source_target_pairs={{0,3},{1,2},{2,1},{3,0},{4,7},{5,6},{6,5},{7,4},{8,11},{9,10},{10,... | collective-permute-start | bytes 786440 | tf_op jit(solution)/shard_map/ppermute | solution.py:400
  8.3 6.6 %collective-permute-start.5 = (f32[32,16,128]{2,1,0:T(8,128)S(1)}, f32[32,16,128]{2,1,0:T(8,128)S(1)}, u32[]{:S(2)}, u32[]{:S(2)}) collective-permute-start(f32[32,16,128]{2,1,0:T(8,128)S(1)} %collective-permute-done.3.refs_1_), channel_id=1, source_target_pairs={{0,8},{8,16},{16,24},{24,28},{28,20},{20,12},{12,4},{4,0},{1,9},{9... | collective-permute-start | bytes 786440 | tf_op jit(solution)/shard_map/ppermute | solution.py:410
  9.5 6.3 %collective-permute-start.6 = (f32[32,16,128]{2,1,0:T(8,128)S(1)}, f32[32,16,128]{2,1,0:T(8,128)S(1)}, u32[]{:S(2)}, u32[]{:S(2)}) collective-permute-start(f32[32,16,128]{2,1,0:T(8,128)S(1)} %collective-permute-done.4.refs_2_), channel_id=1, source_target_pairs={{8,0},{16,8},{24,16},{28,24},{20,28},{12,20},{4,12},{0,4},{9,1},{1... | collective-permute-start | bytes 786440 | tf_op jit(solution)/shard_map/ppermute | solution.py:411
  14.9 9.5 %collective-permute-start.7 = (f32[32,16,128]{2,1,0:T(8,128)S(1)}, f32[32,16,128]{2,1,0:T(8,128)S(1)}, u32[]{:S(2)}, u32[]{:S(2)}) collective-permute-start(f32[32,16,128]{2,1,0:T(8,128)S(1)} %collective-permute-done.5.refs_3_), channel_id=1, source_target_pairs={{0,8},{8,16},{16,24},{24,28},{28,20},{20,12},{12,4},{4,0},{1,9},{9... | collective-permute-start | bytes 786440 | tf_op jit(solution)/shard_map/ppermute | solution.py:410
  15.9 7.0 %collective-permute-start.8 = (f32[32,16,128]{2,1,0:T(8,128)S(1)}, f32[32,16,128]{2,1,0:T(8,128)S(1)}, u32[]{:S(2)}, u32[]{:S(2)}) collective-permute-start(f32[32,16,128]{2,1,0:T(8,128)S(1)} %collective-permute-done.6.refs_4_), channel_id=1, source_target_pairs={{8,0},{16,8},{24,16},{28,24},{20,28},{12,20},{4,12},{0,4},{9,1},{1... | collective-permute-start | bytes 786440 | tf_op jit(solution)/shard_map/ppermute | solution.py:411
  22.9 4.1 %collective-permute-start.10 = (f32[16,16,128]{2,1,0:T(8,128)S(1)}, f32[16,16,128]{2,1,0:T(8,128)S(1)}, u32[]{:S(2)}, u32[]{:S(2)}) collective-permute-start(f32[16,16,128]{2,1,0:T(8,128)S(1)} %slice.9), channel_id=1, source_target_pairs={{8,0},{16,8},{24,16},{28,24},{20,28},{12,20},{4,12},{0,4},{9,1},{1... | collective-permute-start | bytes 393224 | tf_op jit(solution)/shard_map/ppermute | solution.py:411
  24.4 4.4 %collective-permute-start.9 = (f32[16,16,128]{2,1,0:T(8,128)S(1)}, f32[16,16,128]{2,1,0:T(8,128)S(1)}, u32[]{:S(2)}, u32[]{:S(2)}) collective-permute-start(f32[16,16,128]{2,1,0:T(8,128)S(1)} %slice.8), channel_id=1, source_target_pairs={{0,8},{8,16},{16,24},{24,28},{28,20},{20,12},{12,4},{4,0},{1,9},{9... | collective-permute-start | bytes 393224 | tf_op jit(solution)/shard_map/ppermute | solution.py:410
  32.2 10.8 %collective-permute-start.14 = (f32[128,512]{1,0:T(8,128)S(1)}, f32[128,512]{1,0:T(8,128)S(1)}, u32[]{:S(2)}, u32[]{:S(2)}) collective-permute-start(f32[128,512]{1,0:T(8,128)S(1)} %get-tuple-element.30), channel_id=1, source_target_pairs={{0,1},{1,0},{2,3},{3,2},{4,5},{5,4},{6,7},{7,6},{8,9},{9,8},{10,11... | collective-permute-start | bytes 786440 | tf_op jit(solution)/shard_map/ppermute | solution.py:519
  35.2 5.0 %collective-permute-start.13 = (f32[64,512]{1,0:T(8,128)S(1)}, f32[64,512]{1,0:T(8,128)S(1)}, u32[]{:S(2)}, u32[]{:S(2)}) collective-permute-start(f32[64,512]{1,0:T(8,128)S(1)} %shard_map.110), channel_id=1, source_target_pairs={{0,2},{1,3},{2,0},{3,1},{4,6},{5,7},{6,4},{7,5},{8,10},{9,11},{10,... | collective-permute-start | bytes 393224 | tf_op jit(solution)/shard_map/ppermute | solution.py:519
  36.4 6.6 %collective-permute-start.12 = (f32[64,512]{1,0:T(8,128)S(1)}, f32[64,512]{1,0:T(8,128)S(1)}, u32[]{:S(2)}, u32[]{:S(2)}) collective-permute-start(f32[64,512]{1,0:T(8,128)S(1)} %shard_map.109), channel_id=1, source_target_pairs={{0,2},{1,3},{2,0},{3,1},{4,6},{5,7},{6,4},{7,5},{8,10},{9,11},{10,... | collective-permute-start | bytes 393224 | tf_op jit(solution)/shard_map/ppermute | solution.py:519
  37.4 11.4 %collective-permute-start.11 = (f32[128,512]{1,0:T(8,128)S(1)}, f32[128,512]{1,0:T(8,128)S(1)}, u32[]{:S(2)}, u32[]{:S(2)}) collective-permute-start(f32[128,512]{1,0:T(8,128)S(1)} %shard_map.108), channel_id=1, source_target_pairs={{0,3},{1,2},{2,1},{3,0},{4,7},{5,6},{6,5},{7,4},{8,11},{9,10},{10,... | collective-permute-start | bytes 786440 | tf_op jit(solution)/shard_map/ppermute | solution.py:519

commit v5 on v4

--- a/solution.py
+++ b/solution.py
@@ -155,14 +155,19 @@
 
 
 def back_kernel(s, which, started, ended, *refs):
-    in_refs, refs = refs[: sum(which.values())], refs[sum(which.values()) :]
+    in_refs, refs = refs[: len(which)], refs[len(which) :]
     table_ref, out_ref = refs[-2:]
+    part = jnp.zeros((s.batch, s.sticks), f32)
     me = lax.axis_index("plane")
     total = refs[0][...] if started else None
-    at = 0
-    for k, count in which.items():
-        high, low = split(jnp.concatenate([ref[...] for ref in in_refs[at : at + count]], 0))
-        at += count
+    blocks = {}
+    for (k, half, row), ref in zip(which, in_refs, strict=True):
+        if half is None:
+            blocks[k] = ref[...]
+        else:
+            blocks.setdefault(k, [part, part])[half] = ref[row : row + s.batch, :]
+    for k, block in blocks.items():
+        high, low = split(jnp.concatenate(block, 0) if isinstance(block, list) else block)
         table = table_ref[partner(me, k)]
         table = jnp.concatenate([table, table[:, : 2 * s.batch]], 1)
         term = dot(table, jnp.concatenate([high, high, low], 0))
@@ -337,9 +342,9 @@
                     flat_ref[row * s.planes : (row + 1) * s.planes, tile * lanes : (tile + 1) * lanes] = value[mine]
 
 
-def pick_kernel(s, which, count, *refs):
+def pick_kernel(s, which, count, joined, *refs):
     flat_refs, sticks_ref, refs = refs[:count], refs[count], refs[count + 1 :]
-    out_refs, (x_ref, y_ref, hot_ref) = refs[: len(which)], refs[len(which) :]
+    out_refs, (x_ref, y_ref, hot_ref) = refs[:-3], refs[-3:]
     me = lax.axis_index("plane")
     places(s, sticks_ref, [partner(me, k) for k in which], x_ref, y_ref)
     rows = 2 * s.planes
@@ -351,7 +356,8 @@
         found = dot(flat, hot_ref[...])
         for h in range(count):
             row = 2 * h * rows
-            out_refs[i][h * rows : (h + 1) * rows, :] = found[row : row + rows] + found[row + rows : row + 2 * rows]
+            out_ref, at = (out_refs[0], (i * count + h) * rows) if joined else (out_refs[i], h * rows)
+            out_ref[at : at + rows, :] = found[row : row + rows] + found[row + rows : row + 2 * rows]
 
 
 def band_on_ring(place, count):
@@ -376,6 +382,11 @@
 
 def partners(devices):
     return sorted(range(1, devices), key=lambda k: (k == 1, k % 2, k))
+
+
+def send_groups(devices):
+    soon, *others, near = partners(devices)
+    return [[soon, soon ^ 1], *(k for k in others if k != soon ^ 1), near]
 
 
 def stages(devices):
@@ -501,11 +512,13 @@
             for half in range(2)
         ]
 
-        def pick(which, flats):
+        def pick(which, flats, joined=False):
+            size = len(flats) * 2 * s.planes
+            shape = jax.ShapeDtypeStruct((size * len(which) if joined else size, s.sticks), f32)
             return kernel(
-                functools.partial(pick_kernel, s, which, len(flats)),
+                functools.partial(pick_kernel, s, which, len(flats), joined),
                 [*flats, stick_map],
-                [jax.ShapeDtypeStruct((len(flats) * 2 * s.planes, s.sticks), f32)] * len(which),
+                [shape] if joined else [shape] * len(which),
                 16 << 10,
                 1 << 31,
                 [
@@ -518,24 +531,26 @@
         def send(k, block):
             return lax.ppermute(block, "plane", [(i, i ^ k) for i in range(devices)])
 
-        soon, *far, near = partners(devices)
-        returned = {soon: [send(soon, *pick([soon], [flats[h]])) for h in range(2)]}
-        for k in far:
-            returned[k] = [send(k, *pick([k], flats))]
+        (soon, across), *others, near = send_groups(devices)
+        both = send(soon, *pick([across, soon], [flats[0]], True))
+        hop, last = pick([across, soon], [flats[1]])
+        hop = send(soon, hop)
+        last = send(soon, last)
+        returned = [(k, None, 0, send(k, *pick([k], flats))) for k in others]
         beside, own = pick([near, 0], flats)
-        returned |= {near: [send(near, beside)], 0: [own]}
-        late = far[-1]
-        counts = {k: len(blocks) for k, blocks in returned.items() if k != late}
+        returned += [(near, None, 0, send(near, beside)), (0, None, 0, own), (soon, 0, s.batch, both)]
+        returned.append((across, 0, 0, send(near, both[: s.batch])))
+        late = [(across, 1, 0, send(near, hop)), (soon, 1, 0, last)]
         begun = kernel(
-            functools.partial(back_kernel, s, counts, False, False),
-            [*(block for k in counts for block in returned[k]), tab["z_back"]],
+            functools.partial(back_kernel, s, [block[:3] for block in returned], False, False),
+            [*(block[3] for block in returned), tab["z_back"]],
             jax.ShapeDtypeStruct((s.depth_rows, s.sticks), f32),
             16 << 10,
             1 << 31,
         )
         result = kernel(
-            functools.partial(back_kernel, s, {late: 1}, True, True),
-            [*returned[late], begun, stick_map, tab["z_back"]],
+            functools.partial(back_kernel, s, [block[:3] for block in late], True, True),
+            [*(block[3] for block in late), begun, stick_map, tab["z_back"]],
             jax.ShapeDtypeStruct((1,) + given.shape[1:], f32),
             16 << 10,
             1 << 31,

time: 50.2 us -> 46.6 us (0.928)
  waiting for transfers between devices: 15.8 us -> 9.47 us
  starting transfers between devices: 15.7 us -> 17.9 us
    ppermute x4 -> x6, waiting for transfers between devices: 8.99 us -> 2.37 us  [send(): return lax.ppermute(block, 'plane', [(i, i ^ k) for i in range(devices)])]
    ppermute x4 -> x6, starting transfers between devices: 6.27 us -> 8.44 us  [send(): return lax.ppermute(block, 'plane', [(i, i ^ k) for i in range(devices)])]
    ppermute x4, starting transfers between devices: 2.28 us -> 0.79 us  [ring(): down = lax.ppermute(down, 'band', against)]
    ppermute x4, starting transfers between devices: 4.45 us -> 5.92 us  [ring(): up = lax.ppermute(up, 'band', along)]
    pallas_call x14 -> x13, Pallas kernels: 18.3 us -> 18.3 us  [kernel(): pl.pallas_call(body, in_specs=[place] * len(inputs) + [HBM] * len(fetched...]
  transfers between devices with their start and end apart: 15 -> 17, of which waited for: 7 -> 8; matrix products, arithmetic and copies ran while one was open for 0% -> 0% of each run, Pallas kernels for 28% -> 37%
where the time goes in v5:
time: 46.6 us; the launch traced here: 45.9 us
  Pallas kernels  18.3 us (39%)
  starting transfers between devices  17.9 us (38%)
  waiting for transfers between devices  9.47 us (20%)
    pallas_call x13, Pallas kernels, kernel(): pl.pallas_call(body, in_specs=[place] * len(inputs) + [HBM] * len(fetched...  18.3 us
    ppermute x6, starting transfers between devices, send(): return lax.ppermute(block, 'plane', [(i, i ^ k) for i in range(devices)])  8.44 us
    ppermute x4, starting transfers between devices, ring(): up = lax.ppermute(up, 'band', along)  5.92 us
    ppermute x3, waiting for transfers between devices, exchange(): lax.ppermute(blocks[k], 'plane', [(i, i ^ k) for i in range(devices)])  4.83 us
    ppermute x3, starting transfers between devices, exchange(): lax.ppermute(blocks[k], 'plane', [(i, i ^ k) for i in range(devices)])  2.73 us
    ppermute x6, waiting for transfers between devices, send(): return lax.ppermute(block, 'plane', [(i, i ^ k) for i in range(devices)])  2.37 us
    ppermute x4, waiting for transfers between devices, ring(): up = lax.ppermute(up, 'band', along)  2.25 us
  transfers between devices with their start and end apart: 17, of which 8 were waited for; matrix products, arithmetic and copies ran while one was open for 0% of the time, Pallas kernels for 37%

profile of v5, /device:TPU:1, one launch (start us, length us, event | category | flops | bytes accessed | tf_op | source)
XLA Modules:
  0.0 45.9 jit_solution(1649970263939321597)
XLA Ops:
  0.0 2.1 %collective-permute-start.3 = (f32[32,16,128]{2,1,0:T(8,128)}, f32[32,16,128]{2,1,0:T(8,128)S(1)}, u32[]{:S(2)}, u32[]{:S(2)}) collective-permute-start(f32[32,16,128]{2,1,0:T(8,128)} %refs_9_.1), channel_id=1, source_target_pairs={{0,8},{8,16},{16,24},{24,28},{28,20},{20,12},{12,4},{4,0},{1,9},{9... | collective-permute-start | bytes 786440 | tf_op jit(solution)/shard_map/ppermute | solution.py:421
  2.1 2.1 %shard_map.100 = (f32[128,512]{1,0:T(8,128)S(1)}, f32[128,512]{1,0:T(8,128)S(1)}, f32[128,512]{1,0:T(8,128)S(1)}, f32[128,512]{1,0:T(8,128)S(1)}) custom-call(f32[1,65,4,512]{3,2,1,0:T(4,128)} %bitcast.2, s32[3,2048]{1,0:T(4,128)} %refs_3_.2, bf16[4,128,816]{2,1,0:T(8,128)(2,1)} %constant.14.clone.table_hbm), custom_call_target="tpu_custom_call" | custom-call | flops 2147483648 | bytes 1048576 | tf_op jit(solution)/shard_map/pallas_call | solution.py:432
  4.2 1.0 %collective-permute-start.2 = (f32[128,512]{1,0:T(8,128)S(1)}, f32[128,512]{1,0:T(8,128)S(1)}, u32[]{:S(2)}, u32[]{:S(2)}) collective-permute-start(f32[128,512]{1,0:T(8,128)S(1)} %get-tuple-element.24), channel_id=1, source_target_pairs={{0,1},{1,0},{2,3},{3,2},{4,5},{5,4},{6,7},{7,6},{8,9},{9,8},{10,11... | collective-permute-start | bytes 786440 | tf_op jit(solution)/shard_map/ppermute | solution.py:411
  5.3 1.7 %collective-permute-start.1 = (f32[128,512]{1,0:T(8,128)S(1)}, f32[128,512]{1,0:T(8,128)S(1)}, u32[]{:S(2)}, u32[]{:S(2)}) collective-permute-start(f32[128,512]{1,0:T(8,128)S(1)} %get-tuple-element.22), channel_id=1, source_target_pairs={{0,2},{1,3},{2,0},{3,1},{4,6},{5,7},{6,4},{7,5},{8,10},{9,11},{10,... | collective-permute-start | bytes 786440 | tf_op jit(solution)/shard_map/ppermute | solution.py:411
  7.0 1.3 %collective-permute-done.3.refs_1_ = f32[32,16,128]{2,1,0:T(8,128)S(1)} collective-permute-done((f32[32,16,128]{2,1,0:T(8,128)}, f32[32,16,128]{2,1,0:T(8,128)S(1)}, u32[]{:S(2)}, u32[]{:S(2)}) %collective-permute-start.3) | collective-permute-done | bytes 262176 | tf_op jit(solution)/shard_map/ppermute | solution.py:421
  8.3 1.2 %collective-permute-start.5 = (f32[32,16,128]{2,1,0:T(8,128)S(1)}, f32[32,16,128]{2,1,0:T(8,128)S(1)}, u32[]{:S(2)}, u32[]{:S(2)}) collective-permute-start(f32[32,16,128]{2,1,0:T(8,128)S(1)} %collective-permute-done.3.refs_1_), channel_id=1, source_target_pairs={{0,8},{8,16},{16,24},{24,28},{28,20},{20,12},{12,4},{4,0},{1,9},{9... | collective-permute-start | bytes 786440 | tf_op jit(solution)/shard_map/ppermute | solution.py:421
  9.8 1.6 %shard_map.101 = (f32[1088,256]{1,0:T(8,128)S(1)}, bf16[2,256,512]{2,1,0:T(8,128)(2,1)S(1)}, bf16[128,240]{1,0:T(8,128)(2,1)S(1)}, bf16[160,256]{1,0:T(8,128)(2,...) custom-call(f32[128,512]{1,0:T(8,128)S(1)} %get-tuple-element.23.ref, ...), custom_call_target="tpu_custom_call" | custom-call | flops 2147483648 | bytes 1048576 | tf_op jit(solution)/shard_map/pallas_call | solution.py:432
  11.4 2.1 %collective-permute-done.1.refs_0_ = f32[128,512]{1,0:T(8,128)S(1)} collective-permute-done((f32[128,512]{1,0:T(8,128)S(1)}, f32[128,512]{1,0:T(8,128)S(1)}, u32[]{:S(2)}, u32[]{:S(2)}) %collective-permute-start.1) | collective-permute-done | bytes 262176 | tf_op jit(solution)/shard_map/ppermute | solution.py:411
  14.9 1.0 %collective-permute-start.7 = (f32[32,16,128]{2,1,0:T(8,128)S(1)}, f32[32,16,128]{2,1,0:T(8,128)S(1)}, u32[]{:S(2)}, u32[]{:S(2)}) collective-permute-start(f32[32,16,128]{2,1,0:T(8,128)S(1)} %collective-permute-done.5.refs_3_), channel_id=1, source_target_pairs={{0,8},{8,16},{16,24},{24,28},{28,20},{20,12},{12,4},{4,0},{1,9},{9... | collective-permute-start | bytes 786440 | tf_op jit(solution)/shard_map/ppermute | solution.py:421
  16.4 2.7 %collective-permute-done.refs_0_ = f32[128,512]{1,0:T(8,128)S(1)} collective-permute-done((f32[128,512]{1,0:T(8,128)S(1)}, f32[128,512]{1,0:T(8,128)S(1)}, u32[]{:S(2)}, u32[]{:S(2)}) %collective-permute-start) | collective-permute-done | bytes 262176 | tf_op jit(solution)/shard_map/ppermute | solution.py:411
  19.1 1.8 %shard_map.103.half_ref = f32[4,1560,128]{2,1,0:T(8,128)S(1)} custom-call(f32[128,512]{1,0:T(8,128)S(1)} %collective-permute-done.refs_0_, f32[1088,256]{1,0:T(8,128)S(1)} %shard_map.102.refs_1_, s32[3,2048]{1,0:T(4,128)S(1)} %copy-done, bf16[2,256,512]{2,1,0:T(8,128)(2,1)S(1)} %get-tuple-element.26.refs_3_), custom_call_target="tpu_custom_call" | custom-call | flops 2147483648 | bytes 1048576 | tf_op jit(solution)/shard_map/pallas_call | solution.py:432
  20.9 2.0 %shard_map.104.real_ref = f32[32,144,256]{2,1,0:T(8,128)S(1)} custom-call(f32[4,1560,128]{2,1,0:T(8,128)S(1)} %shard_map.103.half_ref, bf16[128,240]{1,0:T(8,128)(2,1)S(1)} %get-tuple-element.27.x_ahead_ref), custom_call_target="tpu_custom_call" | custom-call | flops 2147483648 | bytes 1048576 | tf_op jit(solution)/shard_map/pallas_call | solution.py:432
  22.9 1.6 %collective-permute-start.13 = (f32[16,16,128]{2,1,0:T(8,128)S(1)}, f32[16,16,128]{2,1,0:T(8,128)S(1)}, u32[]{:S(2)}, u32[]{:S(2)}) collective-permute-start(f32[16,16,128]{2,1,0:T(8,128)S(1)} %slice.13), channel_id=1, source_target_pairs={{0,8},{8,16},{16,24},{24,28},{28,20},{20,12},{12,4},{4,0},{1,9},{9... | collective-permute-start | bytes 393224 | tf_op jit(solution)/shard_map/ppermute | solution.py:421
  24.5 2.4 %shard_map.105.first_ref = f32[4,1560,128]{2,1,0:T(8,128)S(1)} custom-call(f32[32,144,256]{2,1,0:T(8,128)S(1)} %shard_map.104.real_ref, f32[32,16,128]{2,1,0:T(8,128)S(1)} %get-tuple-element.28.refs_0_, f32[32,16,128]{2,1,0:T(8,128)S(1)} %collective-permute-done.3.refs_1_, f32[32,16,128]{2,1,0:T(8,128)S(1)} %collective-permute-done.4.refs_2_, ...), custom_call_target="tpu_custom_call" | custom-call | flops 2147483648 | bytes 1048576 | tf_op jit(solution)/shard_map/pallas_call | solution.py:432
  27.3 1.4 %shard_map.108.refs_0_ = bf16[128,2176]{1,0:T(8,128)(2,1)S(1)} custom-call(f32[4,1560,128]{2,1,0:T(8,128)S(1)} %shard_map.105.first_ref, f32[32,144,256]{2,1,0:T(8,128)S(1)} %shard_map.104.real_ref, f32[16,16,128]{2,1,0:T(8,128)S(1)} %collective-permute-done.13.slab_ref, bf16[8,80,48]{2,1,0:T(8,128)(2,1)S(1)} %get-tuple-element.30.x_last_ref, ...), custom_call_target="tpu_custom_call" | custom-call | flops 2147483648 | bytes 1048576 | tf_op jit(solution)/shard_map/pallas_call | solution.py:432
  29.4 2.0 %collective-permute-start.15 = (f32[128,512]{1,0:T(8,128)S(1)}, f32[128,512]{1,0:T(8,128)S(1)}, u32[]{:S(2)}, u32[]{:S(2)}) collective-permute-start(f32[128,512]{1,0:T(8,128)S(1)} %shard_map.110), channel_id=1, source_target_pairs={{0,2},{1,3},{2,0},{3,1},{4,6},{5,7},{6,4},{7,5},{8,10},{9,11},{10,... | collective-permute-start | bytes 786440 | tf_op jit(solution)/shard_map/ppermute | solution.py:532
  31.5 1.4 %shard_map.106.refs_0_.refs_1_ = bf16[128,2176]{1,0:T(8,128)(2,1)S(1)} custom-call(f32[4,1560,128]{2,1,0:T(8,128)S(1)} %shard_map.105.first_ref, f32[32,144,256]{2,1,0:T(8,128)S(1)} %shard_map.104.real_ref, f32[16,16,128]{2,1,0:T(8,128)S(1)} %collective-permute-done.9.slab_ref, bf16[8,80,48]{2,1,0:T(8,128)(2,1)S(1)} %get-tuple-element.30.x_last_ref, ...), custom_call_target="tpu_custom_call" | custom-call | flops 2147483648 | bytes 1048576 | tf_op jit(solution)/shard_map/pallas_call | solution.py:432
  32.8 1.4 %shard_map.109 = (f32[128,512]{1,0:T(8,128)S(1)}, f32[128,512]{1,0:T(8,128)S(1)}) custom-call(bf16[128,2176]{1,0:T(8,128)(2,1)S(1)} %shard_map.108.refs_0_, bf16[128,2176]{1,0:T(8,128)(2,1)S(1)} %shard_map.106.refs_0_.refs_1_, s32[3,2048]{1,0:T(4,128)S(1)} %copy-done), custom_call_target="tpu_custom_call" | custom-call | flops 2147483648 | bytes 1048576 | tf_op jit(solution)/shard_map/pallas_call | solution.py:432
  34.2 1.4 %collective-permute-start.14 = (f32[128,512]{1,0:T(8,128)S(1)}, f32[128,512]{1,0:T(8,128)S(1)}, u32[]{:S(2)}, u32[]{:S(2)}) collective-permute-start(f32[128,512]{1,0:T(8,128)S(1)} %get-tuple-element.34), channel_id=1, source_target_pairs={{0,1},{1,0},{2,3},{3,2},{4,5},{5,4},{6,7},{7,6},{8,9},{9,8},{10,11... | collective-permute-start | bytes 786440 | tf_op jit(solution)/shard_map/ppermute | solution.py:532
  36.8 2.0 %collective-permute-start.16 = (f32[64,512]{1,0:T(8,128)S(1)}, f32[64,512]{1,0:T(8,128)S(1)}, u32[]{:S(2)}, u32[]{:S(2)}) collective-permute-start(f32[64,512]{1,0:T(8,128)S(1)} %slice.14), channel_id=1, source_target_pairs={{0,1},{1,0},{2,3},{3,2},{4,5},{5,4},{6,7},{7,6},{8,9},{9,8},{10,11... | collective-permute-start | bytes 393224 | tf_op jit(solution)/shard_map/ppermute | solution.py:532
  38.8 2.0 %collective-permute-start.12 = (f32[64,512]{1,0:T(8,128)S(1)}, f32[64,512]{1,0:T(8,128)S(1)}, u32[]{:S(2)}, u32[]{:S(2)}) collective-permute-start(f32[64,512]{1,0:T(8,128)S(1)} %get-tuple-element.33), channel_id=1, source_target_pairs={{0,2},{1,3},{2,0},{3,1},{4,6},{5,7},{6,4},{7,5},{8,10},{9,11},{10,... | collective-permute-start | bytes 393224 | tf_op jit(solution)/shard_map/ppermute | solution.py:532
  41.5 0.9 %collective-permute-start.11 = (f32[64,512]{1,0:T(8,128)S(1)}, f32[64,512]{1,0:T(8,128)S(1)}, u32[]{:S(2)}, u32[]{:S(2)}) collective-permute-start(f32[64,512]{1,0:T(8,128)S(1)} %collective-permute-done.10), channel_id=1, source_target_pairs={{0,1},{1,0},{2,3},{3,2},{4,5},{5,4},{6,7},{7,6},{8,9},{9,8},{10,11... | collective-permute-start | bytes 393224 | tf_op jit(solution)/shard_map/ppermute | solution.py:532
  43.2 1.4 %collective-permute-done.12.refs_1_ = f32[64,512]{1,0:T(8,128)S(1)} collective-permute-done((f32[64,512]{1,0:T(8,128)S(1)}, f32[64,512]{1,0:T(8,128)S(1)}, u32[]{:S(2)}, u32[]{:S(2)}) %collective-permute-start.12) | collective-permute-done | bytes 131104 | tf_op jit(solution)/shard_map/ppermute | solution.py:532
  44.6 1.3 %shard_map.112 = f32[1,65,4,512]{3,2,1,0:T(4,128)} custom-call(f32[64,512]{1,0:T(8,128)S(1)} %collective-permute-done.11.refs_0_, f32[64,512]{1,0:T(8,128)S(1)} %collective-permute-done.12.refs_1_, f32[272,512]{1,0:T(8,128)S(1)} %shard_map.111.refs_2_, s32[3,2048]{1,0:T(4,128)S(1)} %copy-done, bf16[4,272,256]{2,1,0:T(8,128)(2,1)S(1)} %get-tuple-element.36.refs_4_), custom_call_target="tpu_custom_call" | custom-call | flops 2147483648 | bytes 1048576 | tf_op jit(solution)/shard_map/pallas_call | solution.py:432
  (28 shorter events, 6.1 us)
Async XLA Ops:
  0.0 8.3 %collective-permute-start.3 = (f32[32,16,128]{2,1,0:T(8,128)}, f32[32,16,128]{2,1,0:T(8,128)S(1)}, u32[]{:S(2)}, u32[]{:S(2)}) collective-permute-start(f32[32,16,128]{2,1,0:T(8,128)} %refs_9_.1), channel_id=1, source_target_pairs={{0,8},{8,16},{16,24},{24,28},{28,20},{20,12},{12,4},{4,0},{1,9},{9... | collective-permute-start | bytes 786440 | tf_op jit(solution)/shard_map/ppermute | solution.py:421
  2.1 7.4 %collective-permute-start.4 = (f32[32,16,128]{2,1,0:T(8,128)}, f32[32,16,128]{2,1,0:T(8,128)S(1)}, u32[]{:S(2)}, u32[]{:S(2)}) collective-permute-start(f32[32,16,128]{2,1,0:T(8,128)} %refs_9_.1), channel_id=1, source_target_pairs={{8,0},{16,8},{24,16},{28,24},{20,28},{12,20},{4,12},{0,4},{9,1},{1... | collective-permute-start | bytes 786440 | tf_op jit(solution)/shard_map/ppermute | solution.py:422
  2.1 7.6 %copy-start = (s32[3,2048]{1,0:T(4,128)S(1)}, s32[3,2048]{1,0:T(4,128)}, u32[]{:S(2)}) copy-start(s32[3,2048]{1,0:T(4,128)} %refs_3_.2) | copy-start | bytes 73732
  4.2 5.5 %collective-permute-start.2 = (f32[128,512]{1,0:T(8,128)S(1)}, f32[128,512]{1,0:T(8,128)S(1)}, u32[]{:S(2)}, u32[]{:S(2)}) collective-permute-start(f32[128,512]{1,0:T(8,128)S(1)} %get-tuple-element.24), channel_id=1, source_target_pairs={{0,1},{1,0},{2,3},{3,2},{4,5},{5,4},{6,7},{7,6},{8,9},{9,8},{10,11... | collective-permute-start | bytes 786440 | tf_op jit(solution)/shard_map/ppermute | solution.py:411
  5.3 8.2 %collective-permute-start.1 = (f32[128,512]{1,0:T(8,128)S(1)}, f32[128,512]{1,0:T(8,128)S(1)}, u32[]{:S(2)}, u32[]{:S(2)}) collective-permute-start(f32[128,512]{1,0:T(8,128)S(1)} %get-tuple-element.22), channel_id=1, source_target_pairs={{0,2},{1,3},{2,0},{3,1},{4,6},{5,7},{6,4},{7,5},{8,10},{9,11},{10,... | collective-permute-start | bytes 786440 | tf_op jit(solution)/shard_map/ppermute | solution.py:411
  6.9 12.2 %collective-permute-start = (f32[128,512]{1,0:T(8,128)S(1)}, f32[128,512]{1,0:T(8,128)S(1)}, u32[]{:S(2)}, u32[]{:S(2)}) collective-permute-start(f32[128,512]{1,0:T(8,128)S(1)} %get-tuple-element.21), channel_id=1, source_target_pairs={{0,3},{1,2},{2,1},{3,0},{4,7},{5,6},{6,5},{7,4},{8,11},{9,10},{10,... | collective-permute-start | bytes 786440 | tf_op jit(solution)/shard_map/ppermute | solution.py:411
  8.3 6.6 %collective-permute-start.5 = (f32[32,16,128]{2,1,0:T(8,128)S(1)}, f32[32,16,128]{2,1,0:T(8,128)S(1)}, u32[]{:S(2)}, u32[]{:S(2)}) collective-permute-start(f32[32,16,128]{2,1,0:T(8,128)S(1)} %collective-permute-done.3.refs_1_), channel_id=1, source_target_pairs={{0,8},{8,16},{16,24},{24,28},{28,20},{20,12},{12,4},{4,0},{1,9},{9... | collective-permute-start | bytes 786440 | tf_op jit(solution)/shard_map/ppermute | solution.py:421
  9.5 6.3 %collective-permute-start.6 = (f32[32,16,128]{2,1,0:T(8,128)S(1)}, f32[32,16,128]{2,1,0:T(8,128)S(1)}, u32[]{:S(2)}, u32[]{:S(2)}) collective-permute-start(f32[32,16,128]{2,1,0:T(8,128)S(1)} %collective-permute-done.4.refs_2_), channel_id=1, source_target_pairs={{8,0},{16,8},{24,16},{28,24},{20,28},{12,20},{4,12},{0,4},{9,1},{1... | collective-permute-start | bytes 786440 | tf_op jit(solution)/shard_map/ppermute | solution.py:422
  14.9 7.9 %collective-permute-start.7 = (f32[32,16,128]{2,1,0:T(8,128)S(1)}, f32[32,16,128]{2,1,0:T(8,128)S(1)}, u32[]{:S(2)}, u32[]{:S(2)}) collective-permute-start(f32[32,16,128]{2,1,0:T(8,128)S(1)} %collective-permute-done.5.refs_3_), channel_id=1, source_target_pairs={{0,8},{8,16},{16,24},{24,28},{28,20},{20,12},{12,4},{4,0},{1,9},{9... | collective-permute-start | bytes 786440 | tf_op jit(solution)/shard_map/ppermute | solution.py:421
  15.9 8.6 %collective-permute-start.8 = (f32[32,16,128]{2,1,0:T(8,128)S(1)}, f32[32,16,128]{2,1,0:T(8,128)S(1)}, u32[]{:S(2)}, u32[]{:S(2)}) collective-permute-start(f32[32,16,128]{2,1,0:T(8,128)S(1)} %collective-permute-done.6.refs_4_), channel_id=1, source_target_pairs={{8,0},{16,8},{24,16},{28,24},{20,28},{12,20},{4,12},{0,4},{9,1},{1... | collective-permute-start | bytes 786440 | tf_op jit(solution)/shard_map/ppermute | solution.py:422
  22.9 4.4 %collective-permute-start.13 = (f32[16,16,128]{2,1,0:T(8,128)S(1)}, f32[16,16,128]{2,1,0:T(8,128)S(1)}, u32[]{:S(2)}, u32[]{:S(2)}) collective-permute-start(f32[16,16,128]{2,1,0:T(8,128)S(1)} %slice.13), channel_id=1, source_target_pairs={{0,8},{8,16},{16,24},{24,28},{28,20},{20,12},{12,4},{4,0},{1,9},{9... | collective-permute-start | bytes 393224 | tf_op jit(solution)/shard_map/ppermute | solution.py:421
  24.5 7.0 %collective-permute-start.9 = (f32[16,16,128]{2,1,0:T(8,128)S(1)}, f32[16,16,128]{2,1,0:T(8,128)S(1)}, u32[]{:S(2)}, u32[]{:S(2)}) collective-permute-start(f32[16,16,128]{2,1,0:T(8,128)S(1)} %slice.12), channel_id=1, source_target_pairs={{8,0},{16,8},{24,16},{28,24},{20,28},{12,20},{4,12},{0,4},{9,1},{1... | collective-permute-start | bytes 393224 | tf_op jit(solution)/shard_map/ppermute | solution.py:422
  29.4 7.3 %collective-permute-start.15 = (f32[128,512]{1,0:T(8,128)S(1)}, f32[128,512]{1,0:T(8,128)S(1)}, u32[]{:S(2)}, u32[]{:S(2)}) collective-permute-start(f32[128,512]{1,0:T(8,128)S(1)} %shard_map.110), channel_id=1, source_target_pairs={{0,2},{1,3},{2,0},{3,1},{4,6},{5,7},{6,4},{7,5},{8,10},{9,11},{10,... | collective-permute-start | bytes 786440 | tf_op jit(solution)/shard_map/ppermute | solution.py:532
  34.2 8.2 %collective-permute-start.14 = (f32[128,512]{1,0:T(8,128)S(1)}, f32[128,512]{1,0:T(8,128)S(1)}, u32[]{:S(2)}, u32[]{:S(2)}) collective-permute-start(f32[128,512]{1,0:T(8,128)S(1)} %get-tuple-element.34), channel_id=1, source_target_pairs={{0,1},{1,0},{2,3},{3,2},{4,5},{5,4},{6,7},{7,6},{8,9},{9,8},{10,11... | collective-permute-start | bytes 786440 | tf_op jit(solution)/shard_map/ppermute | solution.py:532
  36.4 5.1 %collective-permute-start.10 = (f32[64,512]{1,0:T(8,128)S(1)}, f32[64,512]{1,0:T(8,128)S(1)}, u32[]{:S(2)}, u32[]{:S(2)}) collective-permute-start(f32[64,512]{1,0:T(8,128)S(1)} %get-tuple-element.32), channel_id=1, source_target_pairs={{0,2},{1,3},{2,0},{3,1},{4,6},{5,7},{6,4},{7,5},{8,10},{9,11},{10,... | collective-permute-start | bytes 393224 | tf_op jit(solution)/shard_map/ppermute | solution.py:532
  36.8 5.7 %collective-permute-start.16 = (f32[64,512]{1,0:T(8,128)S(1)}, f32[64,512]{1,0:T(8,128)S(1)}, u32[]{:S(2)}, u32[]{:S(2)}) collective-permute-start(f32[64,512]{1,0:T(8,128)S(1)} %slice.14), channel_id=1, source_target_pairs={{0,1},{1,0},{2,3},{3,2},{4,5},{5,4},{6,7},{7,6},{8,9},{9,8},{10,11... | collective-permute-start | bytes 393224 | tf_op jit(solution)/shard_map/ppermute | solution.py:532
  38.8 5.8 %collective-permute-start.12 = (f32[64,512]{1,0:T(8,128)S(1)}, f32[64,512]{1,0:T(8,128)S(1)}, u32[]{:S(2)}, u32[]{:S(2)}) collective-permute-start(f32[64,512]{1,0:T(8,128)S(1)} %get-tuple-element.33), channel_id=1, source_target_pairs={{0,2},{1,3},{2,0},{3,1},{4,6},{5,7},{6,4},{7,5},{8,10},{9,11},{10,... | collective-permute-start | bytes 393224 | tf_op jit(solution)/shard_map/ppermute | solution.py:532
  41.5 3.1 %collective-permute-start.11 = (f32[64,512]{1,0:T(8,128)S(1)}, f32[64,512]{1,0:T(8,128)S(1)}, u32[]{:S(2)}, u32[]{:S(2)}) collective-permute-start(f32[64,512]{1,0:T(8,128)S(1)} %collective-permute-done.10), channel_id=1, source_target_pairs={{0,1},{1,0},{2,3},{3,2},{4,5},{5,4},{6,7},{7,6},{8,9},{9,8},{10,11... | collective-permute-start | bytes 393224 | tf_op jit(solution)/shard_map/ppermute | solution.py:532

commit v6 on v5

--- a/solution.py
+++ b/solution.py
@@ -43,13 +43,14 @@
         self.kept = 2 * (self.even + self.odd)
         self.batch = 2 * planes
         self.step = self.batch + 1
-        self.depth_rows = -(-4 * span // 16) * 16
+        self.depths = span - 2
+        self.depth_rows = -(-4 * self.depths // 16) * 16
 
 
 def tables(s, bands):
     turn = 2.0 * math.pi / s.length
     grid = np.arange(s.length)
-    depth = np.arange(s.span) - s.radius
+    depth = np.arange(s.depths) + 1 - s.radius
     y = np.arange(s.rows_y) + 1 - s.radius
 
     def trig(left, right):
@@ -57,8 +58,8 @@
         return np.cos(angle), np.sin(angle)
 
     cos, sin = trig(depth, grid)
-    ahead = np.zeros((s.devices, 2, 2, s.planes, s.span, 2, 2))
-    back = np.zeros((s.devices, s.span, 2, 2, 2, 2, s.planes))
+    ahead = np.zeros((s.devices, 2, 2, s.planes, s.depths, 2, 2))
+    back = np.zeros((s.devices, s.depths, 2, 2, 2, 2, s.planes))
     scale = 1.0 / float(s.length) ** 3
     for d in range(s.devices):
         own = slice(d * s.planes, (d + 1) * s.planes)
@@ -72,10 +73,10 @@
             back[d, :, o, 0, 1, o] = n * scale
             back[d, :, o, 1, 0, o] = -n * scale
             back[d, :, o, 1, 1, o] = c * scale
-    gap = s.depth_rows - 4 * s.span
-    ahead = np.pad(ahead.reshape(s.devices, 2 * s.batch, 4 * s.span), ((0, 0), (0, 0), (0, gap)))
-    back = back.reshape(s.devices, 4 * s.span, 4, 2, s.planes // 2).transpose(0, 1, 3, 2, 4)
-    back = np.pad(back.reshape(s.devices, 4 * s.span, 2 * s.batch), ((0, 0), (0, gap), (0, 0)))
+    gap = s.depth_rows - 4 * s.depths
+    ahead = np.pad(ahead.reshape(s.devices, 2 * s.batch, 4 * s.depths), ((0, 0), (0, 0), (0, gap)))
+    back = back.reshape(s.devices, 4 * s.depths, 4, 2, s.planes // 2).transpose(0, 1, 3, 2, 4)
+    back = np.pad(back.reshape(s.devices, 4 * s.depths, 2 * s.batch), ((0, 0), (0, gap), (0, 0)))
 
     cos, sin = trig(y, grid)
     y_ahead = np.zeros((2, 2, s.rows_y, 2, 2, s.length))
@@ -111,7 +112,7 @@
     high, low = halves(x_back)
     by_slab = x_back.reshape(s.kept, bands, s.length // bands).transpose(1, 0, 2)
     return dict(
-        z_ahead=beside(ahead, 2, (0, 1, 0)),
+        z_ahead=beside(ahead, 2, (0, 1)),
         z_back=beside(back, 2, (0, 1)),
         y_ahead=np.stack(halves(y_ahead)),
         y_back=np.stack(halves(y_back)),
@@ -131,7 +132,7 @@
 
 def live_of(s, sticks_ref, source):
     columns = pl.ds(pl.multiple_of(source * s.sticks, s.sticks), s.sticks)
-    depth = lax.broadcasted_iota(jnp.int32, (4 * s.span, s.sticks), 0) // 4 - s.radius
+    depth = lax.broadcasted_iota(jnp.int32, (4 * s.depths, s.sticks), 0) // 4 + 1 - s.radius
     return jnp.abs(depth) <= sticks_ref[2:3, columns]
 
 
@@ -145,13 +146,14 @@
     copies[0].wait()
     live = live_of(s, sticks_ref, me)
     copies[1].wait()
-    data = jnp.where(live, coeffs_ref[0].reshape(4 * s.span, s.sticks), 0.0)
-    gap = jnp.zeros((s.depth_rows - 4 * s.span, s.sticks), f32)
+    data = jnp.where(live, coeffs_ref[0, 1 : s.span - 1].reshape(4 * s.depths, s.sticks), 0.0)
+    gap = jnp.zeros((s.depth_rows - 4 * s.depths, s.sticks), f32)
     high, low = split(jnp.concatenate([data, gap], 0))
     data = jnp.concatenate([high, high, low], 0)
     copies[2].wait()
     for k in [*partners(s.devices), 0]:
-        out_refs[k][...] = dot(table_ref[partner(me, k)], data)
+        table = table_ref[partner(me, k)]
+        out_refs[k][...] = dot(jnp.concatenate([table, table[:, : s.depth_rows]], 1), data)
 
 
 def back_kernel(s, which, started, ended, *refs):
@@ -173,8 +175,10 @@
         term = dot(table, jnp.concatenate([high, high, low], 0))
         total = term if total is None else total + term
     if ended:
-        total = jnp.where(live_of(s, refs[-3], me), total[: 4 * s.span], 0.0)
-        out_ref[0] = total.reshape(s.span, 4, s.sticks)
+        total = jnp.where(live_of(s, refs[-3], me), total[: 4 * s.depths], 0.0)
+        out_ref[0, 1 : s.span - 1] = total.reshape(s.depths, 4, s.sticks)
+        for depth in (0, s.span - 1):
+            out_ref[0, depth] = jnp.zeros((4, s.sticks), f32)
     else:
         out_ref[...] = total
 
@@ -534,13 +538,13 @@
         (soon, across), *others, near = send_groups(devices)
         both = send(soon, *pick([across, soon], [flats[0]], True))
         hop, last = pick([across, soon], [flats[1]])
-        hop = send(soon, hop)
+        hop = send(across, hop)
         last = send(soon, last)
         returned = [(k, None, 0, send(k, *pick([k], flats))) for k in others]
         beside, own = pick([near, 0], flats)
         returned += [(near, None, 0, send(near, beside)), (0, None, 0, own), (soon, 0, s.batch, both)]
-        returned.append((across, 0, 0, send(near, both[: s.batch])))
-        late = [(across, 1, 0, send(near, hop)), (soon, 1, 0, last)]
+        late = [(across, 0, 0, send(near, both[: s.batch]))]
+        late += [(across, 1, 0, hop), (soon, 1, 0, last)]
         begun = kernel(
             functools.partial(back_kernel, s, [block[:3] for block in returned], False, False),
             [*(block[3] for block in returned), tab["z_back"]],

time: 46.6 us -> 47.9 us (1.028)
  the two profiles are of different devices: /device:TPU:1 before, /device:TPU:0 now
where the time goes in v6:
time: 47.9 us; the launch traced here: 47.8 us
  Pallas kernels  17.9 us (37%)
  starting transfers between devices  15.2 us (32%)
  waiting for transfers between devices  14.5 us (30%)
    pallas_call x13, Pallas kernels, kernel(): pl.pallas_call(body, in_specs=[place] * len(inputs) + [HBM] * len(fetched...  17.9 us
    ppermute x4, starting transfers between devices, ring(): up = lax.ppermute(up, 'band', along)  7.94 us
    ppermute x5, waiting for transfers between devices, send(): return lax.ppermute(block, 'plane', [(i, i ^ k) for i in range(devices)])  5.81 us
    ppermute x4, waiting for transfers between devices, ring(): up = lax.ppermute(up, 'band', along)  5.47 us
    ppermute x5, starting transfers between devices, send(): return lax.ppermute(block, 'plane', [(i, i ^ k) for i in range(devices)])  3.84 us
    ppermute x3, starting transfers between devices, exchange(): lax.ppermute(blocks[k], 'plane', [(i, i ^ k) for i in range(devices)])  2.11 us
    ppermute x4, waiting for transfers between devices, ring(): down = lax.ppermute(down, 'band', against)  2 us
    ppermute x4, starting transfers between devices, ring(): down = lax.ppermute(down, 'band', against)  1.29 us
  transfers between devices with their start and end apart: 16, of which 8 were waited for; matrix products, arithmetic and copies ran while one was open for 0% of the time, Pallas kernels for 35%

profile of v6, /device:TPU:0, one launch (start us, length us, event | category | flops | bytes accessed | tf_op | source)
XLA Modules:
  0.0 47.8 jit_solution(11777232603621929180)
XLA Ops:
  0.0 3.1 %collective-permute-start.3 = (f32[32,16,128]{2,1,0:T(8,128)}, f32[32,16,128]{2,1,0:T(8,128)S(1)}, u32[]{:S(2)}, u32[]{:S(2)}) collective-permute-start(f32[32,16,128]{2,1,0:T(8,128)} %refs_9_.1), channel_id=1, source_target_pairs={{0,8},{8,16},{16,24},{24,28},{28,20},{20,12},{12,4},{4,0},{1,9},{9... | collective-permute-start | bytes 786440 | tf_op jit(solution)/shard_map/ppermute | solution.py:425
  3.1 1.8 %shard_map.100 = (f32[128,512]{1,0:T(8,128)S(1)}, f32[128,512]{1,0:T(8,128)S(1)}, f32[128,512]{1,0:T(8,128)S(1)}, f32[128,512]{1,0:T(8,128)S(1)}) custom-call(f32[1,65,4,512]{3,2,1,0:T(4,128)} %bitcast.2, s32[3,2048]{1,0:T(4,128)} %refs_4_.2, bf16[4,128,512]{2,1,0:T(8,128)(2,1)} %constant.14.clone.table_hbm), custom_call_target="tpu_custom_call" | custom-call | flops 2147483648 | bytes 1048576 | tf_op jit(solution)/shard_map/pallas_call | solution.py:436
  5.0 2.0 %collective-permute-start.1 = (f32[128,512]{1,0:T(8,128)S(1)}, f32[128,512]{1,0:T(8,128)S(1)}, u32[]{:S(2)}, u32[]{:S(2)}) collective-permute-start(f32[128,512]{1,0:T(8,128)S(1)} %get-tuple-element.22), channel_id=1, source_target_pairs={{0,2},{1,3},{2,0},{3,1},{4,6},{5,7},{6,4},{7,5},{8,10},{9,11},{10,... | collective-permute-start | bytes 786440 | tf_op jit(solution)/shard_map/ppermute | solution.py:415
  7.0 2.5 %collective-permute-done.3.refs_1_ = f32[32,16,128]{2,1,0:T(8,128)S(1)} collective-permute-done((f32[32,16,128]{2,1,0:T(8,128)}, f32[32,16,128]{2,1,0:T(8,128)S(1)}, u32[]{:S(2)}, u32[]{:S(2)}) %collective-permute-start.3) | collective-permute-done | bytes 262176 | tf_op jit(solution)/shard_map/ppermute | solution.py:425
  9.5 1.8 %collective-permute-start.5 = (f32[32,16,128]{2,1,0:T(8,128)S(1)}, f32[32,16,128]{2,1,0:T(8,128)S(1)}, u32[]{:S(2)}, u32[]{:S(2)}) collective-permute-start(f32[32,16,128]{2,1,0:T(8,128)S(1)} %collective-permute-done.3.refs_1_), channel_id=1, source_target_pairs={{0,8},{8,16},{16,24},{24,28},{28,20},{20,12},{12,4},{4,0},{1,9},{9... | collective-permute-start | bytes 786440 | tf_op jit(solution)/shard_map/ppermute | solution.py:425
  11.5 1.6 %shard_map.101 = (f32[1088,256]{1,0:T(8,128)S(1)}, bf16[2,256,512]{2,1,0:T(8,128)(2,1)S(1)}, bf16[128,240]{1,0:T(8,128)(2,1)S(1)}, bf16[160,256]{1,0:T(8,128)(2,...) custom-call(f32[128,512]{1,0:T(8,128)S(1)} %get-tuple-element.23.ref, ...), custom_call_target="tpu_custom_call" | custom-call | flops 2147483648 | bytes 1048576 | tf_op jit(solution)/shard_map/pallas_call | solution.py:436
  13.1 1.1 %collective-permute-done.1.refs_0_ = f32[128,512]{1,0:T(8,128)S(1)} collective-permute-done((f32[128,512]{1,0:T(8,128)S(1)}, f32[128,512]{1,0:T(8,128)S(1)}, u32[]{:S(2)}, u32[]{:S(2)}) %collective-permute-start.1) | collective-permute-done | bytes 262176 | tf_op jit(solution)/shard_map/ppermute | solution.py:415
  14.2 0.8 %shard_map.102.refs_1_ = f32[1088,256]{1,0:T(8,128)S(1)} custom-call(f32[128,512]{1,0:T(8,128)S(1)} %collective-permute-done.1.refs_0_, f32[1088,256]{1,0:T(8,128)S(1)} %get-tuple-element.25.refs_1_, s32[3,2048]{1,0:T(4,128)S(1)} %copy-done), custom_call_target="tpu_custom_call" | custom-call | flops 2147483648 | bytes 1048576 | tf_op jit(solution)/shard_map/pallas_call | solution.py:436
  15.1 1.9 %collective-permute-done.5.refs_3_ = f32[32,16,128]{2,1,0:T(8,128)S(1)} collective-permute-done((f32[32,16,128]{2,1,0:T(8,128)S(1)}, f32[32,16,128]{2,1,0:T(8,128)S(1)}, u32[]{:S(2)}, u32[]{:S(2)}) %collective-permute-start.5) | collective-permute-done | bytes 262176 | tf_op jit(solution)/shard_map/ppermute | solution.py:425
  17.0 1.5 %collective-permute-start.7 = (f32[32,16,128]{2,1,0:T(8,128)S(1)}, f32[32,16,128]{2,1,0:T(8,128)S(1)}, u32[]{:S(2)}, u32[]{:S(2)}) collective-permute-start(f32[32,16,128]{2,1,0:T(8,128)S(1)} %collective-permute-done.5.refs_3_), channel_id=1, source_target_pairs={{0,8},{8,16},{16,24},{24,28},{28,20},{20,12},{12,4},{4,0},{1,9},{9... | collective-permute-start | bytes 786440 | tf_op jit(solution)/shard_map/ppermute | solution.py:425
  19.2 1.8 %shard_map.103.half_ref = f32[4,1560,128]{2,1,0:T(8,128)S(1)} custom-call(f32[128,512]{1,0:T(8,128)S(1)} %collective-permute-done.refs_0_, f32[1088,256]{1,0:T(8,128)S(1)} %shard_map.102.refs_1_, s32[3,2048]{1,0:T(4,128)S(1)} %copy-done, bf16[2,256,512]{2,1,0:T(8,128)(2,1)S(1)} %get-tuple-element.26.refs_3_), custom_call_target="tpu_custom_call" | custom-call | flops 2147483648 | bytes 1048576 | tf_op jit(solution)/shard_map/pallas_call | solution.py:436
  20.9 2.0 %shard_map.104.real_ref = f32[32,144,256]{2,1,0:T(8,128)S(1)} custom-call(f32[4,1560,128]{2,1,0:T(8,128)S(1)} %shard_map.103.half_ref, bf16[128,240]{1,0:T(8,128)(2,1)S(1)} %get-tuple-element.27.x_ahead_ref), custom_call_target="tpu_custom_call" | custom-call | flops 2147483648 | bytes 1048576 | tf_op jit(solution)/shard_map/pallas_call | solution.py:436
  22.9 2.0 %collective-permute-done.8.refs_6_ = f32[32,16,128]{2,1,0:T(8,128)S(1)} collective-permute-done((f32[32,16,128]{2,1,0:T(8,128)S(1)}, f32[32,16,128]{2,1,0:T(8,128)S(1)}, u32[]{:S(2)}, u32[]{:S(2)}) %collective-permute-start.8) | collective-permute-done | bytes 262176 | tf_op jit(solution)/shard_map/ppermute | solution.py:426
  25.5 1.6 %collective-permute-start.9 = (f32[16,16,128]{2,1,0:T(8,128)S(1)}, f32[16,16,128]{2,1,0:T(8,128)S(1)}, u32[]{:S(2)}, u32[]{:S(2)}) collective-permute-start(f32[16,16,128]{2,1,0:T(8,128)S(1)} %slice.12), channel_id=1, source_target_pairs={{0,8},{8,16},{16,24},{24,28},{28,20},{20,12},{12,4},{4,0},{1,9},{9... | collective-permute-start | bytes 393224 | tf_op jit(solution)/shard_map/ppermute | solution.py:425
  27.0 2.4 %shard_map.105.first_ref = f32[4,1560,128]{2,1,0:T(8,128)S(1)} custom-call(f32[32,144,256]{2,1,0:T(8,128)S(1)} %shard_map.104.real_ref, f32[32,16,128]{2,1,0:T(8,128)S(1)} %get-tuple-element.28.refs_0_, f32[32,16,128]{2,1,0:T(8,128)S(1)} %collective-permute-done.3.refs_1_, f32[32,16,128]{2,1,0:T(8,128)S(1)} %collective-permute-done.4.refs_2_, ...), custom_call_target="tpu_custom_call" | custom-call | flops 2147483648 | bytes 1048576 | tf_op jit(solution)/shard_map/pallas_call | solution.py:436
  29.4 1.1 %collective-permute-done.9.slab_ref = f32[16,16,128]{2,1,0:T(8,128)S(1)} collective-permute-done((f32[16,16,128]{2,1,0:T(8,128)S(1)}, f32[16,16,128]{2,1,0:T(8,128)S(1)}, u32[]{:S(2)}, u32[]{:S(2)}) %collective-permute-start.9) | collective-permute-done | bytes 131104 | tf_op jit(solution)/shard_map/ppermute | solution.py:425
  30.5 1.4 %shard_map.106.refs_0_ = bf16[128,2176]{1,0:T(8,128)(2,1)S(1)} custom-call(f32[4,1560,128]{2,1,0:T(8,128)S(1)} %shard_map.105.first_ref, f32[32,144,256]{2,1,0:T(8,128)S(1)} %shard_map.104.real_ref, f32[16,16,128]{2,1,0:T(8,128)S(1)} %collective-permute-done.9.slab_ref, bf16[8,80,48]{2,1,0:T(8,128)(2,1)S(1)} %get-tuple-element.30.x_last_ref, ...), custom_call_target="tpu_custom_call" | custom-call | flops 2147483648 | bytes 1048576 | tf_op jit(solution)/shard_map/pallas_call | solution.py:436
  32.6 1.5 %collective-permute-start.10 = (f32[128,512]{1,0:T(8,128)S(1)}, f32[128,512]{1,0:T(8,128)S(1)}, u32[]{:S(2)}, u32[]{:S(2)}) collective-permute-start(f32[128,512]{1,0:T(8,128)S(1)} %shard_map.107), channel_id=1, source_target_pairs={{0,2},{1,3},{2,0},{3,1},{4,6},{5,7},{6,4},{7,5},{8,10},{9,11},{10,... | collective-permute-start | bytes 786440 | tf_op jit(solution)/shard_map/ppermute | solution.py:536
  34.2 1.4 %shard_map.108.refs_0_.refs_1_ = bf16[128,2176]{1,0:T(8,128)(2,1)S(1)} custom-call(f32[4,1560,128]{2,1,0:T(8,128)S(1)} %shard_map.105.first_ref, f32[32,144,256]{2,1,0:T(8,128)S(1)} %shard_map.104.real_ref, f32[16,16,128]{2,1,0:T(8,128)S(1)} %collective-permute-done.12.slab_ref, bf16[8,80,48]{2,1,0:T(8,128)(2,1)S(1)} %get-tuple-element.30.x_last_ref, ...), custom_call_target="tpu_custom_call" | custom-call | flops 2147483648 | bytes 1048576 | tf_op jit(solution)/shard_map/pallas_call | solution.py:436
  35.5 1.4 %shard_map.110 = (f32[128,512]{1,0:T(8,128)S(1)}, f32[128,512]{1,0:T(8,128)S(1)}) custom-call(bf16[128,2176]{1,0:T(8,128)(2,1)S(1)} %shard_map.106.refs_0_, bf16[128,2176]{1,0:T(8,128)(2,1)S(1)} %shard_map.108.refs_0_.refs_1_, s32[3,2048]{1,0:T(4,128)S(1)} %copy-done), custom_call_target="tpu_custom_call" | custom-call | flops 2147483648 | bytes 1048576 | tf_op jit(solution)/shard_map/pallas_call | solution.py:436
  38.6 1.4 %collective-permute-start.14 = (f32[64,512]{1,0:T(8,128)S(1)}, f32[64,512]{1,0:T(8,128)S(1)}, u32[]{:S(2)}, u32[]{:S(2)}) collective-permute-start(f32[64,512]{1,0:T(8,128)S(1)} %get-tuple-element.33), channel_id=1, source_target_pairs={{0,2},{1,3},{2,0},{3,1},{4,6},{5,7},{6,4},{7,5},{8,10},{9,11},{10,... | collective-permute-start | bytes 393224 | tf_op jit(solution)/shard_map/ppermute | solution.py:536
  40.7 2.3 %collective-permute-done.13.refs_1_ = f32[64,512]{1,0:T(8,128)S(1)} collective-permute-done((f32[64,512]{1,0:T(8,128)S(1)}, f32[64,512]{1,0:T(8,128)S(1)}, u32[]{:S(2)}, u32[]{:S(2)}) %collective-permute-start.13) | collective-permute-done | bytes 131104 | tf_op jit(solution)/shard_map/ppermute | solution.py:536
  43.0 3.5 %collective-permute-done.14.refs_2_ = f32[64,512]{1,0:T(8,128)S(1)} collective-permute-done((f32[64,512]{1,0:T(8,128)S(1)}, f32[64,512]{1,0:T(8,128)S(1)}, u32[]{:S(2)}, u32[]{:S(2)}) %collective-permute-start.14) | collective-permute-done | bytes 131104 | tf_op jit(solution)/shard_map/ppermute | solution.py:536
  46.5 1.2 %shard_map.112 = f32[1,65,4,512]{3,2,1,0:T(4,128)} custom-call(f32[64,512]{1,0:T(8,128)S(1)} %collective-permute-done.11.refs_0_, f32[64,512]{1,0:T(8,128)S(1)} %collective-permute-done.13.refs_1_, f32[64,512]{1,0:T(8,128)S(1)} %collective-permute-done.14.refs_2_, f32[256,512]{1,0:T(8,128)S(1)} %shard_map.111.refs_3_, s32[3,2048]{1,0:T(4,128)S(1)} %copy-done, ...), custom_call_target="tpu_custom_call" | custom-call | flops 2147483648 | bytes 1048576 | tf_op jit(solution)/shard_map/pallas_call | solution.py:436
  (26 shorter events, 4.6 us)
Async XLA Ops:
  0.0 9.5 %collective-permute-start.3 = (f32[32,16,128]{2,1,0:T(8,128)}, f32[32,16,128]{2,1,0:T(8,128)S(1)}, u32[]{:S(2)}, u32[]{:S(2)}) collective-permute-start(f32[32,16,128]{2,1,0:T(8,128)} %refs_9_.1), channel_id=1, source_target_pairs={{0,8},{8,16},{16,24},{24,28},{28,20},{20,12},{12,4},{4,0},{1,9},{9... | collective-permute-start | bytes 786440 | tf_op jit(solution)/shard_map/ppermute | solution.py:425
  3.1 8.3 %collective-permute-start.4 = (f32[32,16,128]{2,1,0:T(8,128)}, f32[32,16,128]{2,1,0:T(8,128)S(1)}, u32[]{:S(2)}, u32[]{:S(2)}) collective-permute-start(f32[32,16,128]{2,1,0:T(8,128)} %refs_9_.1), channel_id=1, source_target_pairs={{8,0},{16,8},{24,16},{28,24},{20,28},{12,20},{4,12},{0,4},{9,1},{1... | collective-permute-start | bytes 786440 | tf_op jit(solution)/shard_map/ppermute | solution.py:426
  3.1 8.5 %copy-start = (s32[3,2048]{1,0:T(4,128)S(1)}, s32[3,2048]{1,0:T(4,128)}, u32[]{:S(2)}) copy-start(s32[3,2048]{1,0:T(4,128)} %refs_4_.2) | copy-start | bytes 73732
  4.9 6.6 %collective-permute-start.2 = (f32[128,512]{1,0:T(8,128)S(1)}, f32[128,512]{1,0:T(8,128)S(1)}, u32[]{:S(2)}, u32[]{:S(2)}) collective-permute-start(f32[128,512]{1,0:T(8,128)S(1)} %get-tuple-element.24), channel_id=1, source_target_pairs={{0,1},{1,0},{2,3},{3,2},{4,5},{5,4},{6,7},{7,6},{8,9},{9,8},{10,11... | collective-permute-start | bytes 786440 | tf_op jit(solution)/shard_map/ppermute | solution.py:415
  5.0 9.2 %collective-permute-start.1 = (f32[128,512]{1,0:T(8,128)S(1)}, f32[128,512]{1,0:T(8,128)S(1)}, u32[]{:S(2)}, u32[]{:S(2)}) collective-permute-start(f32[128,512]{1,0:T(8,128)S(1)} %get-tuple-element.22), channel_id=1, source_target_pairs={{0,2},{1,3},{2,0},{3,1},{4,6},{5,7},{6,4},{7,5},{8,10},{9,11},{10,... | collective-permute-start | bytes 786440 | tf_op jit(solution)/shard_map/ppermute | solution.py:415
  7.0 12.2 %collective-permute-start = (f32[128,512]{1,0:T(8,128)S(1)}, f32[128,512]{1,0:T(8,128)S(1)}, u32[]{:S(2)}, u32[]{:S(2)}) collective-permute-start(f32[128,512]{1,0:T(8,128)S(1)} %get-tuple-element.21), channel_id=1, source_target_pairs={{0,3},{1,2},{2,1},{3,0},{4,7},{5,6},{6,5},{7,4},{8,11},{9,10},{10,... | collective-permute-start | bytes 786440 | tf_op jit(solution)/shard_map/ppermute | solution.py:415
  9.5 7.5 %collective-permute-start.5 = (f32[32,16,128]{2,1,0:T(8,128)S(1)}, f32[32,16,128]{2,1,0:T(8,128)S(1)}, u32[]{:S(2)}, u32[]{:S(2)}) collective-permute-start(f32[32,16,128]{2,1,0:T(8,128)S(1)} %collective-permute-done.3.refs_1_), channel_id=1, source_target_pairs={{0,8},{8,16},{16,24},{24,28},{28,20},{20,12},{12,4},{4,0},{1,9},{9... | collective-permute-start | bytes 786440 | tf_op jit(solution)/shard_map/ppermute | solution.py:425
  11.3 7.2 %collective-permute-start.6 = (f32[32,16,128]{2,1,0:T(8,128)S(1)}, f32[32,16,128]{2,1,0:T(8,128)S(1)}, u32[]{:S(2)}, u32[]{:S(2)}) collective-permute-start(f32[32,16,128]{2,1,0:T(8,128)S(1)} %collective-permute-done.4.refs_2_), channel_id=1, source_target_pairs={{8,0},{16,8},{24,16},{28,24},{20,28},{12,20},{4,12},{0,4},{9,1},{1... | collective-permute-start | bytes 786440 | tf_op jit(solution)/shard_map/ppermute | solution.py:426
  17.0 8.5 %collective-permute-start.7 = (f32[32,16,128]{2,1,0:T(8,128)S(1)}, f32[32,16,128]{2,1,0:T(8,128)S(1)}, u32[]{:S(2)}, u32[]{:S(2)}) collective-permute-start(f32[32,16,128]{2,1,0:T(8,128)S(1)} %collective-permute-done.5.refs_3_), channel_id=1, source_target_pairs={{0,8},{8,16},{16,24},{24,28},{28,20},{20,12},{12,4},{4,0},{1,9},{9... | collective-permute-start | bytes 786440 | tf_op jit(solution)/shard_map/ppermute | solution.py:425
  18.5 6.4 %collective-permute-start.8 = (f32[32,16,128]{2,1,0:T(8,128)S(1)}, f32[32,16,128]{2,1,0:T(8,128)S(1)}, u32[]{:S(2)}, u32[]{:S(2)}) collective-permute-start(f32[32,16,128]{2,1,0:T(8,128)S(1)} %collective-permute-done.6.refs_4_), channel_id=1, source_target_pairs={{8,0},{16,8},{24,16},{28,24},{20,28},{12,20},{4,12},{0,4},{9,1},{1... | collective-permute-start | bytes 786440 | tf_op jit(solution)/shard_map/ppermute | solution.py:426
  24.9 9.3 %collective-permute-start.12 = (f32[16,16,128]{2,1,0:T(8,128)S(1)}, f32[16,16,128]{2,1,0:T(8,128)S(1)}, u32[]{:S(2)}, u32[]{:S(2)}) collective-permute-start(f32[16,16,128]{2,1,0:T(8,128)S(1)} %slice.14), channel_id=1, source_target_pairs={{8,0},{16,8},{24,16},{28,24},{20,28},{12,20},{4,12},{0,4},{9,1},{1... | collective-permute-start | bytes 393224 | tf_op jit(solution)/shard_map/ppermute | solution.py:426
  25.5 5.0 %collective-permute-start.9 = (f32[16,16,128]{2,1,0:T(8,128)S(1)}, f32[16,16,128]{2,1,0:T(8,128)S(1)}, u32[]{:S(2)}, u32[]{:S(2)}) collective-permute-start(f32[16,16,128]{2,1,0:T(8,128)S(1)} %slice.12), channel_id=1, source_target_pairs={{0,8},{8,16},{16,24},{24,28},{28,20},{20,12},{12,4},{4,0},{1,9},{9... | collective-permute-start | bytes 393224 | tf_op jit(solution)/shard_map/ppermute | solution.py:425
  32.6 7.4 %collective-permute-start.10 = (f32[128,512]{1,0:T(8,128)S(1)}, f32[128,512]{1,0:T(8,128)S(1)}, u32[]{:S(2)}, u32[]{:S(2)}) collective-permute-start(f32[128,512]{1,0:T(8,128)S(1)} %shard_map.107), channel_id=1, source_target_pairs={{0,2},{1,3},{2,0},{3,1},{4,6},{5,7},{6,4},{7,5},{8,10},{9,11},{10,... | collective-permute-start | bytes 786440 | tf_op jit(solution)/shard_map/ppermute | solution.py:536
  36.9 3.2 %collective-permute-start.15 = (f32[128,512]{1,0:T(8,128)S(1)}, f32[128,512]{1,0:T(8,128)S(1)}, u32[]{:S(2)}, u32[]{:S(2)}) collective-permute-start(f32[128,512]{1,0:T(8,128)S(1)} %get-tuple-element.34), channel_id=1, source_target_pairs={{0,1},{1,0},{2,3},{3,2},{4,5},{5,4},{6,7},{7,6},{8,9},{9,8},{10,11... | collective-permute-start | bytes 786440 | tf_op jit(solution)/shard_map/ppermute | solution.py:536
  37.8 5.2 %collective-permute-start.13 = (f32[64,512]{1,0:T(8,128)S(1)}, f32[64,512]{1,0:T(8,128)S(1)}, u32[]{:S(2)}, u32[]{:S(2)}) collective-permute-start(f32[64,512]{1,0:T(8,128)S(1)} %get-tuple-element.32), channel_id=1, source_target_pairs={{0,3},{1,2},{2,1},{3,0},{4,7},{5,6},{6,5},{7,4},{8,11},{9,10},{10,... | collective-permute-start | bytes 393224 | tf_op jit(solution)/shard_map/ppermute | solution.py:536
  38.6 7.9 %collective-permute-start.14 = (f32[64,512]{1,0:T(8,128)S(1)}, f32[64,512]{1,0:T(8,128)S(1)}, u32[]{:S(2)}, u32[]{:S(2)}) collective-permute-start(f32[64,512]{1,0:T(8,128)S(1)} %get-tuple-element.33), channel_id=1, source_target_pairs={{0,2},{1,3},{2,0},{3,1},{4,6},{5,7},{6,4},{7,5},{8,10},{9,11},{10,... | collective-permute-start | bytes 393224 | tf_op jit(solution)/shard_map/ppermute | solution.py:536
  40.0 6.5 %collective-permute-start.11 = (f32[64,512]{1,0:T(8,128)S(1)}, f32[64,512]{1,0:T(8,128)S(1)}, u32[]{:S(2)}, u32[]{:S(2)}) collective-permute-start(f32[64,512]{1,0:T(8,128)S(1)} %slice.13), channel_id=1, source_target_pairs={{0,1},{1,0},{2,3},{3,2},{4,5},{5,4},{6,7},{7,6},{8,9},{9,8},{10,11... | collective-permute-start | bytes 393224 | tf_op jit(solution)/shard_map/ppermute | solution.py:536

commit v7 on v6

--- a/solution.py
+++ b/solution.py
@@ -79,19 +79,8 @@
     back = np.pad(back.reshape(s.devices, 4 * s.depths, 2 * s.batch), ((0, 0), (0, gap), (0, 0)))
 
     cos, sin = trig(y, grid)
-    y_ahead = np.zeros((2, 2, s.rows_y, 2, 2, s.length))
-    y_back = np.zeros((2, 2, s.length, 2, 2, s.rows_y))
-    for parity in range(2):
-        y_ahead[0, parity, :, parity, 0] = cos
-        y_ahead[1, parity, :, parity, 0] = -sin
-        y_ahead[0, parity, :, parity, 1] = sin
-        y_ahead[1, parity, :, parity, 1] = cos
-        y_back[parity, 0, :, 0, parity] = cos.T
-        y_back[parity, 1, :, 0, parity] = sin.T
-        y_back[parity, 0, :, 1, parity] = -sin.T
-        y_back[parity, 1, :, 1, parity] = cos.T
-    y_ahead = y_ahead.reshape(4 * s.rows_y, 4 * s.length)
-    y_back = y_back.reshape(4 * s.length, 4 * s.rows_y)
+    y_ahead = np.stack([np.stack([cos, sin], 1), np.stack([-sin, cos], 1)]).reshape(2 * s.rows_y, 2 * s.length)
+    y_back = np.stack([np.stack([cos.T, -sin.T], 1), np.stack([sin.T, cos.T], 1)]).reshape(2 * s.length, 2 * s.rows_y)
 
     x_ahead = np.zeros((s.length, s.kept))
     x_back = np.zeros((s.kept, s.length))
@@ -108,18 +97,28 @@
         parts = halves(table)
         return np.concatenate([parts[i] for i in order], axis)
 
-    zero = np.zeros(x_back.shape, ml_dtypes.bfloat16)
-    high, low = halves(x_back)
+    def folded(table, axis):
+        high, low = halves(table)
+        zero = np.zeros(table.shape, ml_dtypes.bfloat16)
+        first, second = (high, high), (low, zero)
+        return np.concatenate([np.concatenate(first, 1 - axis), np.concatenate(second, 1 - axis)], axis)
+
     by_slab = x_back.reshape(s.kept, bands, s.length // bands).transpose(1, 0, 2)
     return dict(
         z_ahead=beside(ahead, 2, (0, 1)),
         z_back=beside(back, 2, (0, 1)),
         y_ahead=np.stack(halves(y_ahead)),
-        y_back=np.stack(halves(y_back)),
+        y_back=folded(y_back, 1),
         x_ahead=beside(x_ahead, 1, (0, 1, 0)),
         x_last=beside(by_slab, 2, (0, 0, 1)),
-        x_back=np.concatenate([np.concatenate([high, high], 1), np.concatenate([low, zero], 1)], 0),
+        x_back=folded(x_back, 0),
     )
+
+
+def braid(left, right):
+    half = left.shape[1] // 2
+    first = lax.broadcasted_iota(jnp.int32, left.shape, 1) < half
+    return jnp.where(first, left, pltpu.roll(right, half, 1)), jnp.where(first, pltpu.roll(left, half, 1), right)
 
 
 def dot(left, right):
@@ -239,12 +238,15 @@
     table = jnp.concatenate([table_ref[0], table_ref[0], table_ref[1]], 0)
     for start in range(0, total, 4 * s.batch):
         end = min(total, start + 4 * s.batch)
-        high, low = split(grid_ref[start:end, :])
+        sides = braid(grid_ref[start:end, :lanes], grid_ref[start:end, lanes:])
+        high, low = split(jnp.concatenate(sides, 0))
         moved = dot(jnp.concatenate([high, low, high], 1), table)
         for t in range(4):
             for row in range(0, end - start, s.batch):
                 at = (start + row) // s.batch * s.step
-                out_ref[t, at : at + s.batch, :] = moved[row : row + s.batch, t * s.length : (t + 1) * s.length]
+                own = t // 2 * (end - start) + row
+                part = moved[own : own + s.batch, t % 2 * s.length : (t % 2 + 1) * s.length]
+                out_ref[t, at : at + s.batch, :] = part
     for t in range(4):
         out_ref[t, s.tiles * s.step :, :] = jnp.zeros(((s.even - s.tiles) * s.step, s.length), f32)
 
@@ -326,24 +328,27 @@
     lax.fori_loop(0, part, plane, 0, unroll=4)
 
     lanes = 2 * s.rows_y
-    table = jnp.concatenate([y_back_ref[0], y_back_ref[0], y_back_ref[1]], 0)
     for start in range(0, s.tiles, 8):
         end = min(s.tiles, start + 8)
         parts = []
-        for tile in range(start, end):
-            for o in range(2):
-                row = tile * s.step + o * s.planes + half * part
-                own = slice(row, row + part)
-                parts.append(jnp.concatenate([first_ref[t, own, :] + turned_ref[t, own, :] for t in range(4)], 1))
+        for parity in range(2):
+            for tile in range(start, end):
+                for o in range(2):
+                    row = tile * s.step + o * s.planes + half * part
+                    own = slice(row, row + part)
+                    both = [first_ref[t, own, :] + turned_ref[t, own, :] for t in (2 * parity, 2 * parity + 1)]
+                    parts.append(jnp.concatenate(both, 1))
         high, low = split(jnp.concatenate(parts, 0))
-        moved = dot(jnp.concatenate([high, low, high], 1), table)
-        high, low = split(moved)
-        for tile in range(start, end):
-            at = (tile - start) * s.planes
-            for component in range(2):
-                mine = slice(at, at + s.planes), slice(component * lanes, (component + 1) * lanes)
-                for row, value in ((component, high), (2 + component, low)):
-                    flat_ref[row * s.planes : (row + 1) * s.planes, tile * lanes : (tile + 1) * lanes] = value[mine]
+        moved = dot(jnp.concatenate([high, low], 1), y_back_ref[...])
+        moved = moved[:, :lanes] + moved[:, lanes:]
+        count = (end - start) * s.planes
+        for component, value in enumerate(braid(moved[:count], moved[count:])):
+            for row, piece in zip((component, 2 + component), split(value), strict=True):
+                for tile in range(start, end):
+                    at = (tile - start) * s.planes
+                    flat_ref[row * s.planes : (row + 1) * s.planes, tile * lanes : (tile + 1) * lanes] = piece[
+                        at : at + s.planes
+                    ]
 
 
 def pick_kernel(s, which, count, joined, *refs):

time: 47.9 us -> 47.7 us (level)
  Pallas kernels: 17.9 us -> 17.3 us
    pallas_call x13, Pallas kernels: 17.9 us -> 17.3 us  [kernel(): pl.pallas_call(body, in_specs=[place] * len(inputs) + [HBM] * len(fetched...]
  transfers between devices with their start and end apart: 16 -> 16, of which waited for: 8 -> 8; matrix products, arithmetic and copies ran while one was open for 0% -> 0% of each run, Pallas kernels for 35% -> 34%
where the time goes in v7:
time: 47.7 us; the launch traced here: 47.5 us
  Pallas kernels  17.3 us (36%)
  starting transfers between devices  15.2 us (32%)
  waiting for transfers between devices  14.9 us (31%)
    pallas_call x13, Pallas kernels, kernel(): pl.pallas_call(body, in_specs=[place] * len(inputs) + [HBM] * len(fetched...  17.3 us
    ppermute x4, starting transfers between devices, ring(): up = lax.ppermute(up, 'band', along)  7.94 us
    ppermute x5, waiting for transfers between devices, send(): return lax.ppermute(block, 'plane', [(i, i ^ k) for i in range(devices)])  5.81 us
    ppermute x4, waiting for transfers between devices, ring(): up = lax.ppermute(up, 'band', along)  5.47 us
    ppermute x5, starting transfers between devices, send(): return lax.ppermute(block, 'plane', [(i, i ^ k) for i in range(devices)])  3.84 us
    ppermute x4, waiting for transfers between devices, ring(): down = lax.ppermute(down, 'band', against)  2.27 us
    ppermute x3, starting transfers between devices, exchange(): lax.ppermute(blocks[k], 'plane', [(i, i ^ k) for i in range(devices)])  2.11 us
    ppermute x3, waiting for transfers between devices, exchange(): lax.ppermute(blocks[k], 'plane', [(i, i ^ k) for i in range(devices)])  1.3 us
  transfers between devices with their start and end apart: 16, of which 8 were waited for; matrix products, arithmetic and copies ran while one was open for 0% of the time, Pallas kernels for 34%

profile of v7, /device:TPU:0, one launch (start us, length us, event | category | flops | bytes accessed | tf_op | source)
XLA Modules:
  0.0 47.5 jit_solution(10935448657964453379)
XLA Ops:
  0.0 3.1 %collective-permute-start.3 = (f32[32,16,128]{2,1,0:T(8,128)}, f32[32,16,128]{2,1,0:T(8,128)S(1)}, u32[]{:S(2)}, u32[]{:S(2)}) collective-permute-start(f32[32,16,128]{2,1,0:T(8,128)} %refs_9_.1), channel_id=1, source_target_pairs={{0,8},{8,16},{16,24},{24,28},{28,20},{20,12},{12,4},{4,0},{1,9},{9... | collective-permute-start | bytes 786440 | tf_op jit(solution)/shard_map/ppermute | solution.py:430
  3.1 1.8 %shard_map.100 = (f32[128,512]{1,0:T(8,128)S(1)}, f32[128,512]{1,0:T(8,128)S(1)}, f32[128,512]{1,0:T(8,128)S(1)}, f32[128,512]{1,0:T(8,128)S(1)}) custom-call(f32[1,65,4,512]{3,2,1,0:T(4,128)} %bitcast.2, s32[3,2048]{1,0:T(4,128)} %refs_4_.2, bf16[4,128,512]{2,1,0:T(8,128)(2,1)} %constant.14.clone.table_hbm), custom_call_target="tpu_custom_call" | custom-call | flops 2147483648 | bytes 1048576 | tf_op jit(solution)/shard_map/pallas_call | solution.py:441
  5.0 2.0 %collective-permute-start.1 = (f32[128,512]{1,0:T(8,128)S(1)}, f32[128,512]{1,0:T(8,128)S(1)}, u32[]{:S(2)}, u32[]{:S(2)}) collective-permute-start(f32[128,512]{1,0:T(8,128)S(1)} %get-tuple-element.22), channel_id=1, source_target_pairs={{0,2},{1,3},{2,0},{3,1},{4,6},{5,7},{6,4},{7,5},{8,10},{9,11},{10,... | collective-permute-start | bytes 786440 | tf_op jit(solution)/shard_map/ppermute | solution.py:420
  7.0 2.5 %collective-permute-done.3.refs_1_ = f32[32,16,128]{2,1,0:T(8,128)S(1)} collective-permute-done((f32[32,16,128]{2,1,0:T(8,128)}, f32[32,16,128]{2,1,0:T(8,128)S(1)}, u32[]{:S(2)}, u32[]{:S(2)}) %collective-permute-start.3) | collective-permute-done | bytes 262176 | tf_op jit(solution)/shard_map/ppermute | solution.py:430
  9.5 1.8 %collective-permute-start.5 = (f32[32,16,128]{2,1,0:T(8,128)S(1)}, f32[32,16,128]{2,1,0:T(8,128)S(1)}, u32[]{:S(2)}, u32[]{:S(2)}) collective-permute-start(f32[32,16,128]{2,1,0:T(8,128)S(1)} %collective-permute-done.3.refs_1_), channel_id=1, source_target_pairs={{0,8},{8,16},{16,24},{24,28},{28,20},{20,12},{12,4},{4,0},{1,9},{9... | collective-permute-start | bytes 786440 | tf_op jit(solution)/shard_map/ppermute | solution.py:430
  11.5 1.5 %shard_map.101 = (f32[1088,256]{1,0:T(8,128)S(1)}, bf16[2,128,256]{2,1,0:T(8,128)(2,1)S(1)}, bf16[128,240]{1,0:T(8,128)(2,1)S(1)}, bf16[160,256]{1,0:T(8,128)(2,...) custom-call(f32[128,512]{1,0:T(8,128)S(1)} %get-tuple-element.23.ref, ...), custom_call_target="tpu_custom_call" | custom-call | flops 2147483648 | bytes 1048576 | tf_op jit(solution)/shard_map/pallas_call | solution.py:441
  13.1 1.2 %collective-permute-done.1.refs_0_ = f32[128,512]{1,0:T(8,128)S(1)} collective-permute-done((f32[128,512]{1,0:T(8,128)S(1)}, f32[128,512]{1,0:T(8,128)S(1)}, u32[]{:S(2)}, u32[]{:S(2)}) %collective-permute-start.1) | collective-permute-done | bytes 262176 | tf_op jit(solution)/shard_map/ppermute | solution.py:420
  14.2 0.8 %shard_map.102.refs_1_ = f32[1088,256]{1,0:T(8,128)S(1)} custom-call(f32[128,512]{1,0:T(8,128)S(1)} %collective-permute-done.1.refs_0_, f32[1088,256]{1,0:T(8,128)S(1)} %get-tuple-element.25.refs_1_, s32[3,2048]{1,0:T(4,128)S(1)} %copy-done), custom_call_target="tpu_custom_call" | custom-call | flops 2147483648 | bytes 1048576 | tf_op jit(solution)/shard_map/pallas_call | solution.py:441
  15.1 1.9 %collective-permute-done.5.refs_3_ = f32[32,16,128]{2,1,0:T(8,128)S(1)} collective-permute-done((f32[32,16,128]{2,1,0:T(8,128)S(1)}, f32[32,16,128]{2,1,0:T(8,128)S(1)}, u32[]{:S(2)}, u32[]{:S(2)}) %collective-permute-start.5) | collective-permute-done | bytes 262176 | tf_op jit(solution)/shard_map/ppermute | solution.py:430
  17.0 1.5 %collective-permute-start.7 = (f32[32,16,128]{2,1,0:T(8,128)S(1)}, f32[32,16,128]{2,1,0:T(8,128)S(1)}, u32[]{:S(2)}, u32[]{:S(2)}) collective-permute-start(f32[32,16,128]{2,1,0:T(8,128)S(1)} %collective-permute-done.5.refs_3_), channel_id=1, source_target_pairs={{0,8},{8,16},{16,24},{24,28},{28,20},{20,12},{12,4},{4,0},{1,9},{9... | collective-permute-start | bytes 786440 | tf_op jit(solution)/shard_map/ppermute | solution.py:430
  19.2 1.5 %shard_map.103.half_ref = f32[4,1560,128]{2,1,0:T(8,128)S(1)} custom-call(f32[128,512]{1,0:T(8,128)S(1)} %collective-permute-done.refs_0_, f32[1088,256]{1,0:T(8,128)S(1)} %shard_map.102.refs_1_, s32[3,2048]{1,0:T(4,128)S(1)} %copy-done, bf16[2,128,256]{2,1,0:T(8,128)(2,1)S(1)} %get-tuple-element.26.refs_3_), custom_call_target="tpu_custom_call" | custom-call | flops 2147483648 | bytes 1048576 | tf_op jit(solution)/shard_map/pallas_call | solution.py:441
  20.6 2.0 %shard_map.104.real_ref = f32[32,144,256]{2,1,0:T(8,128)S(1)} custom-call(f32[4,1560,128]{2,1,0:T(8,128)S(1)} %shard_map.103.half_ref, bf16[128,240]{1,0:T(8,128)(2,1)S(1)} %get-tuple-element.27.x_ahead_ref), custom_call_target="tpu_custom_call" | custom-call | flops 2147483648 | bytes 1048576 | tf_op jit(solution)/shard_map/pallas_call | solution.py:441
  22.6 2.3 %collective-permute-done.8.refs_6_ = f32[32,16,128]{2,1,0:T(8,128)S(1)} collective-permute-done((f32[32,16,128]{2,1,0:T(8,128)S(1)}, f32[32,16,128]{2,1,0:T(8,128)S(1)}, u32[]{:S(2)}, u32[]{:S(2)}) %collective-permute-start.8) | collective-permute-done | bytes 262176 | tf_op jit(solution)/shard_map/ppermute | solution.py:431
  25.5 1.6 %collective-permute-start.9 = (f32[16,16,128]{2,1,0:T(8,128)S(1)}, f32[16,16,128]{2,1,0:T(8,128)S(1)}, u32[]{:S(2)}, u32[]{:S(2)}) collective-permute-start(f32[16,16,128]{2,1,0:T(8,128)S(1)} %slice.12), channel_id=1, source_target_pairs={{0,8},{8,16},{16,24},{24,28},{28,20},{20,12},{12,4},{4,0},{1,9},{9... | collective-permute-start | bytes 393224 | tf_op jit(solution)/shard_map/ppermute | solution.py:430
  27.0 2.4 %shard_map.105.first_ref = f32[4,1560,128]{2,1,0:T(8,128)S(1)} custom-call(f32[32,144,256]{2,1,0:T(8,128)S(1)} %shard_map.104.real_ref, f32[32,16,128]{2,1,0:T(8,128)S(1)} %get-tuple-element.28.refs_0_, f32[32,16,128]{2,1,0:T(8,128)S(1)} %collective-permute-done.3.refs_1_, f32[32,16,128]{2,1,0:T(8,128)S(1)} %collective-permute-done.4.refs_2_, ...), custom_call_target="tpu_custom_call" | custom-call | flops 2147483648 | bytes 1048576 | tf_op jit(solution)/shard_map/pallas_call | solution.py:441
  29.4 1.1 %collective-permute-done.9.slab_ref = f32[16,16,128]{2,1,0:T(8,128)S(1)} collective-permute-done((f32[16,16,128]{2,1,0:T(8,128)S(1)}, f32[16,16,128]{2,1,0:T(8,128)S(1)}, u32[]{:S(2)}, u32[]{:S(2)}) %collective-permute-start.9) | collective-permute-done | bytes 131104 | tf_op jit(solution)/shard_map/ppermute | solution.py:430
  30.5 1.2 %shard_map.106.refs_0_ = bf16[128,2176]{1,0:T(8,128)(2,1)S(1)} custom-call(f32[4,1560,128]{2,1,0:T(8,128)S(1)} %shard_map.105.first_ref, f32[32,144,256]{2,1,0:T(8,128)S(1)} %shard_map.104.real_ref, f32[16,16,128]{2,1,0:T(8,128)S(1)} %collective-permute-done.9.slab_ref, bf16[8,80,48]{2,1,0:T(8,128)(2,1)S(1)} %get-tuple-element.30.x_last_ref, ...), custom_call_target="tpu_custom_call" | custom-call | flops 2147483648 | bytes 1048576 | tf_op jit(solution)/shard_map/pallas_call | solution.py:441
  32.5 1.5 %collective-permute-start.10 = (f32[128,512]{1,0:T(8,128)S(1)}, f32[128,512]{1,0:T(8,128)S(1)}, u32[]{:S(2)}, u32[]{:S(2)}) collective-permute-start(f32[128,512]{1,0:T(8,128)S(1)} %shard_map.107), channel_id=1, source_target_pairs={{0,2},{1,3},{2,0},{3,1},{4,6},{5,7},{6,4},{7,5},{8,10},{9,11},{10,... | collective-permute-start | bytes 786440 | tf_op jit(solution)/shard_map/ppermute | solution.py:541
  34.1 1.3 %shard_map.108.refs_0_.refs_1_ = bf16[128,2176]{1,0:T(8,128)(2,1)S(1)} custom-call(f32[4,1560,128]{2,1,0:T(8,128)S(1)} %shard_map.105.first_ref, f32[32,144,256]{2,1,0:T(8,128)S(1)} %shard_map.104.real_ref, f32[16,16,128]{2,1,0:T(8,128)S(1)} %collective-permute-done.12.slab_ref, bf16[8,80,48]{2,1,0:T(8,128)(2,1)S(1)} %get-tuple-element.30.x_last_ref, ...), custom_call_target="tpu_custom_call" | custom-call | flops 2147483648 | bytes 1048576 | tf_op jit(solution)/shard_map/pallas_call | solution.py:441
  35.3 1.4 %shard_map.110 = (f32[128,512]{1,0:T(8,128)S(1)}, f32[128,512]{1,0:T(8,128)S(1)}) custom-call(bf16[128,2176]{1,0:T(8,128)(2,1)S(1)} %shard_map.106.refs_0_, bf16[128,2176]{1,0:T(8,128)(2,1)S(1)} %shard_map.108.refs_0_.refs_1_, s32[3,2048]{1,0:T(4,128)S(1)} %copy-done), custom_call_target="tpu_custom_call" | custom-call | flops 2147483648 | bytes 1048576 | tf_op jit(solution)/shard_map/pallas_call | solution.py:441
  38.3 1.4 %collective-permute-start.14 = (f32[64,512]{1,0:T(8,128)S(1)}, f32[64,512]{1,0:T(8,128)S(1)}, u32[]{:S(2)}, u32[]{:S(2)}) collective-permute-start(f32[64,512]{1,0:T(8,128)S(1)} %get-tuple-element.33), channel_id=1, source_target_pairs={{0,2},{1,3},{2,0},{3,1},{4,6},{5,7},{6,4},{7,5},{8,10},{9,11},{10,... | collective-permute-start | bytes 393224 | tf_op jit(solution)/shard_map/ppermute | solution.py:541
  40.5 2.3 %collective-permute-done.13.refs_1_ = f32[64,512]{1,0:T(8,128)S(1)} collective-permute-done((f32[64,512]{1,0:T(8,128)S(1)}, f32[64,512]{1,0:T(8,128)S(1)}, u32[]{:S(2)}, u32[]{:S(2)}) %collective-permute-start.13) | collective-permute-done | bytes 131104 | tf_op jit(solution)/shard_map/ppermute | solution.py:541
  42.8 3.5 %collective-permute-done.14.refs_2_ = f32[64,512]{1,0:T(8,128)S(1)} collective-permute-done((f32[64,512]{1,0:T(8,128)S(1)}, f32[64,512]{1,0:T(8,128)S(1)}, u32[]{:S(2)}, u32[]{:S(2)}) %collective-permute-start.14) | collective-permute-done | bytes 131104 | tf_op jit(solution)/shard_map/ppermute | solution.py:541
  46.3 1.2 %shard_map.112 = f32[1,65,4,512]{3,2,1,0:T(4,128)} custom-call(f32[64,512]{1,0:T(8,128)S(1)} %collective-permute-done.11.refs_0_, f32[64,512]{1,0:T(8,128)S(1)} %collective-permute-done.13.refs_1_, f32[64,512]{1,0:T(8,128)S(1)} %collective-permute-done.14.refs_2_, f32[256,512]{1,0:T(8,128)S(1)} %shard_map.111.refs_3_, s32[3,2048]{1,0:T(4,128)S(1)} %copy-done, ...), custom_call_target="tpu_custom_call" | custom-call | flops 2147483648 | bytes 1048576 | tf_op jit(solution)/shard_map/pallas_call | solution.py:441
  (26 shorter events, 4.6 us)
Async XLA Ops:
  0.0 9.5 %collective-permute-start.3 = (f32[32,16,128]{2,1,0:T(8,128)}, f32[32,16,128]{2,1,0:T(8,128)S(1)}, u32[]{:S(2)}, u32[]{:S(2)}) collective-permute-start(f32[32,16,128]{2,1,0:T(8,128)} %refs_9_.1), channel_id=1, source_target_pairs={{0,8},{8,16},{16,24},{24,28},{28,20},{20,12},{12,4},{4,0},{1,9},{9... | collective-permute-start | bytes 786440 | tf_op jit(solution)/shard_map/ppermute | solution.py:430
  3.1 8.3 %collective-permute-start.4 = (f32[32,16,128]{2,1,0:T(8,128)}, f32[32,16,128]{2,1,0:T(8,128)S(1)}, u32[]{:S(2)}, u32[]{:S(2)}) collective-permute-start(f32[32,16,128]{2,1,0:T(8,128)} %refs_9_.1), channel_id=1, source_target_pairs={{8,0},{16,8},{24,16},{28,24},{20,28},{12,20},{4,12},{0,4},{9,1},{1... | collective-permute-start | bytes 786440 | tf_op jit(solution)/shard_map/ppermute | solution.py:431
  3.1 8.5 %copy-start = (s32[3,2048]{1,0:T(4,128)S(1)}, s32[3,2048]{1,0:T(4,128)}, u32[]{:S(2)}) copy-start(s32[3,2048]{1,0:T(4,128)} %refs_4_.2) | copy-start | bytes 73732
  4.9 6.6 %collective-permute-start.2 = (f32[128,512]{1,0:T(8,128)S(1)}, f32[128,512]{1,0:T(8,128)S(1)}, u32[]{:S(2)}, u32[]{:S(2)}) collective-permute-start(f32[128,512]{1,0:T(8,128)S(1)} %get-tuple-element.24), channel_id=1, source_target_pairs={{0,1},{1,0},{2,3},{3,2},{4,5},{5,4},{6,7},{7,6},{8,9},{9,8},{10,11... | collective-permute-start | bytes 786440 | tf_op jit(solution)/shard_map/ppermute | solution.py:420
  5.0 9.2 %collective-permute-start.1 = (f32[128,512]{1,0:T(8,128)S(1)}, f32[128,512]{1,0:T(8,128)S(1)}, u32[]{:S(2)}, u32[]{:S(2)}) collective-permute-start(f32[128,512]{1,0:T(8,128)S(1)} %get-tuple-element.22), channel_id=1, source_target_pairs={{0,2},{1,3},{2,0},{3,1},{4,6},{5,7},{6,4},{7,5},{8,10},{9,11},{10,... | collective-permute-start | bytes 786440 | tf_op jit(solution)/shard_map/ppermute | solution.py:420
  7.0 12.2 %collective-permute-start = (f32[128,512]{1,0:T(8,128)S(1)}, f32[128,512]{1,0:T(8,128)S(1)}, u32[]{:S(2)}, u32[]{:S(2)}) collective-permute-start(f32[128,512]{1,0:T(8,128)S(1)} %get-tuple-element.21), channel_id=1, source_target_pairs={{0,3},{1,2},{2,1},{3,0},{4,7},{5,6},{6,5},{7,4},{8,11},{9,10},{10,... | collective-permute-start | bytes 786440 | tf_op jit(solution)/shard_map/ppermute | solution.py:420
  9.5 7.5 %collective-permute-start.5 = (f32[32,16,128]{2,1,0:T(8,128)S(1)}, f32[32,16,128]{2,1,0:T(8,128)S(1)}, u32[]{:S(2)}, u32[]{:S(2)}) collective-permute-start(f32[32,16,128]{2,1,0:T(8,128)S(1)} %collective-permute-done.3.refs_1_), channel_id=1, source_target_pairs={{0,8},{8,16},{16,24},{24,28},{28,20},{20,12},{12,4},{4,0},{1,9},{9... | collective-permute-start | bytes 786440 | tf_op jit(solution)/shard_map/ppermute | solution.py:430
  11.3 7.2 %collective-permute-start.6 = (f32[32,16,128]{2,1,0:T(8,128)S(1)}, f32[32,16,128]{2,1,0:T(8,128)S(1)}, u32[]{:S(2)}, u32[]{:S(2)}) collective-permute-start(f32[32,16,128]{2,1,0:T(8,128)S(1)} %collective-permute-done.4.refs_2_), channel_id=1, source_target_pairs={{8,0},{16,8},{24,16},{28,24},{20,28},{12,20},{4,12},{0,4},{9,1},{1... | collective-permute-start | bytes 786440 | tf_op jit(solution)/shard_map/ppermute | solution.py:431
  17.0 8.5 %collective-permute-start.7 = (f32[32,16,128]{2,1,0:T(8,128)S(1)}, f32[32,16,128]{2,1,0:T(8,128)S(1)}, u32[]{:S(2)}, u32[]{:S(2)}) collective-permute-start(f32[32,16,128]{2,1,0:T(8,128)S(1)} %collective-permute-done.5.refs_3_), channel_id=1, source_target_pairs={{0,8},{8,16},{16,24},{24,28},{28,20},{20,12},{12,4},{4,0},{1,9},{9... | collective-permute-start | bytes 786440 | tf_op jit(solution)/shard_map/ppermute | solution.py:430
  18.5 6.4 %collective-permute-start.8 = (f32[32,16,128]{2,1,0:T(8,128)S(1)}, f32[32,16,128]{2,1,0:T(8,128)S(1)}, u32[]{:S(2)}, u32[]{:S(2)}) collective-permute-start(f32[32,16,128]{2,1,0:T(8,128)S(1)} %collective-permute-done.6.refs_4_), channel_id=1, source_target_pairs={{8,0},{16,8},{24,16},{28,24},{20,28},{12,20},{4,12},{0,4},{9,1},{1... | collective-permute-start | bytes 786440 | tf_op jit(solution)/shard_map/ppermute | solution.py:431
  24.9 9.2 %collective-permute-start.12 = (f32[16,16,128]{2,1,0:T(8,128)S(1)}, f32[16,16,128]{2,1,0:T(8,128)S(1)}, u32[]{:S(2)}, u32[]{:S(2)}) collective-permute-start(f32[16,16,128]{2,1,0:T(8,128)S(1)} %slice.14), channel_id=1, source_target_pairs={{8,0},{16,8},{24,16},{28,24},{20,28},{12,20},{4,12},{0,4},{9,1},{1... | collective-permute-start | bytes 393224 | tf_op jit(solution)/shard_map/ppermute | solution.py:431
  25.5 5.0 %collective-permute-start.9 = (f32[16,16,128]{2,1,0:T(8,128)S(1)}, f32[16,16,128]{2,1,0:T(8,128)S(1)}, u32[]{:S(2)}, u32[]{:S(2)}) collective-permute-start(f32[16,16,128]{2,1,0:T(8,128)S(1)} %slice.12), channel_id=1, source_target_pairs={{0,8},{8,16},{16,24},{24,28},{28,20},{20,12},{12,4},{4,0},{1,9},{9... | collective-permute-start | bytes 393224 | tf_op jit(solution)/shard_map/ppermute | solution.py:430
  32.5 7.3 %collective-permute-start.10 = (f32[128,512]{1,0:T(8,128)S(1)}, f32[128,512]{1,0:T(8,128)S(1)}, u32[]{:S(2)}, u32[]{:S(2)}) collective-permute-start(f32[128,512]{1,0:T(8,128)S(1)} %shard_map.107), channel_id=1, source_target_pairs={{0,2},{1,3},{2,0},{3,1},{4,6},{5,7},{6,4},{7,5},{8,10},{9,11},{10,... | collective-permute-start | bytes 786440 | tf_op jit(solution)/shard_map/ppermute | solution.py:541
  36.7 3.2 %collective-permute-start.15 = (f32[128,512]{1,0:T(8,128)S(1)}, f32[128,512]{1,0:T(8,128)S(1)}, u32[]{:S(2)}, u32[]{:S(2)}) collective-permute-start(f32[128,512]{1,0:T(8,128)S(1)} %get-tuple-element.34), channel_id=1, source_target_pairs={{0,1},{1,0},{2,3},{3,2},{4,5},{5,4},{6,7},{7,6},{8,9},{9,8},{10,11... | collective-permute-start | bytes 786440 | tf_op jit(solution)/shard_map/ppermute | solution.py:541
  37.6 5.2 %collective-permute-start.13 = (f32[64,512]{1,0:T(8,128)S(1)}, f32[64,512]{1,0:T(8,128)S(1)}, u32[]{:S(2)}, u32[]{:S(2)}) collective-permute-start(f32[64,512]{1,0:T(8,128)S(1)} %get-tuple-element.32), channel_id=1, source_target_pairs={{0,3},{1,2},{2,1},{3,0},{4,7},{5,6},{6,5},{7,4},{8,11},{9,10},{10,... | collective-permute-start | bytes 393224 | tf_op jit(solution)/shard_map/ppermute | solution.py:541
  38.3 7.9 %collective-permute-start.14 = (f32[64,512]{1,0:T(8,128)S(1)}, f32[64,512]{1,0:T(8,128)S(1)}, u32[]{:S(2)}, u32[]{:S(2)}) collective-permute-start(f32[64,512]{1,0:T(8,128)S(1)} %get-tuple-element.33), channel_id=1, source_target_pairs={{0,2},{1,3},{2,0},{3,1},{4,6},{5,7},{6,4},{7,5},{8,10},{9,11},{10,... | collective-permute-start | bytes 393224 | tf_op jit(solution)/shard_map/ppermute | solution.py:541
  39.8 6.5 %collective-permute-start.11 = (f32[64,512]{1,0:T(8,128)S(1)}, f32[64,512]{1,0:T(8,128)S(1)}, u32[]{:S(2)}, u32[]{:S(2)}) collective-permute-start(f32[64,512]{1,0:T(8,128)S(1)} %slice.13), channel_id=1, source_target_pairs={{0,1},{1,0},{2,3},{3,2},{4,5},{5,4},{6,7},{7,6},{8,9},{9,8},{10,11... | collective-permute-start | bytes 393224 | tf_op jit(solution)/shard_map/ppermute | solution.py:541

commit v8 on v7

--- a/solution.py
+++ b/solution.py
@@ -274,7 +274,7 @@
         real_ref[z] = dot(table, jnp.concatenate([high, high, low], 0))
         return carry
 
-    lax.fori_loop(0, s.planes, plane, 0, unroll=4)
+    lax.fori_loop(0, s.planes, plane, 0, unroll=s.planes)
 
 
 def space_kernel(s, bands, real_ref, *refs):
@@ -298,7 +298,7 @@
         keep_turned(s, turned_ref, z, turned[: s.kept] + turned[s.kept :])
         return carry
 
-    lax.fori_loop(0, s.planes, plane, 0, unroll=4)
+    lax.fori_loop(0, s.planes, plane, 0, unroll=s.planes)
 
 
 def keep_turned(s, turned_ref, z, turned):
@@ -325,7 +325,7 @@
         keep_turned(s, turned_ref, half * part + z, dot(x_last, jnp.concatenate([high, low, high], 0)))
         return carry
 
-    lax.fori_loop(0, part, plane, 0, unroll=4)
+    lax.fori_loop(0, part, plane, 0, unroll=part)
 
     lanes = 2 * s.rows_y
     for start in range(0, s.tiles, 8):

time: 47.7 us -> 46.8 us (0.981)
  Pallas kernels: 17.3 us -> 14 us
  waiting for transfers between devices: 14.9 us -> 17.4 us
    pallas_call x13, Pallas kernels: 17.3 us -> 14 us  [kernel(): pl.pallas_call(body, in_specs=[place] * len(inputs) + [HBM] * len(fetched...]
    ppermute x4, waiting for transfers between devices: 2.27 us -> 3.82 us  [ring(): down = lax.ppermute(down, 'band', against)]
    ppermute x4, waiting for transfers between devices: 5.47 us -> 6.43 us  [ring(): up = lax.ppermute(up, 'band', along)]
  transfers between devices with their start and end apart: 16 -> 16, of which waited for: 8 -> 8; matrix products, arithmetic and copies ran while one was open for 0% -> 0% of each run, Pallas kernels for 34% -> 27%
where the time goes in v8:
time: 46.8 us; the launch traced here: 46.7 us
  waiting for transfers between devices  17.4 us (37%)
  starting transfers between devices  15.2 us (32%)
  Pallas kernels  14 us (30%)
    pallas_call x13, Pallas kernels, kernel(): pl.pallas_call(body, in_specs=[place] * len(inputs) + [HBM] * len(fetched...  14 us
    ppermute x4, starting transfers between devices, ring(): up = lax.ppermute(up, 'band', along)  8.3 us
    ppermute x4, waiting for transfers between devices, ring(): up = lax.ppermute(up, 'band', along)  6.43 us
    ppermute x5, waiting for transfers between devices, send(): return lax.ppermute(block, 'plane', [(i, i ^ k) for i in range(devices)])  5.81 us
    ppermute x5, starting transfers between devices, send(): return lax.ppermute(block, 'plane', [(i, i ^ k) for i in range(devices)])  3.84 us
    ppermute x4, waiting for transfers between devices, ring(): down = lax.ppermute(down, 'band', against)  3.82 us
    ppermute x3, starting transfers between devices, exchange(): lax.ppermute(blocks[k], 'plane', [(i, i ^ k) for i in range(devices)])  2.11 us
    ppermute x3, waiting for transfers between devices, exchange(): lax.ppermute(blocks[k], 'plane', [(i, i ^ k) for i in range(devices)])  1.3 us
  transfers between devices with their start and end apart: 16, of which 8 were waited for; matrix products, arithmetic and copies ran while one was open for 0% of the time, Pallas kernels for 27%

profile of v8, /device:TPU:0, one launch (start us, length us, event | category | flops | bytes accessed | tf_op | source)
XLA Modules:
  0.0 46.7 jit_solution(16687492034618825887)
XLA Ops:
  0.0 3.1 %collective-permute-start.3 = (f32[32,16,128]{2,1,0:T(8,128)}, f32[32,16,128]{2,1,0:T(8,128)S(1)}, u32[]{:S(2)}, u32[]{:S(2)}) collective-permute-start(f32[32,16,128]{2,1,0:T(8,128)} %refs_9_.1), channel_id=1, source_target_pairs={{0,8},{8,16},{16,24},{24,28},{28,20},{20,12},{12,4},{4,0},{1,9},{9... | collective-permute-start | bytes 786440 | tf_op jit(solution)/shard_map/ppermute | solution.py:430
  3.1 1.8 %shard_map.100 = (f32[128,512]{1,0:T(8,128)S(1)}, f32[128,512]{1,0:T(8,128)S(1)}, f32[128,512]{1,0:T(8,128)S(1)}, f32[128,512]{1,0:T(8,128)S(1)}) custom-call(f32[1,65,4,512]{3,2,1,0:T(4,128)} %bitcast.2, s32[3,2048]{1,0:T(4,128)} %refs_4_.2, bf16[4,128,512]{2,1,0:T(8,128)(2,1)} %constant.14.clone.table_hbm), custom_call_target="tpu_custom_call" | custom-call | flops 2147483648 | bytes 1048576 | tf_op jit(solution)/shard_map/pallas_call | solution.py:441
  5.0 2.0 %collective-permute-start.1 = (f32[128,512]{1,0:T(8,128)S(1)}, f32[128,512]{1,0:T(8,128)S(1)}, u32[]{:S(2)}, u32[]{:S(2)}) collective-permute-start(f32[128,512]{1,0:T(8,128)S(1)} %get-tuple-element.22), channel_id=1, source_target_pairs={{0,2},{1,3},{2,0},{3,1},{4,6},{5,7},{6,4},{7,5},{8,10},{9,11},{10,... | collective-permute-start | bytes 786440 | tf_op jit(solution)/shard_map/ppermute | solution.py:420
  7.0 2.5 %collective-permute-done.3.refs_1_ = f32[32,16,128]{2,1,0:T(8,128)S(1)} collective-permute-done((f32[32,16,128]{2,1,0:T(8,128)}, f32[32,16,128]{2,1,0:T(8,128)S(1)}, u32[]{:S(2)}, u32[]{:S(2)}) %collective-permute-start.3) | collective-permute-done | bytes 262176 | tf_op jit(solution)/shard_map/ppermute | solution.py:430
  9.5 1.8 %collective-permute-start.5 = (f32[32,16,128]{2,1,0:T(8,128)S(1)}, f32[32,16,128]{2,1,0:T(8,128)S(1)}, u32[]{:S(2)}, u32[]{:S(2)}) collective-permute-start(f32[32,16,128]{2,1,0:T(8,128)S(1)} %collective-permute-done.3.refs_1_), channel_id=1, source_target_pairs={{0,8},{8,16},{16,24},{24,28},{28,20},{20,12},{12,4},{4,0},{1,9},{9... | collective-permute-start | bytes 786440 | tf_op jit(solution)/shard_map/ppermute | solution.py:430
  11.5 1.5 %shard_map.101 = (f32[1088,256]{1,0:T(8,128)S(1)}, bf16[2,128,256]{2,1,0:T(8,128)(2,1)S(1)}, bf16[128,240]{1,0:T(8,128)(2,1)S(1)}, bf16[160,256]{1,0:T(8,128)(2,...) custom-call(f32[128,512]{1,0:T(8,128)S(1)} %get-tuple-element.23.ref, ...), custom_call_target="tpu_custom_call" | custom-call | flops 2147483648 | bytes 1048576 | tf_op jit(solution)/shard_map/pallas_call | solution.py:441
  13.1 1.2 %collective-permute-done.1.refs_0_ = f32[128,512]{1,0:T(8,128)S(1)} collective-permute-done((f32[128,512]{1,0:T(8,128)S(1)}, f32[128,512]{1,0:T(8,128)S(1)}, u32[]{:S(2)}, u32[]{:S(2)}) %collective-permute-start.1) | collective-permute-done | bytes 262176 | tf_op jit(solution)/shard_map/ppermute | solution.py:420
  14.2 0.8 %shard_map.102.refs_1_ = f32[1088,256]{1,0:T(8,128)S(1)} custom-call(f32[128,512]{1,0:T(8,128)S(1)} %collective-permute-done.1.refs_0_, f32[1088,256]{1,0:T(8,128)S(1)} %get-tuple-element.25.refs_1_, s32[3,2048]{1,0:T(4,128)S(1)} %copy-done), custom_call_target="tpu_custom_call" | custom-call | flops 2147483648 | bytes 1048576 | tf_op jit(solution)/shard_map/pallas_call | solution.py:441
  15.1 1.9 %collective-permute-done.5.refs_3_ = f32[32,16,128]{2,1,0:T(8,128)S(1)} collective-permute-done((f32[32,16,128]{2,1,0:T(8,128)S(1)}, f32[32,16,128]{2,1,0:T(8,128)S(1)}, u32[]{:S(2)}, u32[]{:S(2)}) %collective-permute-start.5) | collective-permute-done | bytes 262176 | tf_op jit(solution)/shard_map/ppermute | solution.py:430
  17.0 1.5 %collective-permute-start.7 = (f32[32,16,128]{2,1,0:T(8,128)S(1)}, f32[32,16,128]{2,1,0:T(8,128)S(1)}, u32[]{:S(2)}, u32[]{:S(2)}) collective-permute-start(f32[32,16,128]{2,1,0:T(8,128)S(1)} %collective-permute-done.5.refs_3_), channel_id=1, source_target_pairs={{0,8},{8,16},{16,24},{24,28},{28,20},{20,12},{12,4},{4,0},{1,9},{9... | collective-permute-start | bytes 786440 | tf_op jit(solution)/shard_map/ppermute | solution.py:430
  19.2 1.5 %shard_map.103.half_ref = f32[4,1560,128]{2,1,0:T(8,128)S(1)} custom-call(f32[128,512]{1,0:T(8,128)S(1)} %collective-permute-done.refs_0_, f32[1088,256]{1,0:T(8,128)S(1)} %shard_map.102.refs_1_, s32[3,2048]{1,0:T(4,128)S(1)} %copy-done, bf16[2,128,256]{2,1,0:T(8,128)(2,1)S(1)} %get-tuple-element.26.refs_3_), custom_call_target="tpu_custom_call" | custom-call | flops 2147483648 | bytes 1048576 | tf_op jit(solution)/shard_map/pallas_call | solution.py:441
  21.4 3.8 %collective-permute-done.8.refs_6_ = f32[32,16,128]{2,1,0:T(8,128)S(1)} collective-permute-done((f32[32,16,128]{2,1,0:T(8,128)S(1)}, f32[32,16,128]{2,1,0:T(8,128)S(1)}, u32[]{:S(2)}, u32[]{:S(2)}) %collective-permute-start.8) | collective-permute-done | bytes 262176 | tf_op jit(solution)/shard_map/ppermute | solution.py:431
  25.5 1.9 %collective-permute-start.9 = (f32[16,16,128]{2,1,0:T(8,128)S(1)}, f32[16,16,128]{2,1,0:T(8,128)S(1)}, u32[]{:S(2)}, u32[]{:S(2)}) collective-permute-start(f32[16,16,128]{2,1,0:T(8,128)S(1)} %slice.12), channel_id=1, source_target_pairs={{0,8},{8,16},{16,24},{24,28},{28,20},{20,12},{12,4},{4,0},{1,9},{9... | collective-permute-start | bytes 393224 | tf_op jit(solution)/shard_map/ppermute | solution.py:430
  27.4 1.1 %shard_map.105.first_ref = f32[4,1560,128]{2,1,0:T(8,128)S(1)} custom-call(f32[32,144,256]{2,1,0:T(8,128)S(1)} %shard_map.104.real_ref, f32[32,16,128]{2,1,0:T(8,128)S(1)} %get-tuple-element.28.refs_0_, f32[32,16,128]{2,1,0:T(8,128)S(1)} %collective-permute-done.3.refs_1_, f32[32,16,128]{2,1,0:T(8,128)S(1)} %collective-permute-done.4.refs_2_, ...), custom_call_target="tpu_custom_call" | custom-call | flops 2147483648 | bytes 1048576 | tf_op jit(solution)/shard_map/pallas_call | solution.py:441
  28.5 2.0 %collective-permute-done.9.slab_ref = f32[16,16,128]{2,1,0:T(8,128)S(1)} collective-permute-done((f32[16,16,128]{2,1,0:T(8,128)S(1)}, f32[16,16,128]{2,1,0:T(8,128)S(1)}, u32[]{:S(2)}, u32[]{:S(2)}) %collective-permute-start.9) | collective-permute-done | bytes 131104 | tf_op jit(solution)/shard_map/ppermute | solution.py:430
  30.5 0.8 %shard_map.106.refs_0_ = bf16[128,2176]{1,0:T(8,128)(2,1)S(1)} custom-call(f32[4,1560,128]{2,1,0:T(8,128)S(1)} %shard_map.105.first_ref, f32[32,144,256]{2,1,0:T(8,128)S(1)} %shard_map.104.real_ref, f32[16,16,128]{2,1,0:T(8,128)S(1)} %collective-permute-done.9.slab_ref, bf16[8,80,48]{2,1,0:T(8,128)(2,1)S(1)} %get-tuple-element.30.x_last_ref, ...), custom_call_target="tpu_custom_call" | custom-call | flops 2147483648 | bytes 1048576 | tf_op jit(solution)/shard_map/pallas_call | solution.py:441
  32.1 1.5 %collective-permute-start.10 = (f32[128,512]{1,0:T(8,128)S(1)}, f32[128,512]{1,0:T(8,128)S(1)}, u32[]{:S(2)}, u32[]{:S(2)}) collective-permute-start(f32[128,512]{1,0:T(8,128)S(1)} %shard_map.107), channel_id=1, source_target_pairs={{0,2},{1,3},{2,0},{3,1},{4,6},{5,7},{6,4},{7,5},{8,10},{9,11},{10,... | collective-permute-start | bytes 786440 | tf_op jit(solution)/shard_map/ppermute | solution.py:541
  33.6 0.8 %shard_map.108.refs_0_.refs_1_ = bf16[128,2176]{1,0:T(8,128)(2,1)S(1)} custom-call(f32[4,1560,128]{2,1,0:T(8,128)S(1)} %shard_map.105.first_ref, f32[32,144,256]{2,1,0:T(8,128)S(1)} %shard_map.104.real_ref, f32[16,16,128]{2,1,0:T(8,128)S(1)} %collective-permute-done.12.slab_ref, bf16[8,80,48]{2,1,0:T(8,128)(2,1)S(1)} %get-tuple-element.30.x_last_ref, ...), custom_call_target="tpu_custom_call" | custom-call | flops 2147483648 | bytes 1048576 | tf_op jit(solution)/shard_map/pallas_call | solution.py:441
  34.5 1.4 %shard_map.110 = (f32[128,512]{1,0:T(8,128)S(1)}, f32[128,512]{1,0:T(8,128)S(1)}) custom-call(bf16[128,2176]{1,0:T(8,128)(2,1)S(1)} %shard_map.106.refs_0_, bf16[128,2176]{1,0:T(8,128)(2,1)S(1)} %shard_map.108.refs_0_.refs_1_, s32[3,2048]{1,0:T(4,128)S(1)} %copy-done), custom_call_target="tpu_custom_call" | custom-call | flops 2147483648 | bytes 1048576 | tf_op jit(solution)/shard_map/pallas_call | solution.py:441
  36.0 0.8 %shard_map.109 = (f32[64,512]{1,0:T(8,128)S(1)}, f32[64,512]{1,0:T(8,128)S(1)}) custom-call(bf16[128,2176]{1,0:T(8,128)(2,1)S(1)} %shard_map.108.refs_0_.refs_1_, s32[3,2048]{1,0:T(4,128)S(1)} %copy-done), custom_call_target="tpu_custom_call" | custom-call | flops 2147483648 | bytes 1048576 | tf_op jit(solution)/shard_map/pallas_call | solution.py:441
  37.5 1.5 %collective-permute-start.14 = (f32[64,512]{1,0:T(8,128)S(1)}, f32[64,512]{1,0:T(8,128)S(1)}, u32[]{:S(2)}, u32[]{:S(2)}) collective-permute-start(f32[64,512]{1,0:T(8,128)S(1)} %get-tuple-element.33), channel_id=1, source_target_pairs={{0,2},{1,3},{2,0},{3,1},{4,6},{5,7},{6,4},{7,5},{8,10},{9,11},{10,... | collective-permute-start | bytes 393224 | tf_op jit(solution)/shard_map/ppermute | solution.py:541
  39.6 2.3 %collective-permute-done.13.refs_1_ = f32[64,512]{1,0:T(8,128)S(1)} collective-permute-done((f32[64,512]{1,0:T(8,128)S(1)}, f32[64,512]{1,0:T(8,128)S(1)}, u32[]{:S(2)}, u32[]{:S(2)}) %collective-permute-start.13) | collective-permute-done | bytes 131104 | tf_op jit(solution)/shard_map/ppermute | solution.py:541
  41.9 3.5 %collective-permute-done.14.refs_2_ = f32[64,512]{1,0:T(8,128)S(1)} collective-permute-done((f32[64,512]{1,0:T(8,128)S(1)}, f32[64,512]{1,0:T(8,128)S(1)}, u32[]{:S(2)}, u32[]{:S(2)}) %collective-permute-start.14) | collective-permute-done | bytes 131104 | tf_op jit(solution)/shard_map/ppermute | solution.py:541
  45.4 1.2 %shard_map.112 = f32[1,65,4,512]{3,2,1,0:T(4,128)} custom-call(f32[64,512]{1,0:T(8,128)S(1)} %collective-permute-done.11.refs_0_, f32[64,512]{1,0:T(8,128)S(1)} %collective-permute-done.13.refs_1_, f32[64,512]{1,0:T(8,128)S(1)} %collective-permute-done.14.refs_2_, f32[256,512]{1,0:T(8,128)S(1)} %shard_map.111.refs_3_, s32[3,2048]{1,0:T(4,128)S(1)} %copy-done, ...), custom_call_target="tpu_custom_call" | custom-call | flops 2147483648 | bytes 1048576 | tf_op jit(solution)/shard_map/pallas_call | solution.py:441
  (26 shorter events, 4.3 us)
Async XLA Ops:
  0.0 9.5 %collective-permute-start.3 = (f32[32,16,128]{2,1,0:T(8,128)}, f32[32,16,128]{2,1,0:T(8,128)S(1)}, u32[]{:S(2)}, u32[]{:S(2)}) collective-permute-start(f32[32,16,128]{2,1,0:T(8,128)} %refs_9_.1), channel_id=1, source_target_pairs={{0,8},{8,16},{16,24},{24,28},{28,20},{20,12},{12,4},{4,0},{1,9},{9... | collective-permute-start | bytes 786440 | tf_op jit(solution)/shard_map/ppermute | solution.py:430
  3.1 8.3 %collective-permute-start.4 = (f32[32,16,128]{2,1,0:T(8,128)}, f32[32,16,128]{2,1,0:T(8,128)S(1)}, u32[]{:S(2)}, u32[]{:S(2)}) collective-permute-start(f32[32,16,128]{2,1,0:T(8,128)} %refs_9_.1), channel_id=1, source_target_pairs={{8,0},{16,8},{24,16},{28,24},{20,28},{12,20},{4,12},{0,4},{9,1},{1... | collective-permute-start | bytes 786440 | tf_op jit(solution)/shard_map/ppermute | solution.py:431
  3.1 8.5 %copy-start = (s32[3,2048]{1,0:T(4,128)S(1)}, s32[3,2048]{1,0:T(4,128)}, u32[]{:S(2)}) copy-start(s32[3,2048]{1,0:T(4,128)} %refs_4_.2) | copy-start | bytes 73732
  4.9 6.6 %collective-permute-start.2 = (f32[128,512]{1,0:T(8,128)S(1)}, f32[128,512]{1,0:T(8,128)S(1)}, u32[]{:S(2)}, u32[]{:S(2)}) collective-permute-start(f32[128,512]{1,0:T(8,128)S(1)} %get-tuple-element.24), channel_id=1, source_target_pairs={{0,1},{1,0},{2,3},{3,2},{4,5},{5,4},{6,7},{7,6},{8,9},{9,8},{10,11... | collective-permute-start | bytes 786440 | tf_op jit(solution)/shard_map/ppermute | solution.py:420
  5.0 9.2 %collective-permute-start.1 = (f32[128,512]{1,0:T(8,128)S(1)}, f32[128,512]{1,0:T(8,128)S(1)}, u32[]{:S(2)}, u32[]{:S(2)}) collective-permute-start(f32[128,512]{1,0:T(8,128)S(1)} %get-tuple-element.22), channel_id=1, source_target_pairs={{0,2},{1,3},{2,0},{3,1},{4,6},{5,7},{6,4},{7,5},{8,10},{9,11},{10,... | collective-permute-start | bytes 786440 | tf_op jit(solution)/shard_map/ppermute | solution.py:420
  7.0 12.2 %collective-permute-start = (f32[128,512]{1,0:T(8,128)S(1)}, f32[128,512]{1,0:T(8,128)S(1)}, u32[]{:S(2)}, u32[]{:S(2)}) collective-permute-start(f32[128,512]{1,0:T(8,128)S(1)} %get-tuple-element.21), channel_id=1, source_target_pairs={{0,3},{1,2},{2,1},{3,0},{4,7},{5,6},{6,5},{7,4},{8,11},{9,10},{10,... | collective-permute-start | bytes 786440 | tf_op jit(solution)/shard_map/ppermute | solution.py:420
  9.5 7.5 %collective-permute-start.5 = (f32[32,16,128]{2,1,0:T(8,128)S(1)}, f32[32,16,128]{2,1,0:T(8,128)S(1)}, u32[]{:S(2)}, u32[]{:S(2)}) collective-permute-start(f32[32,16,128]{2,1,0:T(8,128)S(1)} %collective-permute-done.3.refs_1_), channel_id=1, source_target_pairs={{0,8},{8,16},{16,24},{24,28},{28,20},{20,12},{12,4},{4,0},{1,9},{9... | collective-permute-start | bytes 786440 | tf_op jit(solution)/shard_map/ppermute | solution.py:430
  11.3 7.2 %collective-permute-start.6 = (f32[32,16,128]{2,1,0:T(8,128)S(1)}, f32[32,16,128]{2,1,0:T(8,128)S(1)}, u32[]{:S(2)}, u32[]{:S(2)}) collective-permute-start(f32[32,16,128]{2,1,0:T(8,128)S(1)} %collective-permute-done.4.refs_2_), channel_id=1, source_target_pairs={{8,0},{16,8},{24,16},{28,24},{20,28},{12,20},{4,12},{0,4},{9,1},{1... | collective-permute-start | bytes 786440 | tf_op jit(solution)/shard_map/ppermute | solution.py:431
  17.0 8.5 %collective-permute-start.7 = (f32[32,16,128]{2,1,0:T(8,128)S(1)}, f32[32,16,128]{2,1,0:T(8,128)S(1)}, u32[]{:S(2)}, u32[]{:S(2)}) collective-permute-start(f32[32,16,128]{2,1,0:T(8,128)S(1)} %collective-permute-done.5.refs_3_), channel_id=1, source_target_pairs={{0,8},{8,16},{16,24},{24,28},{28,20},{20,12},{12,4},{4,0},{1,9},{9... | collective-permute-start | bytes 786440 | tf_op jit(solution)/shard_map/ppermute | solution.py:430
  18.5 6.7 %collective-permute-start.8 = (f32[32,16,128]{2,1,0:T(8,128)S(1)}, f32[32,16,128]{2,1,0:T(8,128)S(1)}, u32[]{:S(2)}, u32[]{:S(2)}) collective-permute-start(f32[32,16,128]{2,1,0:T(8,128)S(1)} %collective-permute-done.6.refs_4_), channel_id=1, source_target_pairs={{8,0},{16,8},{24,16},{28,24},{20,28},{12,20},{4,12},{0,4},{9,1},{1... | collective-permute-start | bytes 786440 | tf_op jit(solution)/shard_map/ppermute | solution.py:431
  25.2 8.4 %collective-permute-start.12 = (f32[16,16,128]{2,1,0:T(8,128)S(1)}, f32[16,16,128]{2,1,0:T(8,128)S(1)}, u32[]{:S(2)}, u32[]{:S(2)}) collective-permute-start(f32[16,16,128]{2,1,0:T(8,128)S(1)} %slice.14), channel_id=1, source_target_pairs={{8,0},{16,8},{24,16},{28,24},{20,28},{12,20},{4,12},{0,4},{9,1},{1... | collective-permute-start | bytes 393224 | tf_op jit(solution)/shard_map/ppermute | solution.py:431
  25.5 5.0 %collective-permute-start.9 = (f32[16,16,128]{2,1,0:T(8,128)S(1)}, f32[16,16,128]{2,1,0:T(8,128)S(1)}, u32[]{:S(2)}, u32[]{:S(2)}) collective-permute-start(f32[16,16,128]{2,1,0:T(8,128)S(1)} %slice.12), channel_id=1, source_target_pairs={{0,8},{8,16},{16,24},{24,28},{28,20},{20,12},{12,4},{4,0},{1,9},{9... | collective-permute-start | bytes 393224 | tf_op jit(solution)/shard_map/ppermute | solution.py:430
  32.1 6.8 %collective-permute-start.10 = (f32[128,512]{1,0:T(8,128)S(1)}, f32[128,512]{1,0:T(8,128)S(1)}, u32[]{:S(2)}, u32[]{:S(2)}) collective-permute-start(f32[128,512]{1,0:T(8,128)S(1)} %shard_map.107), channel_id=1, source_target_pairs={{0,2},{1,3},{2,0},{3,1},{4,6},{5,7},{6,4},{7,5},{8,10},{9,11},{10,... | collective-permute-start | bytes 786440 | tf_op jit(solution)/shard_map/ppermute | solution.py:541
  35.9 3.2 %collective-permute-start.15 = (f32[128,512]{1,0:T(8,128)S(1)}, f32[128,512]{1,0:T(8,128)S(1)}, u32[]{:S(2)}, u32[]{:S(2)}) collective-permute-start(f32[128,512]{1,0:T(8,128)S(1)} %get-tuple-element.34), channel_id=1, source_target_pairs={{0,1},{1,0},{2,3},{3,2},{4,5},{5,4},{6,7},{7,6},{8,9},{9,8},{10,11... | collective-permute-start | bytes 786440 | tf_op jit(solution)/shard_map/ppermute | solution.py:541
  36.8 5.2 %collective-permute-start.13 = (f32[64,512]{1,0:T(8,128)S(1)}, f32[64,512]{1,0:T(8,128)S(1)}, u32[]{:S(2)}, u32[]{:S(2)}) collective-permute-start(f32[64,512]{1,0:T(8,128)S(1)} %get-tuple-element.32), channel_id=1, source_target_pairs={{0,3},{1,2},{2,1},{3,0},{4,7},{5,6},{6,5},{7,4},{8,11},{9,10},{10,... | collective-permute-start | bytes 393224 | tf_op jit(solution)/shard_map/ppermute | solution.py:541
  37.5 7.9 %collective-permute-start.14 = (f32[64,512]{1,0:T(8,128)S(1)}, f32[64,512]{1,0:T(8,128)S(1)}, u32[]{:S(2)}, u32[]{:S(2)}) collective-permute-start(f32[64,512]{1,0:T(8,128)S(1)} %get-tuple-element.33), channel_id=1, source_target_pairs={{0,2},{1,3},{2,0},{3,1},{4,6},{5,7},{6,4},{7,5},{8,10},{9,11},{10,... | collective-permute-start | bytes 393224 | tf_op jit(solution)/shard_map/ppermute | solution.py:541
  39.0 6.5 %collective-permute-start.11 = (f32[64,512]{1,0:T(8,128)S(1)}, f32[64,512]{1,0:T(8,128)S(1)}, u32[]{:S(2)}, u32[]{:S(2)}) collective-permute-start(f32[64,512]{1,0:T(8,128)S(1)} %slice.13), channel_id=1, source_target_pairs={{0,1},{1,0},{2,3},{3,2},{4,5},{5,4},{6,7},{7,6},{8,9},{9,8},{10,11... | collective-permute-start | bytes 393224 | tf_op jit(solution)/shard_map/ppermute | solution.py:541

commit v9 on v8

--- a/solution.py
+++ b/solution.py
@@ -157,29 +157,41 @@
 
 def back_kernel(s, which, started, ended, *refs):
     in_refs, refs = refs[: len(which)], refs[len(which) :]
-    table_ref, out_ref = refs[-2:]
+    table_ref, out_ref = refs[len(refs) - 4 : len(refs) - 2] if ended else refs[-2:]
     part = jnp.zeros((s.batch, s.sticks), f32)
     me = lax.axis_index("plane")
-    total = refs[0][...] if started else None
     blocks = {}
     for (k, half, row), ref in zip(which, in_refs, strict=True):
         if half is None:
             blocks[k] = ref[...]
         else:
             blocks.setdefault(k, [part, part])[half] = ref[row : row + s.batch, :]
+    tables, data = [], []
     for k, block in blocks.items():
         high, low = split(jnp.concatenate(block, 0) if isinstance(block, list) else block)
         table = table_ref[partner(me, k)]
-        table = jnp.concatenate([table, table[:, : 2 * s.batch]], 1)
-        term = dot(table, jnp.concatenate([high, high, low], 0))
-        total = term if total is None else total + term
-    if ended:
-        total = jnp.where(live_of(s, refs[-3], me), total[: 4 * s.depths], 0.0)
-        out_ref[0, 1 : s.span - 1] = total.reshape(s.depths, 4, s.sticks)
-        for depth in (0, s.span - 1):
-            out_ref[0, depth] = jnp.zeros((4, s.sticks), f32)
-    else:
-        out_ref[...] = total
+        tables.append(jnp.concatenate([table, table[:, : 2 * s.batch]], 1))
+        data.append(jnp.concatenate([high, high, low], 0))
+    if not ended:
+        out_ref[...] = sum(dot(table, block) for table, block in zip(tables[1:], data[1:])) + dot(tables[0], data[0])
+        return
+    staged_ref, sems = refs[-2:]
+    live = live_of(s, refs[1], me)
+    for depth in (0, s.span - 1):
+        staged_ref[0, depth] = jnp.zeros((4, s.sticks), f32)
+    middle = s.depths // 2 + 1
+    copies = []
+    for i, (first, end) in enumerate(((1, middle), (middle, s.span - 1))):
+        rows = slice(4 * (first - 1), 4 * (end - 1))
+        total = refs[0][rows, :] if started else 0.0
+        for table, block in zip(tables, data, strict=True):
+            total = total + dot(table[rows], block)
+        staged_ref[0, first:end] = jnp.where(live[rows], total, 0.0).reshape(end - first, 4, s.sticks)
+        own = slice(0, middle) if i == 0 else slice(middle, s.span)
+        copies.append(pltpu.make_async_copy(staged_ref.at[0, own], out_ref.at[0, own], sems.at[i]))
+        copies[-1].start()
+    for copy in copies:
+        copy.wait()
 
 
 def fetching_kernel(body, inputs, outs, count, *refs):
@@ -353,16 +365,15 @@
 
 def pick_kernel(s, which, count, joined, *refs):
     flat_refs, sticks_ref, refs = refs[:count], refs[count], refs[count + 1 :]
-    out_refs, (x_ref, y_ref, hot_ref) = refs[:-3], refs[-3:]
+    out_refs, (x_ref, y_ref) = refs[:-2], refs[-2:]
     me = lax.axis_index("plane")
     places(s, sticks_ref, [partner(me, k) for k in which], x_ref, y_ref)
     rows = 2 * s.planes
     flat = jnp.concatenate([flat_ref[...] for flat_ref in flat_refs], 0)
     for i in range(len(which)):
         columns = slice(i * s.sticks, (i + 1) * s.sticks)
-        for x in range(2 * s.tiles):
-            hot_ref[x * s.rows_y : (x + 1) * s.rows_y, :] = one_hot(x, x_ref[:, columns], y_ref[:, columns])
-        found = dot(flat, hot_ref[...])
+        hot = [one_hot(x, x_ref[:, columns], y_ref[:, columns]) for x in range(2 * s.tiles)]
+        found = dot(flat, jnp.concatenate(hot, 0))
         for h in range(count):
             row = 2 * h * rows
             out_ref, at = (out_refs[0], (i * count + h) * rows) if joined else (out_refs[i], h * rows)
@@ -432,7 +443,7 @@
             slabs += [up, down]
         return slabs
 
-    def kernel(body, inputs, out_shape, limit, flops, scratch_shapes=(), place=VMEM, fetched=()):
+    def kernel(body, inputs, out_shape, limit, flops, scratch_shapes=(), place=VMEM, fetched=(), into=VMEM):
         single = not isinstance(out_shape, list)
         outs = [out_shape] if single else out_shape
         extra = [jax.ShapeDtypeStruct(a.shape, a.dtype) for a in fetched]
@@ -441,7 +452,7 @@
         results = pl.pallas_call(
             body,
             in_specs=[place] * len(inputs) + [HBM] * len(fetched),
-            out_specs=[VMEM] * (len(outs) + len(fetched)),
+            out_specs=[into] * (len(outs) + len(fetched)),
             out_shape=outs + extra,
             scratch_shapes=[*scratch_shapes] + [pltpu.SemaphoreType.DMA((len(fetched),))] * bool(fetched),
             compiler_params=pltpu.CompilerParams(vmem_limit_bytes=limit << 10),
@@ -533,7 +544,6 @@
                 [
                     pltpu.VMEM((s.rows_y, len(which) * s.sticks), bf16),
                     pltpu.VMEM((s.rows_y, len(which) * s.sticks), bf16),
-                    pltpu.VMEM((positions, s.sticks), bf16),
                 ],
             )
 
@@ -563,6 +573,8 @@
             jax.ShapeDtypeStruct((1,) + given.shape[1:], f32),
             16 << 10,
             1 << 31,
+            [pltpu.VMEM((1,) + given.shape[1:], f32), pltpu.SemaphoreType.DMA((2,))],
+            into=HBM,
         )
         results.append(jnp.transpose(result, (0, 2, 1, 3)))
     return results[0] if len(results) == 1 else jnp.concatenate(results, 0)

time: 46.8 us -> 46.8 us (level)
  no operation moved by 1% of the time
where the time goes in v9:
time: 46.8 us; the launch traced here: 46.6 us
  waiting for transfers between devices  17.4 us (37%)
  starting transfers between devices  15.2 us (32%)
  Pallas kernels  13.9 us (30%)
    pallas_call x13, Pallas kernels, kernel(): pl.pallas_call(body, in_specs=[place] * len(inputs) + [HBM] * len(fetched...  13.9 us
    ppermute x4, starting transfers between devices, ring(): up = lax.ppermute(up, 'band', along)  8.3 us
    ppermute x4, waiting for transfers between devices, ring(): up = lax.ppermute(up, 'band', along)  6.43 us
    ppermute x5, waiting for transfers between devices, send(): return lax.ppermute(block, 'plane', [(i, i ^ k) for i in range(devices)])  5.82 us
    ppermute x5, starting transfers between devices, send(): return lax.ppermute(block, 'plane', [(i, i ^ k) for i in range(devices)])  3.84 us
    ppermute x4, waiting for transfers between devices, ring(): down = lax.ppermute(down, 'band', against)  3.82 us
    ppermute x3, starting transfers between devices, exchange(): lax.ppermute(blocks[k], 'plane', [(i, i ^ k) for i in range(devices)])  2.11 us
    ppermute x3, waiting for transfers between devices, exchange(): lax.ppermute(blocks[k], 'plane', [(i, i ^ k) for i in range(devices)])  1.3 us
  transfers between devices with their start and end apart: 16, of which 8 were waited for; matrix products, arithmetic and copies ran while one was open for 0% of the time, Pallas kernels for 27%

profile of v9, /device:TPU:0, one launch (start us, length us, event | category | flops | bytes accessed | tf_op | source)
XLA Modules:
  0.0 46.6 jit_solution(11088970920092947825)
XLA Ops:
  0.0 3.1 %collective-permute-start.3 = (f32[32,16,128]{2,1,0:T(8,128)}, f32[32,16,128]{2,1,0:T(8,128)S(1)}, u32[]{:S(2)}, u32[]{:S(2)}) collective-permute-start(f32[32,16,128]{2,1,0:T(8,128)} %refs_9_.1), channel_id=1, source_target_pairs={{0,8},{8,16},{16,24},{24,28},{28,20},{20,12},{12,4},{4,0},{1,9},{9... | collective-permute-start | bytes 786440 | tf_op jit(solution)/shard_map/ppermute | solution.py:441
  3.1 1.8 %shard_map.100 = (f32[128,512]{1,0:T(8,128)S(1)}, f32[128,512]{1,0:T(8,128)S(1)}, f32[128,512]{1,0:T(8,128)S(1)}, f32[128,512]{1,0:T(8,128)S(1)}) custom-call(f32[1,65,4,512]{3,2,1,0:T(4,128)} %bitcast.2, s32[3,2048]{1,0:T(4,128)} %refs_4_.2, bf16[4,128,512]{2,1,0:T(8,128)(2,1)} %constant.14.clone.table_hbm), custom_call_target="tpu_custom_call" | custom-call | flops 2147483648 | bytes 1048576 | tf_op jit(solution)/shard_map/pallas_call | solution.py:452
  5.0 2.0 %collective-permute-start.1 = (f32[128,512]{1,0:T(8,128)S(1)}, f32[128,512]{1,0:T(8,128)S(1)}, u32[]{:S(2)}, u32[]{:S(2)}) collective-permute-start(f32[128,512]{1,0:T(8,128)S(1)} %get-tuple-element.22), channel_id=1, source_target_pairs={{0,2},{1,3},{2,0},{3,1},{4,6},{5,7},{6,4},{7,5},{8,10},{9,11},{10,... | collective-permute-start | bytes 786440 | tf_op jit(solution)/shard_map/ppermute | solution.py:431
  7.0 2.5 %collective-permute-done.3.refs_1_ = f32[32,16,128]{2,1,0:T(8,128)S(1)} collective-permute-done((f32[32,16,128]{2,1,0:T(8,128)}, f32[32,16,128]{2,1,0:T(8,128)S(1)}, u32[]{:S(2)}, u32[]{:S(2)}) %collective-permute-start.3) | collective-permute-done | bytes 262176 | tf_op jit(solution)/shard_map/ppermute | solution.py:441
  9.5 1.8 %collective-permute-start.5 = (f32[32,16,128]{2,1,0:T(8,128)S(1)}, f32[32,16,128]{2,1,0:T(8,128)S(1)}, u32[]{:S(2)}, u32[]{:S(2)}) collective-permute-start(f32[32,16,128]{2,1,0:T(8,128)S(1)} %collective-permute-done.3.refs_1_), channel_id=1, source_target_pairs={{0,8},{8,16},{16,24},{24,28},{28,20},{20,12},{12,4},{4,0},{1,9},{9... | collective-permute-start | bytes 786440 | tf_op jit(solution)/shard_map/ppermute | solution.py:441
  11.5 1.5 %shard_map.101 = (f32[1088,256]{1,0:T(8,128)S(1)}, bf16[2,128,256]{2,1,0:T(8,128)(2,1)S(1)}, bf16[128,240]{1,0:T(8,128)(2,1)S(1)}, bf16[160,256]{1,0:T(8,128)(2,...) custom-call(f32[128,512]{1,0:T(8,128)S(1)} %get-tuple-element.23.ref, ...), custom_call_target="tpu_custom_call" | custom-call | flops 2147483648 | bytes 1048576 | tf_op jit(solution)/shard_map/pallas_call | solution.py:452
  13.1 1.2 %collective-permute-done.1.refs_0_ = f32[128,512]{1,0:T(8,128)S(1)} collective-permute-done((f32[128,512]{1,0:T(8,128)S(1)}, f32[128,512]{1,0:T(8,128)S(1)}, u32[]{:S(2)}, u32[]{:S(2)}) %collective-permute-start.1) | collective-permute-done | bytes 262176 | tf_op jit(solution)/shard_map/ppermute | solution.py:431
  14.2 0.8 %shard_map.102.refs_1_ = f32[1088,256]{1,0:T(8,128)S(1)} custom-call(f32[128,512]{1,0:T(8,128)S(1)} %collective-permute-done.1.refs_0_, f32[1088,256]{1,0:T(8,128)S(1)} %get-tuple-element.25.refs_1_, s32[3,2048]{1,0:T(4,128)S(1)} %copy-done), custom_call_target="tpu_custom_call" | custom-call | flops 2147483648 | bytes 1048576 | tf_op jit(solution)/shard_map/pallas_call | solution.py:452
  15.1 1.9 %collective-permute-done.5.refs_3_ = f32[32,16,128]{2,1,0:T(8,128)S(1)} collective-permute-done((f32[32,16,128]{2,1,0:T(8,128)S(1)}, f32[32,16,128]{2,1,0:T(8,128)S(1)}, u32[]{:S(2)}, u32[]{:S(2)}) %collective-permute-start.5) | collective-permute-done | bytes 262176 | tf_op jit(solution)/shard_map/ppermute | solution.py:441
  17.0 1.5 %collective-permute-start.7 = (f32[32,16,128]{2,1,0:T(8,128)S(1)}, f32[32,16,128]{2,1,0:T(8,128)S(1)}, u32[]{:S(2)}, u32[]{:S(2)}) collective-permute-start(f32[32,16,128]{2,1,0:T(8,128)S(1)} %collective-permute-done.5.refs_3_), channel_id=1, source_target_pairs={{0,8},{8,16},{16,24},{24,28},{28,20},{20,12},{12,4},{4,0},{1,9},{9... | collective-permute-start | bytes 786440 | tf_op jit(solution)/shard_map/ppermute | solution.py:441
  19.2 1.5 %shard_map.103.half_ref = f32[4,1560,128]{2,1,0:T(8,128)S(1)} custom-call(f32[128,512]{1,0:T(8,128)S(1)} %collective-permute-done.refs_0_, f32[1088,256]{1,0:T(8,128)S(1)} %shard_map.102.refs_1_, s32[3,2048]{1,0:T(4,128)S(1)} %copy-done, bf16[2,128,256]{2,1,0:T(8,128)(2,1)S(1)} %get-tuple-element.26.refs_3_), custom_call_target="tpu_custom_call" | custom-call | flops 2147483648 | bytes 1048576 | tf_op jit(solution)/shard_map/pallas_call | solution.py:452
  21.4 3.8 %collective-permute-done.8.refs_6_ = f32[32,16,128]{2,1,0:T(8,128)S(1)} collective-permute-done((f32[32,16,128]{2,1,0:T(8,128)S(1)}, f32[32,16,128]{2,1,0:T(8,128)S(1)}, u32[]{:S(2)}, u32[]{:S(2)}) %collective-permute-start.8) | collective-permute-done | bytes 262176 | tf_op jit(solution)/shard_map/ppermute | solution.py:442
  25.5 1.9 %collective-permute-start.9 = (f32[16,16,128]{2,1,0:T(8,128)S(1)}, f32[16,16,128]{2,1,0:T(8,128)S(1)}, u32[]{:S(2)}, u32[]{:S(2)}) collective-permute-start(f32[16,16,128]{2,1,0:T(8,128)S(1)} %slice.12), channel_id=1, source_target_pairs={{0,8},{8,16},{16,24},{24,28},{28,20},{20,12},{12,4},{4,0},{1,9},{9... | collective-permute-start | bytes 393224 | tf_op jit(solution)/shard_map/ppermute | solution.py:441
  27.4 1.1 %shard_map.105.first_ref = f32[4,1560,128]{2,1,0:T(8,128)S(1)} custom-call(f32[32,144,256]{2,1,0:T(8,128)S(1)} %shard_map.104.real_ref, f32[32,16,128]{2,1,0:T(8,128)S(1)} %get-tuple-element.28.refs_0_, f32[32,16,128]{2,1,0:T(8,128)S(1)} %collective-permute-done.3.refs_1_, f32[32,16,128]{2,1,0:T(8,128)S(1)} %collective-permute-done.4.refs_2_, ...), custom_call_target="tpu_custom_call" | custom-call | flops 2147483648 | bytes 1048576 | tf_op jit(solution)/shard_map/pallas_call | solution.py:452
  28.5 2.0 %collective-permute-done.9.slab_ref = f32[16,16,128]{2,1,0:T(8,128)S(1)} collective-permute-done((f32[16,16,128]{2,1,0:T(8,128)S(1)}, f32[16,16,128]{2,1,0:T(8,128)S(1)}, u32[]{:S(2)}, u32[]{:S(2)}) %collective-permute-start.9) | collective-permute-done | bytes 131104 | tf_op jit(solution)/shard_map/ppermute | solution.py:441
  30.5 0.8 %shard_map.106.refs_0_ = bf16[128,2176]{1,0:T(8,128)(2,1)S(1)} custom-call(f32[4,1560,128]{2,1,0:T(8,128)S(1)} %shard_map.105.first_ref, f32[32,144,256]{2,1,0:T(8,128)S(1)} %shard_map.104.real_ref, f32[16,16,128]{2,1,0:T(8,128)S(1)} %collective-permute-done.9.slab_ref, bf16[8,80,48]{2,1,0:T(8,128)(2,1)S(1)} %get-tuple-element.30.x_last_ref, ...), custom_call_target="tpu_custom_call" | custom-call | flops 2147483648 | bytes 1048576 | tf_op jit(solution)/shard_map/pallas_call | solution.py:452
  32.1 1.5 %collective-permute-start.10 = (f32[128,512]{1,0:T(8,128)S(1)}, f32[128,512]{1,0:T(8,128)S(1)}, u32[]{:S(2)}, u32[]{:S(2)}) collective-permute-start(f32[128,512]{1,0:T(8,128)S(1)} %shard_map.107), channel_id=1, source_target_pairs={{0,2},{1,3},{2,0},{3,1},{4,6},{5,7},{6,4},{7,5},{8,10},{9,11},{10,... | collective-permute-start | bytes 786440 | tf_op jit(solution)/shard_map/ppermute | solution.py:551
  33.6 0.8 %shard_map.108.refs_0_.refs_1_ = bf16[128,2176]{1,0:T(8,128)(2,1)S(1)} custom-call(f32[4,1560,128]{2,1,0:T(8,128)S(1)} %shard_map.105.first_ref, f32[32,144,256]{2,1,0:T(8,128)S(1)} %shard_map.104.real_ref, f32[16,16,128]{2,1,0:T(8,128)S(1)} %collective-permute-done.12.slab_ref, bf16[8,80,48]{2,1,0:T(8,128)(2,1)S(1)} %get-tuple-element.30.x_last_ref, ...), custom_call_target="tpu_custom_call" | custom-call | flops 2147483648 | bytes 1048576 | tf_op jit(solution)/shard_map/pallas_call | solution.py:452
  34.5 1.4 %shard_map.110 = (f32[128,512]{1,0:T(8,128)S(1)}, f32[128,512]{1,0:T(8,128)S(1)}) custom-call(bf16[128,2176]{1,0:T(8,128)(2,1)S(1)} %shard_map.106.refs_0_, bf16[128,2176]{1,0:T(8,128)(2,1)S(1)} %shard_map.108.refs_0_.refs_1_, s32[3,2048]{1,0:T(4,128)S(1)} %copy-done), custom_call_target="tpu_custom_call" | custom-call | flops 2147483648 | bytes 1048576 | tf_op jit(solution)/shard_map/pallas_call | solution.py:452
  36.0 0.8 %shard_map.109 = (f32[64,512]{1,0:T(8,128)S(1)}, f32[64,512]{1,0:T(8,128)S(1)}) custom-call(bf16[128,2176]{1,0:T(8,128)(2,1)S(1)} %shard_map.108.refs_0_.refs_1_, s32[3,2048]{1,0:T(4,128)S(1)} %copy-done), custom_call_target="tpu_custom_call" | custom-call | flops 2147483648 | bytes 1048576 | tf_op jit(solution)/shard_map/pallas_call | solution.py:452
  37.5 1.5 %collective-permute-start.14 = (f32[64,512]{1,0:T(8,128)S(1)}, f32[64,512]{1,0:T(8,128)S(1)}, u32[]{:S(2)}, u32[]{:S(2)}) collective-permute-start(f32[64,512]{1,0:T(8,128)S(1)} %get-tuple-element.33), channel_id=1, source_target_pairs={{0,2},{1,3},{2,0},{3,1},{4,6},{5,7},{6,4},{7,5},{8,10},{9,11},{10,... | collective-permute-start | bytes 393224 | tf_op jit(solution)/shard_map/ppermute | solution.py:551
  39.6 2.3 %collective-permute-done.13.refs_1_ = f32[64,512]{1,0:T(8,128)S(1)} collective-permute-done((f32[64,512]{1,0:T(8,128)S(1)}, f32[64,512]{1,0:T(8,128)S(1)}, u32[]{:S(2)}, u32[]{:S(2)}) %collective-permute-start.13) | collective-permute-done | bytes 131104 | tf_op jit(solution)/shard_map/ppermute | solution.py:551
  41.9 3.5 %collective-permute-done.14.refs_2_ = f32[64,512]{1,0:T(8,128)S(1)} collective-permute-done((f32[64,512]{1,0:T(8,128)S(1)}, f32[64,512]{1,0:T(8,128)S(1)}, u32[]{:S(2)}, u32[]{:S(2)}) %collective-permute-start.14) | collective-permute-done | bytes 131104 | tf_op jit(solution)/shard_map/ppermute | solution.py:551
  45.4 1.2 %shard_map.112 = f32[1,65,4,512]{3,2,1,0:T(4,128)} custom-call(f32[64,512]{1,0:T(8,128)S(1)} %collective-permute-done.11.refs_0_, f32[64,512]{1,0:T(8,128)S(1)} %collective-permute-done.13.refs_1_, f32[64,512]{1,0:T(8,128)S(1)} %collective-permute-done.14.refs_2_, f32[256,512]{1,0:T(8,128)S(1)} %shard_map.111.refs_3_, s32[3,2048]{1,0:T(4,128)S(1)} %copy-done, ...), custom_call_target="tpu_custom_call" | custom-call | flops 2147483648 | bytes 1048576 | tf_op jit(solution)/shard_map/pallas_call | solution.py:452
  (26 shorter events, 4.3 us)
Async XLA Ops:
  0.0 9.5 %collective-permute-start.3 = (f32[32,16,128]{2,1,0:T(8,128)}, f32[32,16,128]{2,1,0:T(8,128)S(1)}, u32[]{:S(2)}, u32[]{:S(2)}) collective-permute-start(f32[32,16,128]{2,1,0:T(8,128)} %refs_9_.1), channel_id=1, source_target_pairs={{0,8},{8,16},{16,24},{24,28},{28,20},{20,12},{12,4},{4,0},{1,9},{9... | collective-permute-start | bytes 786440 | tf_op jit(solution)/shard_map/ppermute | solution.py:441
  3.1 8.3 %collective-permute-start.4 = (f32[32,16,128]{2,1,0:T(8,128)}, f32[32,16,128]{2,1,0:T(8,128)S(1)}, u32[]{:S(2)}, u32[]{:S(2)}) collective-permute-start(f32[32,16,128]{2,1,0:T(8,128)} %refs_9_.1), channel_id=1, source_target_pairs={{8,0},{16,8},{24,16},{28,24},{20,28},{12,20},{4,12},{0,4},{9,1},{1... | collective-permute-start | bytes 786440 | tf_op jit(solution)/shard_map/ppermute | solution.py:442
  3.1 8.5 %copy-start = (s32[3,2048]{1,0:T(4,128)S(1)}, s32[3,2048]{1,0:T(4,128)}, u32[]{:S(2)}) copy-start(s32[3,2048]{1,0:T(4,128)} %refs_4_.2) | copy-start | bytes 73732
  4.9 6.6 %collective-permute-start.2 = (f32[128,512]{1,0:T(8,128)S(1)}, f32[128,512]{1,0:T(8,128)S(1)}, u32[]{:S(2)}, u32[]{:S(2)}) collective-permute-start(f32[128,512]{1,0:T(8,128)S(1)} %get-tuple-element.24), channel_id=1, source_target_pairs={{0,1},{1,0},{2,3},{3,2},{4,5},{5,4},{6,7},{7,6},{8,9},{9,8},{10,11... | collective-permute-start | bytes 786440 | tf_op jit(solution)/shard_map/ppermute | solution.py:431
  5.0 9.2 %collective-permute-start.1 = (f32[128,512]{1,0:T(8,128)S(1)}, f32[128,512]{1,0:T(8,128)S(1)}, u32[]{:S(2)}, u32[]{:S(2)}) collective-permute-start(f32[128,512]{1,0:T(8,128)S(1)} %get-tuple-element.22), channel_id=1, source_target_pairs={{0,2},{1,3},{2,0},{3,1},{4,6},{5,7},{6,4},{7,5},{8,10},{9,11},{10,... | collective-permute-start | bytes 786440 | tf_op jit(solution)/shard_map/ppermute | solution.py:431
  7.0 12.2 %collective-permute-start = (f32[128,512]{1,0:T(8,128)S(1)}, f32[128,512]{1,0:T(8,128)S(1)}, u32[]{:S(2)}, u32[]{:S(2)}) collective-permute-start(f32[128,512]{1,0:T(8,128)S(1)} %get-tuple-element.21), channel_id=1, source_target_pairs={{0,3},{1,2},{2,1},{3,0},{4,7},{5,6},{6,5},{7,4},{8,11},{9,10},{10,... | collective-permute-start | bytes 786440 | tf_op jit(solution)/shard_map/ppermute | solution.py:431
  9.5 7.5 %collective-permute-start.5 = (f32[32,16,128]{2,1,0:T(8,128)S(1)}, f32[32,16,128]{2,1,0:T(8,128)S(1)}, u32[]{:S(2)}, u32[]{:S(2)}) collective-permute-start(f32[32,16,128]{2,1,0:T(8,128)S(1)} %collective-permute-done.3.refs_1_), channel_id=1, source_target_pairs={{0,8},{8,16},{16,24},{24,28},{28,20},{20,12},{12,4},{4,0},{1,9},{9... | collective-permute-start | bytes 786440 | tf_op jit(solution)/shard_map/ppermute | solution.py:441
  11.3 7.2 %collective-permute-start.6 = (f32[32,16,128]{2,1,0:T(8,128)S(1)}, f32[32,16,128]{2,1,0:T(8,128)S(1)}, u32[]{:S(2)}, u32[]{:S(2)}) collective-permute-start(f32[32,16,128]{2,1,0:T(8,128)S(1)} %collective-permute-done.4.refs_2_), channel_id=1, source_target_pairs={{8,0},{16,8},{24,16},{28,24},{20,28},{12,20},{4,12},{0,4},{9,1},{1... | collective-permute-start | bytes 786440 | tf_op jit(solution)/shard_map/ppermute | solution.py:442
  17.0 8.5 %collective-permute-start.7 = (f32[32,16,128]{2,1,0:T(8,128)S(1)}, f32[32,16,128]{2,1,0:T(8,128)S(1)}, u32[]{:S(2)}, u32[]{:S(2)}) collective-permute-start(f32[32,16,128]{2,1,0:T(8,128)S(1)} %collective-permute-done.5.refs_3_), channel_id=1, source_target_pairs={{0,8},{8,16},{16,24},{24,28},{28,20},{20,12},{12,4},{4,0},{1,9},{9... | collective-permute-start | bytes 786440 | tf_op jit(solution)/shard_map/ppermute | solution.py:441
  18.5 6.7 %collective-permute-start.8 = (f32[32,16,128]{2,1,0:T(8,128)S(1)}, f32[32,16,128]{2,1,0:T(8,128)S(1)}, u32[]{:S(2)}, u32[]{:S(2)}) collective-permute-start(f32[32,16,128]{2,1,0:T(8,128)S(1)} %collective-permute-done.6.refs_4_), channel_id=1, source_target_pairs={{8,0},{16,8},{24,16},{28,24},{20,28},{12,20},{4,12},{0,4},{9,1},{1... | collective-permute-start | bytes 786440 | tf_op jit(solution)/shard_map/ppermute | solution.py:442
  25.2 8.4 %collective-permute-start.12 = (f32[16,16,128]{2,1,0:T(8,128)S(1)}, f32[16,16,128]{2,1,0:T(8,128)S(1)}, u32[]{:S(2)}, u32[]{:S(2)}) collective-permute-start(f32[16,16,128]{2,1,0:T(8,128)S(1)} %slice.14), channel_id=1, source_target_pairs={{8,0},{16,8},{24,16},{28,24},{20,28},{12,20},{4,12},{0,4},{9,1},{1... | collective-permute-start | bytes 393224 | tf_op jit(solution)/shard_map/ppermute | solution.py:442
  25.5 5.0 %collective-permute-start.9 = (f32[16,16,128]{2,1,0:T(8,128)S(1)}, f32[16,16,128]{2,1,0:T(8,128)S(1)}, u32[]{:S(2)}, u32[]{:S(2)}) collective-permute-start(f32[16,16,128]{2,1,0:T(8,128)S(1)} %slice.12), channel_id=1, source_target_pairs={{0,8},{8,16},{16,24},{24,28},{28,20},{20,12},{12,4},{4,0},{1,9},{9... | collective-permute-start | bytes 393224 | tf_op jit(solution)/shard_map/ppermute | solution.py:441
  32.1 6.8 %collective-permute-start.10 = (f32[128,512]{1,0:T(8,128)S(1)}, f32[128,512]{1,0:T(8,128)S(1)}, u32[]{:S(2)}, u32[]{:S(2)}) collective-permute-start(f32[128,512]{1,0:T(8,128)S(1)} %shard_map.107), channel_id=1, source_target_pairs={{0,2},{1,3},{2,0},{3,1},{4,6},{5,7},{6,4},{7,5},{8,10},{9,11},{10,... | collective-permute-start | bytes 786440 | tf_op jit(solution)/shard_map/ppermute | solution.py:551
  35.9 3.2 %collective-permute-start.15 = (f32[128,512]{1,0:T(8,128)S(1)}, f32[128,512]{1,0:T(8,128)S(1)}, u32[]{:S(2)}, u32[]{:S(2)}) collective-permute-start(f32[128,512]{1,0:T(8,128)S(1)} %get-tuple-element.34), channel_id=1, source_target_pairs={{0,1},{1,0},{2,3},{3,2},{4,5},{5,4},{6,7},{7,6},{8,9},{9,8},{10,11... | collective-permute-start | bytes 786440 | tf_op jit(solution)/shard_map/ppermute | solution.py:551
  36.8 5.2 %collective-permute-start.13 = (f32[64,512]{1,0:T(8,128)S(1)}, f32[64,512]{1,0:T(8,128)S(1)}, u32[]{:S(2)}, u32[]{:S(2)}) collective-permute-start(f32[64,512]{1,0:T(8,128)S(1)} %get-tuple-element.32), channel_id=1, source_target_pairs={{0,3},{1,2},{2,1},{3,0},{4,7},{5,6},{6,5},{7,4},{8,11},{9,10},{10,... | collective-permute-start | bytes 393224 | tf_op jit(solution)/shard_map/ppermute | solution.py:551
  37.5 7.9 %collective-permute-start.14 = (f32[64,512]{1,0:T(8,128)S(1)}, f32[64,512]{1,0:T(8,128)S(1)}, u32[]{:S(2)}, u32[]{:S(2)}) collective-permute-start(f32[64,512]{1,0:T(8,128)S(1)} %get-tuple-element.33), channel_id=1, source_target_pairs={{0,2},{1,3},{2,0},{3,1},{4,6},{5,7},{6,4},{7,5},{8,10},{9,11},{10,... | collective-permute-start | bytes 393224 | tf_op jit(solution)/shard_map/ppermute | solution.py:551
  39.0 6.5 %collective-permute-start.11 = (f32[64,512]{1,0:T(8,128)S(1)}, f32[64,512]{1,0:T(8,128)S(1)}, u32[]{:S(2)}, u32[]{:S(2)}) collective-permute-start(f32[64,512]{1,0:T(8,128)S(1)} %slice.13), channel_id=1, source_target_pairs={{0,1},{1,0},{2,3},{3,2},{4,5},{5,4},{6,7},{7,6},{8,9},{9,8},{10,11... | collective-permute-start | bytes 393224 | tf_op jit(solution)/shard_map/ppermute | solution.py:551
